TPU v7x, 256 devices: a whole 4x4x8 slice. The times are simulated.
256 devices in a mesh: row: 16 (over y, x), col: 16 (over z, core).
Axes of the slice: x: 4, y: 4, z: 8, core: 2. Of those that a mesh axis runs over, the one named last changes fastest.
Arguments:
- hidden_in: bfloat16 [1024, 4096], P('col', 'row'), may hold values from -250 to 250
- norm_gain: bfloat16 [4096], P('row'), may hold values from 0.099609375 to 1.8984375
- w_qkv: bfloat16 [4096, 6144], P('row', 'col'), may hold values from -0.125 to 0.125
- w_out: bfloat16 [4096, 4096], P('row', 'col'), may hold values from -0.125 to 0.125
- cache_k: bfloat16 [16, 4096, 1024], P('col', 'row'), may hold values from -1300 to 1300
- value_cache: bfloat16 [16, 4096, 1024], P('col', 'row'), may hold values from -6 to 6
- cache_len: int32 [16], P('col'), may hold values from 1 to 4096, as said below
- parents: int32 [16, 64], P('col'), may hold values from -1 to 62, as said below
Outputs:
- update: bfloat16 [1024, 4096], P('col', 'row')
Inputs may be any that keep to these rules, and one draw needn't show every extreme that they name: Slots 0 to cache_len - 1 of a request's window are filled; some request fills all 4096 slots. `parents`: slot 0 of every request is the root with parent -1; every other slot's parent is an earlier slot of the same request; slot 63 has parent 64 - 2.
All inputs are finite; a program needn't handle non-finite values.
Results may differ from a plain program's by a relative error of at most 0.011.
The roundings to bfloat16 on the way count: a program that leaves them out, or rounds other values in their place, can miss the bound.
Values may be sent and summed in bfloat16 or wider, within the bound.
A program may use at most 128 MiB of HBM per device.

v0:
```python
import jax
import jax.numpy as jnp
from jax import lax
from jax.sharding import PartitionSpec as P

D = 4096
QUERY_HEADS = 32
KEY_VALUE_HEADS = 8
HEAD_SIZE = 128


masked_score = -1e30


def merged(value, axis, join):
    pieces = jax.tree.map(lambda part: lax.all_gather(part, axis), value)
    head = jax.tree.map(lambda part: part[0], pieces)
    tail = jax.tree.map(lambda part: part[1:], pieces)
    so_far, _ = lax.scan(lambda so_far, piece: (join(so_far, piece), None), head, tail)
    return so_far


def ancestors(parents):
    draft_tree = parents.shape[1]
    slot_ids = jnp.arange(draft_tree, dtype=jnp.int32)
    parent_links = (parents[:, :, None] == slot_ids[None, None, :]).astype(jnp.float32)
    reachable = parent_links + jnp.eye(draft_tree, dtype=jnp.float32)[None]
    for squaring in range(max(1, (draft_tree - 1).bit_length())):
        product = jnp.einsum("rij,rjk->rik", reachable, reachable, precision=lax.Precision.HIGHEST)
        reachable = (product > 0.5).astype(jnp.float32)
    return reachable > 0.5


def pair_merge(first, second):
    peak = jnp.maximum(first[0], second[0])
    first_scale = jnp.exp(first[0] - peak)
    second_scale = jnp.exp(second[0] - peak)
    totals = first[1] * first_scale + second[1] * second_scale
    blended = first[2] * first_scale[..., None] + second[2] * second_scale[..., None]
    return (peak, totals, blended)


def shards(hidden_in, norm_gain, w_qkv, w_out, cache_k, value_cache, cache_len, parents):
    rows_here = hidden_in.shape[0]
    request_list = cache_k.shape[0]
    token_positions = cache_k.shape[1]
    draft_tree = parents.shape[1]
    head_groups = QUERY_HEADS // KEY_VALUE_HEADS
    heads_dev = QUERY_HEADS // lax.axis_size("row")
    row_index = lax.axis_index("row")
    score_scale = HEAD_SIZE ** (-0.5)
    features = hidden_in.astype(jnp.float32)
    squares = lax.psum(jnp.sum(features * features, axis=1), "row")
    row_scale = lax.rsqrt(squares / D + 1e-05)
    normed = (features * row_scale[:, None] * norm_gain.astype(jnp.float32)[None, :]).astype(
        jnp.bfloat16
    )
    partial_value = jnp.dot(
        normed, lax.all_gather(w_qkv, "col", axis=1, tiled=True), preferred_element_type=jnp.float32
    )
    summed = lax.psum_scatter(partial_value, "row", scatter_dimension=1, tiled=True).astype(
        jnp.bfloat16
    )
    projected_output = lax.all_gather(summed, "row", axis=1, tiled=True)
    query_block = projected_output[:, : QUERY_HEADS * HEAD_SIZE].reshape(
        request_list, draft_tree, KEY_VALUE_HEADS, head_groups, HEAD_SIZE
    )
    new_key_block = projected_output[
        :, QUERY_HEADS * HEAD_SIZE : (QUERY_HEADS + KEY_VALUE_HEADS) * HEAD_SIZE
    ].reshape(request_list, draft_tree, KEY_VALUE_HEADS, HEAD_SIZE)
    new_value_block = projected_output[:, (QUERY_HEADS + KEY_VALUE_HEADS) * HEAD_SIZE :].reshape(
        request_list, draft_tree, KEY_VALUE_HEADS, HEAD_SIZE
    )
    first_slot = row_index * token_positions
    slot_ids = first_slot + jnp.arange(token_positions, dtype=jnp.int32)

    def cache_part(request_item):
        query_rows, cached_key_rows, cached_value_rows, length = request_item
        key_row_block = cached_key_rows.reshape(token_positions, KEY_VALUE_HEADS, HEAD_SIZE)
        value_row_block = cached_value_rows.reshape(token_positions, KEY_VALUE_HEADS, HEAD_SIZE)
        scores = (
            jnp.einsum(
                "tkgd,pkd->kgtp", query_rows, key_row_block, preferred_element_type=jnp.float32
            )
            * score_scale
        )
        visible = (slot_ids < length)[None, None, None, :]
        scores = jnp.where(visible, scores, masked_score)
        highest = jnp.max(scores, axis=-1)
        weights = jnp.where(visible, jnp.exp(scores - highest[..., None]), 0.0)
        totals = jnp.sum(weights, axis=-1)
        blended = jnp.einsum(
            "kgtp,pkd->kgtd",
            weights.astype(jnp.bfloat16),
            value_row_block,
            preferred_element_type=jnp.float32,
        )
        return (
            highest.reshape(QUERY_HEADS, draft_tree),
            totals.reshape(QUERY_HEADS, draft_tree),
            blended.reshape(QUERY_HEADS, draft_tree, HEAD_SIZE),
        )

    maxima, totals, blended = lax.map(cache_part, (query_block, cache_k, value_cache, cache_len))
    maxima, totals, blended = merged((maxima, totals, blended), "row", pair_merge)
    max_own = lax.dynamic_slice_in_dim(maxima, row_index * heads_dev, heads_dev, 1)
    total_own = lax.dynamic_slice_in_dim(totals, row_index * heads_dev, heads_dev, 1)
    blend_own = lax.dynamic_slice_in_dim(blended, row_index * heads_dev, heads_dev, 1)
    allowed = ancestors(parents)[:, None, :, :]
    query_heads = projected_output[:, : QUERY_HEADS * HEAD_SIZE].reshape(
        request_list, draft_tree, QUERY_HEADS, HEAD_SIZE
    )
    query_own = lax.dynamic_slice_in_dim(query_heads, row_index * heads_dev, heads_dev, 2)
    key_own = lax.dynamic_slice_in_dim(
        jnp.repeat(new_key_block, head_groups, axis=2), row_index * heads_dev, heads_dev, 2
    )
    value_own = lax.dynamic_slice_in_dim(
        jnp.repeat(new_value_block, head_groups, axis=2), row_index * heads_dev, heads_dev, 2
    )
    tree_scores = (
        jnp.einsum("rthd,rshd->rhts", query_own, key_own, preferred_element_type=jnp.float32)
        * score_scale
    )
    tree_scores = jnp.where(allowed, tree_scores, masked_score)
    tree_max = jnp.max(tree_scores, axis=-1)
    tree_weights = jnp.where(allowed, jnp.exp(tree_scores - tree_max[..., None]), 0.0)
    tree_total = jnp.sum(tree_weights, axis=-1)
    tree_blend = jnp.einsum(
        "rhts,rshd->rhtd",
        tree_weights.astype(jnp.bfloat16),
        value_own,
        preferred_element_type=jnp.float32,
    )
    joint_max = jnp.maximum(max_own, tree_max)
    cache_scale = jnp.exp(max_own - joint_max)
    tree_scale = jnp.exp(tree_max - joint_max)
    numerator = blend_own * cache_scale[..., None] + tree_blend * tree_scale[..., None]
    denominator = total_own * cache_scale + tree_total * tree_scale
    attended = (numerator / denominator[..., None]).astype(jnp.bfloat16)
    attended = attended.transpose(0, 2, 1, 3).reshape(rows_here, heads_dev * HEAD_SIZE)
    partial_out = jnp.dot(
        attended,
        lax.all_gather(w_out, "col", axis=1, tiled=True),
        preferred_element_type=jnp.float32,
    )
    return lax.psum_scatter(partial_out, "row", scatter_dimension=1, tiled=True).astype(
        jnp.bfloat16
    )


def solution(mesh):
    placed = (
        P("col", "row"),
        P("row"),
        P("row", "col"),
        P("row", "col"),
        P("col", "row", None),
        P("col", "row", None),
        P("col"),
        P("col", None),
    )
    return jax.shard_map(
        shards, mesh=mesh, in_specs=placed, out_specs=P("col", "row"), check_vma=False
    )
```

profile of v0, /device:TPU:2, one launch (start us, length us, event | category | flops | bytes accessed | tf_op | source)
XLA Modules:
  0.0 420.8 jit_solution(8517399735573453257)
XLA Ops:
  8.8 37.7 %psum.7 = f32[64]{0:T(128)S(1)} all-reduce(f32[64]{0:T(128)S(1)} %fusion.29), channel_id=1, replica_groups=mesh['row'=16,'col'=16] {'row'}, use_global_device_ids=true, to_apply=%region_1.0 | all-reduce | flops 64 | bytes 512 | tf_op jit(solution)/shard_map/psum | solution.py:53
  46.5 6.5 %all-gather.4.cloned.1.call-done = bf16[256,6144]{1,0:T(8,128)(2,1)} async-done(((bf16[256,384]{1,0:T(8,128)(2,1)}), bf16[256,6144]{1,0:T(8,128)(2,1)}) %all-gather.4.cloned.1.call-update) | async-done | bytes 3145744 | tf_op jit(solution)/shard_map/all_gather | solution.py:59
  53.0 3.8 fusion.35
  59.3 75.1 %reduce-scatter.3.cloned.1.call-done = f32[64,384]{1,0:T(8,128)} async-done(((f32[64,6144]{1,0:T(8,128)}), f32[64,384]{1,0:T(8,128)}) %reduce-scatter.3.cloned.1.call-update) | async-done | bytes 98320 | tf_op jit(solution)/shard_map/reduce_scatter | solution.py:61
  135.3 22.6 %all_gather.28 = bf16[64,6144]{1,0:T(8,128)(2,1)S(1)} all-gather(bf16[64,384]{1,0:T(8,128)(2,1)S(1)} %convert_element_type.85), channel_id=1, replica_groups=mesh['row'=16,'col'=16] {'row'}, dimensions={1}, use_global_device_ids=true | all-gather | bytes 835584 | tf_op jit(solution)/shard_map/all_gather | solution.py:64
  158.1 1.2 squeeze.36
  159.3 1.9 bitcast_reduce_fusion
  161.2 1.6 fusion.17
  165.5 24.1 %all_gather.32 = f32[16,1,32,64]{3,2,1,0:T(8,128)S(1)} all-gather(f32[1,1,32,64]{3,2,1,0:T(8,128)S(1)} %bitcast.147), channel_id=1, replica_groups=mesh['row'=16,'col'=16] {'row'}, dimensions={0}, use_global_device_ids=true | all-gather | bytes 139264 | tf_op jit(solution)/shard_map/all_gather | solution.py:16
  189.6 22.0 %all_gather.30 = f32[16,1,32,64]{3,2,1,0:T(8,128)S(1)} all-gather(f32[1,1,32,64]{3,2,1,0:T(8,128)S(1)} %bitcast.146), channel_id=1, replica_groups=mesh['row'=16,'col'=16] {'row'}, dimensions={0}, use_global_device_ids=true | all-gather | bytes 139264 | tf_op jit(solution)/shard_map/all_gather | solution.py:16
  212.2 68.4 %all-gather.6.cloned.1.call-done = f32[16,1,32,64,128]{4,3,2,1,0:T(8,128)} async-done(((f32[1,1,32,64,128]{4,3,2,1,0:T(8,128)}), f32[16,1,32,64,128]{4,3,2,1,0:T(8,128)}) %all-gather.6.cloned.1.call-update) | async-done | bytes 16777232 | tf_op jit(solution)/shard_map/all_gather | solution.py:16
  280.6 1.3 slice_bitcast_fusion
  281.9 14.5 %slice.43 = f32[15,1,32,64,128]{4,3,2,1,0:T(8,128)} slice(f32[16,1,32,64,128]{4,3,2,1,0:T(8,128)} %all-gather.6.cloned.1.call-done), slice={[1:16], [0:1], [0:32], [0:64], [0:128]} | slice | bytes 31457280 | tf_op jit(solution)/shard_map/slice | solution.py:18
  296.5 34.1 %while.2 = (s32[]{:T(128)}, f32[1,32,64]{2,1,0:T(8,128)S(1)}, f32[1,32,64]{2,1,0:T(8,128)S(1)}, f32[1,32,64,128]{3,2,1,0:T(8,128)S(1)}, f32[15,1,32,64]{3,2,1,0:...) while((s32[]{:T(128)}, f32[1,32,64]{2,1,0:T(8,128)S(1)}, ...), condition=%wide.region_6.7_spmd, body=%wide.region_5.6_spmd.sunk | while | flops 800770 | bytes 3268713 | solution.py:19
  296.5 2.2 fusion.83
  298.8 2.2 fusion.83
  301.1 2.2 fusion.83
  303.4 2.2 fusion.83
  305.6 2.2 fusion.83
  307.9 2.2 fusion.83
  310.2 2.2 fusion.83
  312.5 2.2 fusion.83
  314.7 2.2 fusion.83
  317.0 2.2 fusion.83
  319.3 2.2 fusion.83
  321.6 2.2 fusion.83
  323.8 2.2 fusion.83
  326.1 2.2 fusion.83
  328.4 2.2 fusion.83
  331.0 3.0 fusion.38
  334.1 78.7 %reduce-scatter.5.cloned.1.call-done = f32[64,256]{1,0:T(8,128)} async-done(((f32[64,4096]{1,0:T(8,128)}), f32[64,256]{1,0:T(8,128)}) %reduce-scatter.5.cloned.1.call-update) | async-done | bytes 65552 | tf_op jit(solution)/shard_map/reduce_scatter | solution.py:146
  412.8 1.5 convert_element_type.92
  (96 shorter events, 9.4 us)
Async XLA Ops:
  6.5 46.5 %all-gather.4.cloned.1.call-start = ((), (), s32[]{:S(2)}) async-start(), calls=%async_computation.2 | async-start | bytes 3342336 | tf_op jit(solution)/shard_map/all_gather | solution.py:59
  7.3 127.2 %reduce-scatter.3.cloned.1.call-start = ((), (), s32[]{:S(2)}) async-start(), calls=%async_computation.3 | async-start | bytes 1671168 | tf_op jit(solution)/shard_map/reduce_scatter | solution.py:61
  46.5 11.0 %copy-start = (bf16[1,256,1024]{2,1,0:T(8,128)(2,1)S(1)}, bf16[1,256,1024]{2,1,0:T(8,128)(2,1)}, u32[]{:S(2)}) copy-start(bf16[1,256,1024]{2,1,0:T(8,128)(2,1)} %param.14) | copy-start | bytes 1572868
  56.8 1.7 copy-start.1
  56.8 223.8 %all-gather.6.cloned.1.call-start = ((), (), s32[]{:S(2)}) async-start(), calls=%async_computation.4 | async-start | bytes 17825792 | tf_op jit(solution)/shard_map/all_gather | solution.py:16
  159.3 1.9 copy-start.2
  161.2 2.3 copy-start.3
  162.8 168.2 %all-gather.8.cloned.1.call-start = ((), (), s32[]{:S(2)}) async-start(), calls=%async_computation.5 | async-start | bytes 2228224 | tf_op jit(solution)/shard_map/all_gather | solution.py:143
  163.4 249.4 %reduce-scatter.5.cloned.1.call-start = ((), (), s32[]{:S(2)}) async-start(), calls=%async_computation.6 | async-start | bytes 1114112 | tf_op jit(solution)/shard_map/reduce_scatter | solution.py:146
Sparse Core Ops, SparseCore 0:
  9.1 43.8 all-gather.3
  56.9 77.4 reduce-scatter.2
  162.9 117.6 all-gather.5
  282.2 40.3 all-gather.7
  334.2 78.5 reduce-scatter.4
where the time goes:
time: 422 us; the launch traced here: 421 us
  waiting for transfers between devices  230 us (55%)
  blocking collectives  106 us (25%)
  other arithmetic  38.4 us (9%)
  local copies, waits for them, and re-layouts  19.6 us (5%)
  between operations  14 us (3%)
  matrix products  11.5 us (3%)
    reduce_scatter x1, waiting for transfers between devices, shards(): lax.psum_scatter(partial_out, 'row', scatter_dimension=1, tiled=True)  78.7 us
    reduce_scatter x1, waiting for transfers between devices, shards(): lax.psum_scatter(partial_value, 'row', scatter_dimension=1, tiled=True)  75.1 us
    all_gather x1, waiting for transfers between devices, merged(): pieces = jax.tree.map(lambda part: lax.all_gather(part, axis), value)  68.4 us
    all_gather x2, blocking collectives, merged(): pieces = jax.tree.map(lambda part: lax.all_gather(part, axis), value)  46.1 us
    psum x1, blocking collectives, shards(): squares = lax.psum(jnp.sum(features * features, axis=1), 'row')  37.7 us
    add x15, other arithmetic, pair_merge(): first[2] * first_scale[..., None] + second[2] * second_scale[..., None]  32.9 us
    all_gather x1, blocking collectives, shards(): projected_output = lax.all_gather(summed, 'row', axis=1, tiled=True)  22.6 us
    slice x3, local copies, waits for them, and re-layouts, merged(): tail = jax.tree.map(lambda part: part[1:], pieces)  14.6 us
  transfers between devices with their start and end apart: 5, of which 4 were waited for; matrix products, arithmetic and copies ran while one was open for 13% of the time, Pallas kernels for 0%

commit v1 on v0

--- a/solution.py
+++ b/solution.py
@@ -12,14 +12,6 @@
 masked_score = -1e30
 
 
-def merged(value, axis, join):
-    pieces = jax.tree.map(lambda part: lax.all_gather(part, axis), value)
-    head = jax.tree.map(lambda part: part[0], pieces)
-    tail = jax.tree.map(lambda part: part[1:], pieces)
-    so_far, _ = lax.scan(lambda so_far, piece: (join(so_far, piece), None), head, tail)
-    return so_far
-
-
 def ancestors(parents):
     draft_tree = parents.shape[1]
     slot_ids = jnp.arange(draft_tree, dtype=jnp.int32)
@@ -31,13 +23,12 @@
     return reachable > 0.5
 
 
-def pair_merge(first, second):
-    peak = jnp.maximum(first[0], second[0])
-    first_scale = jnp.exp(first[0] - peak)
-    second_scale = jnp.exp(second[0] - peak)
-    totals = first[1] * first_scale + second[1] * second_scale
-    blended = first[2] * first_scale[..., None] + second[2] * second_scale[..., None]
-    return (peak, totals, blended)
+def row_reduce(partial, axis_name):
+    count = lax.axis_size(axis_name)
+    rows, cols = partial.shape
+    pieces = partial.reshape(rows, count, cols // count).transpose(1, 0, 2)
+    received = lax.all_to_all(pieces, axis_name, 0, 0)
+    return jnp.sum(received, axis=0)
 
 
 def shards(hidden_in, norm_gain, w_qkv, w_out, cache_k, value_cache, cache_len, parents):
@@ -46,7 +37,8 @@
     token_positions = cache_k.shape[1]
     draft_tree = parents.shape[1]
     head_groups = QUERY_HEADS // KEY_VALUE_HEADS
-    heads_dev = QUERY_HEADS // lax.axis_size("row")
+    row_count = lax.axis_size("row")
+    heads_dev = QUERY_HEADS // row_count
     row_index = lax.axis_index("row")
     score_scale = HEAD_SIZE ** (-0.5)
     features = hidden_in.astype(jnp.float32)
@@ -58,9 +50,7 @@
     partial_value = jnp.dot(
         normed, lax.all_gather(w_qkv, "col", axis=1, tiled=True), preferred_element_type=jnp.float32
     )
-    summed = lax.psum_scatter(partial_value, "row", scatter_dimension=1, tiled=True).astype(
-        jnp.bfloat16
-    )
+    summed = row_reduce(partial_value, "row").astype(jnp.bfloat16)
     projected_output = lax.all_gather(summed, "row", axis=1, tiled=True)
     query_block = projected_output[:, : QUERY_HEADS * HEAD_SIZE].reshape(
         request_list, draft_tree, KEY_VALUE_HEADS, head_groups, HEAD_SIZE
@@ -95,17 +85,20 @@
             value_row_block,
             preferred_element_type=jnp.float32,
         )
-        return (
-            highest.reshape(QUERY_HEADS, draft_tree),
-            totals.reshape(QUERY_HEADS, draft_tree),
-            blended.reshape(QUERY_HEADS, draft_tree, HEAD_SIZE),
+        stats = jnp.concatenate(
+            [highest.reshape(QUERY_HEADS, draft_tree), totals.reshape(QUERY_HEADS, draft_tree)],
+            axis=-1,
+        )
+        return jnp.concatenate(
+            [blended.reshape(QUERY_HEADS, draft_tree, HEAD_SIZE), stats[:, None, :]], axis=1
         )
 
-    maxima, totals, blended = lax.map(cache_part, (query_block, cache_k, value_cache, cache_len))
-    maxima, totals, blended = merged((maxima, totals, blended), "row", pair_merge)
-    max_own = lax.dynamic_slice_in_dim(maxima, row_index * heads_dev, heads_dev, 1)
-    total_own = lax.dynamic_slice_in_dim(totals, row_index * heads_dev, heads_dev, 1)
-    blend_own = lax.dynamic_slice_in_dim(blended, row_index * heads_dev, heads_dev, 1)
+    packed = lax.map(cache_part, (query_block, cache_k, value_cache, cache_len))
+    packed = packed.reshape(request_list, row_count, heads_dev, draft_tree + 1, HEAD_SIZE)
+    gathered = lax.all_to_all(packed, "row", 1, 1)
+    block_blend = gathered[:, :, :, :draft_tree, :]
+    block_max = gathered[:, :, :, draft_tree, :draft_tree]
+    block_total = gathered[:, :, :, draft_tree, draft_tree : 2 * draft_tree]
     allowed = ancestors(parents)[:, None, :, :]
     query_heads = projected_output[:, : QUERY_HEADS * HEAD_SIZE].reshape(
         request_list, draft_tree, QUERY_HEADS, HEAD_SIZE
@@ -131,11 +124,11 @@
         value_own,
         preferred_element_type=jnp.float32,
     )
-    joint_max = jnp.maximum(max_own, tree_max)
-    cache_scale = jnp.exp(max_own - joint_max)
+    joint_max = jnp.maximum(jnp.max(block_max, axis=1), tree_max)
+    block_scale = jnp.exp(block_max - joint_max[:, None])
     tree_scale = jnp.exp(tree_max - joint_max)
-    numerator = blend_own * cache_scale[..., None] + tree_blend * tree_scale[..., None]
-    denominator = total_own * cache_scale + tree_total * tree_scale
+    numerator = jnp.sum(block_blend * block_scale[..., None], axis=1) + tree_blend * tree_scale[..., None]
+    denominator = jnp.sum(block_total * block_scale, axis=1) + tree_total * tree_scale
     attended = (numerator / denominator[..., None]).astype(jnp.bfloat16)
     attended = attended.transpose(0, 2, 1, 3).reshape(rows_here, heads_dev * HEAD_SIZE)
     partial_out = jnp.dot(
@@ -143,9 +136,7 @@
         lax.all_gather(w_out, "col", axis=1, tiled=True),
         preferred_element_type=jnp.float32,
     )
-    return lax.psum_scatter(partial_out, "row", scatter_dimension=1, tiled=True).astype(
-        jnp.bfloat16
-    )
+    return row_reduce(partial_out, "row").astype(jnp.bfloat16)
 
 
 def solution(mesh):

time: 422 us -> 165 us (0.39)
  waiting for transfers between devices: 230 us -> 33.2 us
  other arithmetic: 38.4 us -> 7.3 us
  blocking collectives: 106 us -> 78.9 us
  starting transfers between devices: 0.16 us -> 13 us
  local copies, waits for them, and re-layouts: 19.6 us -> 11.5 us
  matrix products: 11.5 us -> 5.84 us
    reduce_scatter x2 -> x0, waiting for transfers between devices: 154 us -> none  [the longest x1 78.7 us: shards(): lax.psum_scatter(partial_out, 'row', scatter_dimension=1, tiled=True)]
    all_gather x1 -> x0, waiting for transfers between devices: 68.4 us -> none  [merged(): pieces = jax.tree.map(lambda part: lax.all_gather(part, axis), value)]
    all_gather x2 -> x0, blocking collectives: 46.1 us -> none  [merged(): pieces = jax.tree.map(lambda part: lax.all_gather(part, axis), value)]
    add x15 -> x1, other arithmetic: 32.9 us -> 0.01 us  [shards(): jnp.sum(block_total * block_scale, axis=1) + tree_total * tree_scale]
    all_to_all x0 -> x2, waiting for transfers between devices: none -> 26 us  [the longest x1 20.1 us: row_reduce(): received = lax.all_to_all(pieces, axis_name, 0, 0)]
    all_to_all x0 -> x1, blocking collectives: none -> 15.9 us  [row_reduce(): received = lax.all_to_all(pieces, axis_name, 0, 0)]
    slice x3 -> x0, local copies, waits for them, and re-layouts: 14.6 us -> none  [merged(): tail = jax.tree.map(lambda part: part[1:], pieces)]
    all_to_all x0 -> x2, starting transfers between devices: none -> 12.9 us  [the longest x1 7.4 us: row_reduce(): received = lax.all_to_all(pieces, axis_name, 0, 0)]
  transfers between devices with their start and end apart: 5 -> 4, of which waited for: 4 -> 3; matrix products, arithmetic and copies ran while one was open for 13% -> 11% of each run, Pallas kernels for 0% -> 0%
where the time goes in v1:
time: 165 us; the launch traced here: 164 us
  blocking collectives  78.9 us (48%)
  waiting for transfers between devices  33.2 us (20%)
  between operations  14.3 us (9%)
  starting transfers between devices  13 us (8%)
  local copies, waits for them, and re-layouts  11.5 us (7%)
  other arithmetic  7.3 us (4%)
  matrix products  5.84 us (4%)
    psum x1, blocking collectives, shards(): squares = lax.psum(jnp.sum(features * features, axis=1), 'row')  37.7 us
    all_gather x1, blocking collectives, shards(): projected_output = lax.all_gather(summed, 'row', axis=1, tiled=True)  25.3 us
    all_to_all x1, waiting for transfers between devices, row_reduce(): received = lax.all_to_all(pieces, axis_name, 0, 0)  20.1 us
    all_to_all x1, blocking collectives, row_reduce(): received = lax.all_to_all(pieces, axis_name, 0, 0)  15.9 us
    all_to_all x1, starting transfers between devices, row_reduce(): received = lax.all_to_all(pieces, axis_name, 0, 0)  7.4 us
    all_to_all x1, waiting for transfers between devices, shards(): gathered = lax.all_to_all(packed, 'row', 1, 1)  5.91 us
    all_gather x1, waiting for transfers between devices, shards(): lax.all_gather(w_qkv, 'col', axis=1, tiled=True)  5.77 us
    all_to_all x1, starting transfers between devices, shards(): gathered = lax.all_to_all(packed, 'row', 1, 1)  5.54 us
  transfers between devices with their start and end apart: 4, of which 3 were waited for; matrix products, arithmetic and copies ran while one was open for 11% of the time, Pallas kernels for 0%

profile of v1, /device:TPU:2, one launch (start us, length us, event | category | flops | bytes accessed | tf_op | source)
XLA Modules:
  0.0 164.0 jit_solution(14819680928935763903)
XLA Ops:
  6.5 0.7 all-gather.3.cloned.1.call-update
  7.3 0.7 all-gather.5.cloned.1.call-update
  8.0 0.7 convert_element_type.86
  8.7 0.9 fusion.24
  9.5 37.7 %psum.7 = f32[64]{0:T(128)S(1)} all-reduce(f32[64]{0:T(128)S(1)} %fusion.24), channel_id=1, replica_groups=mesh['row'=16,'col'=16] {'row'}, use_global_device_ids=true, to_apply=%region_1.0 | all-reduce | flops 64 | bytes 512 | tf_op jit(solution)/shard_map/psum | solution.py:45
  47.2 5.8 %all-gather.3.cloned.1.call-done = bf16[256,6144]{1,0:T(8,128)(2,1)} async-done(((bf16[256,384]{1,0:T(8,128)(2,1)}), bf16[256,6144]{1,0:T(8,128)(2,1)}) %all-gather.3.cloned.1.call-update) | async-done | bytes 3145744 | tf_op jit(solution)/shard_map/all_gather | solution.py:51
  53.0 2.6 %fusion.30 = f32[64,6144]{1,0:T(8,128)S(1)} fusion(bf16[256,6144]{1,0:T(8,128)(2,1)} %all-gather.3.cloned.1.call-done, bf16[64,256]{1,0:T(8,128)(2,1)} %param.8, f32[256]{0:T(256)S(1)} %convert_element_type.86, f32[64]{0:T(128)S(1)} %add_rsqrt_fusion), kind=kOutput, calls=%fused_computation.52 | convolution fusion | flops 201392128 | bytes 4752640 | tf_op jit(solution)/shard_map/dot_general | solution.py:50
  55.6 1.3 copy.91
  56.9 7.4 %all-to-all-start = ((f32[16,64,384]{2,1,0:T(8,128)}), f32[16,64,384]{2,1,0:T(8,128)S(1)}, u32[]{:S(2)}, u32[]{:S(2)}) async-start(f32[16,64,384]{2,1,0:T(8,128)} %bitcast.96), calls=%async_computation | async-start | bytes 3145728 | tf_op jit(solution)/shard_map/all_to_all | solution.py:30
  65.4 0.2 convolution_compare_fusion.5
  66.1 20.1 %all-to-all-done = f32[16,64,384]{2,1,0:T(8,128)S(1)} async-done(((f32[16,64,384]{2,1,0:T(8,128)}), f32[16,64,384]{2,1,0:T(8,128)S(1)}, u32[]{:S(2)}, u32[]{:S(2)}) %all-to-all-start) | async-done | bytes 1572896 | tf_op jit(solution)/shard_map/all_to_all | solution.py:30
  86.3 25.3 %all_gather.10 = bf16[64,6144]{1,0:T(8,128)(2,1)S(1)} all-gather(bf16[64,384]{1,0:T(8,128)(2,1)S(1)} %reduce_sum.65), channel_id=1, replica_groups=mesh['row'=16,'col'=16] {'row'}, dimensions={1}, use_global_device_ids=true | all-gather | bytes 835584 | tf_op jit(solution)/shard_map/all_gather | solution.py:54
  111.6 0.9 copy-done
  112.6 1.0 slice_bitcast_fusion.3
  113.5 0.4 squeeze.24
  113.9 0.6 bitcast_reduce_fusion
  114.5 0.7 fusion.11
  115.2 0.8 copy.46
  116.0 0.9 fusion.2
  116.9 1.5 maximum_maximum_fusion
  118.4 5.5 %all-to-all-start.1 = ((f32[1,16,2,65,128]{4,2,3,0,1:T(2,128)}), f32[1,16,2,65,128]{4,2,3,0,1:T(2,128)S(1)}, u32[]{:S(2)}, u32[]{:S(2)}) async-start(f32[1,16,2,65,128]{4,2,3,0,1:T(2,128)} %maximum_maximum_fusion), calls=%async_computation.1 | async-start | bytes 2129920 | tf_op jit(solution)/shard_map/all_to_all | solution.py:98
  124.2 3.3 %copy.56 = bf16[4096,256]{1,0:T(8,128)(2,1)S(1)} copy(bf16[4096,256]{0,1:T(8,128)(2,1)} %bitcast.100) | data formatting | bytes 4194304 | tf_op jit(solution)/shard_map/dot_general | solution.py:134
  127.5 1.1 copy.70
  128.7 1.0 slice_bitcast_fusion
  129.9 0.2 fusion.52
  130.1 5.9 %all-to-all-done.1 = f32[1,16,2,65,128]{4,2,3,0,1:T(2,128)S(1)} async-done(((f32[1,16,2,65,128]{4,2,3,0,1:T(2,128)}), f32[1,16,2,65,128]{4,2,3,0,1:T(2,128)S(1)}, u32[]{:S(2)}, u32[]{:S(2)}) %all-to-all-start.1) | async-done | bytes 1064992 | tf_op jit(solution)/shard_map/all_to_all | solution.py:98
  136.1 1.0 copy.51
  137.2 2.2 %fusion.13 = f32[2,64,128]{2,0,1:T(2,128)S(1)} fusion(f32[1,16,2,65,128]{4,2,3,0,1:T(2,128)S(1)} %all-to-all-done.1, f32[16,2,64]{1,2,0:T(8,128)} %copy.51), kind=kLoop, calls=%fused_computation.27 | loop fusion | flops 507904 | bytes 1122304 | tf_op jit(solution)/shard_map/reduce_sum | solution.py:130
  139.6 0.2 fusion.8
  139.9 0.7 convolution_bitcast_fusion
  140.6 15.9 %all_to_all.15 = f32[16,64,256]{2,1,0:T(8,128)S(1)} all-to-all(f32[16,64,256]{2,1,0:T(8,128)S(1)} %convolution_bitcast_fusion), channel_id=1, replica_groups=mesh['row'=16,'col'=16] {'row'}, dimensions={0} | all-to-all | bytes 2097152 | tf_op jit(solution)/shard_map/all_to_all | solution.py:30
  156.5 0.7 reduce_sum.70
  (34 shorter events, 1.8 us)
Async XLA Ops:
  6.5 46.5 %all-gather.3.cloned.1.call-start = ((), (), s32[]{:S(2)}) async-start(), calls=%async_computation.3 | async-start | bytes 3342336 | tf_op jit(solution)/shard_map/all_gather | solution.py:51
  7.3 117.0 %all-gather.5.cloned.1.call-start = ((), (), s32[]{:S(2)}) async-start(), calls=%async_computation.4 | async-start | bytes 2228224 | tf_op jit(solution)/shard_map/all_gather | solution.py:136
  56.9 8.1 %copy-start.1 = (bf16[1,256,1024]{2,1,0:T(8,128)(2,1)S(1)}, bf16[1,256,1024]{2,1,0:T(8,128)(2,1)}, u32[]{:S(2)}) copy-start(bf16[1,256,1024]{2,1,0:T(8,128)(2,1)} %param.12) | copy-start | bytes 1572868
  56.9 8.2 %copy-start.2 = (bf16[1,256,1024]{2,1,0:T(8,128)(2,1)S(1)}, bf16[1,256,1024]{2,1,0:T(8,128)(2,1)}, u32[]{:S(2)}) copy-start(bf16[1,256,1024]{2,1,0:T(8,128)(2,1)} %param.13) | copy-start | bytes 1572868
  56.9 8.3 %copy-start.3 = (s32[1,64]{1,0:T(1,128)S(1)}, s32[1,64]{1,0:T(1,128)}, u32[]{:S(2)}) copy-start(s32[1,64]{1,0:T(1,128)} %param.15) | copy-start | bytes 772
  56.9 29.3 %all-to-all-start = ((f32[16,64,384]{2,1,0:T(8,128)}), f32[16,64,384]{2,1,0:T(8,128)S(1)}, u32[]{:S(2)}, u32[]{:S(2)}) async-start(f32[16,64,384]{2,1,0:T(8,128)} %bitcast.96), calls=%async_computation | async-start | bytes 3145728 | tf_op jit(solution)/shard_map/all_to_all | solution.py:30
  111.6 0.9 copy-start
  118.4 17.6 %all-to-all-start.1 = ((f32[1,16,2,65,128]{4,2,3,0,1:T(2,128)}), f32[1,16,2,65,128]{4,2,3,0,1:T(2,128)S(1)}, u32[]{:S(2)}, u32[]{:S(2)}) async-start(f32[1,16,2,65,128]{4,2,3,0,1:T(2,128)} %maximum_maximum_fusion), calls=%async_computation.1 | async-start | bytes 2129920 | tf_op jit(solution)/shard_map/all_to_all | solution.py:98
Sparse Core Ops, SparseCore 0:
  9.1 43.8 all-gather.2
  54.7 38.9 all-gather.4

commit v2 on v1

--- a/solution.py
+++ b/solution.py
@@ -23,12 +23,12 @@
     return reachable > 0.5
 
 
-def row_reduce(partial, axis_name):
+def row_reduce(partial, axis_name, sent=jnp.float32):
     count = lax.axis_size(axis_name)
     rows, cols = partial.shape
-    pieces = partial.reshape(rows, count, cols // count).transpose(1, 0, 2)
+    pieces = partial.reshape(rows, count, cols // count).transpose(1, 0, 2).astype(sent)
     received = lax.all_to_all(pieces, axis_name, 0, 0)
-    return jnp.sum(received, axis=0)
+    return jnp.sum(received.astype(jnp.float32), axis=0)
 
 
 def shards(hidden_in, norm_gain, w_qkv, w_out, cache_k, value_cache, cache_len, parents):
@@ -76,7 +76,7 @@
         )
         visible = (slot_ids < length)[None, None, None, :]
         scores = jnp.where(visible, scores, masked_score)
-        highest = jnp.max(scores, axis=-1)
+        highest = jnp.max(scores, axis=-1).astype(jnp.bfloat16).astype(jnp.float32)
         weights = jnp.where(visible, jnp.exp(scores - highest[..., None]), 0.0)
         totals = jnp.sum(weights, axis=-1)
         blended = jnp.einsum(
@@ -91,11 +91,11 @@
         )
         return jnp.concatenate(
             [blended.reshape(QUERY_HEADS, draft_tree, HEAD_SIZE), stats[:, None, :]], axis=1
-        )
+        ).astype(jnp.bfloat16)
 
     packed = lax.map(cache_part, (query_block, cache_k, value_cache, cache_len))
     packed = packed.reshape(request_list, row_count, heads_dev, draft_tree + 1, HEAD_SIZE)
-    gathered = lax.all_to_all(packed, "row", 1, 1)
+    gathered = lax.all_to_all(packed, "row", 1, 1).astype(jnp.float32)
     block_blend = gathered[:, :, :, :draft_tree, :]
     block_max = gathered[:, :, :, draft_tree, :draft_tree]
     block_total = gathered[:, :, :, draft_tree, draft_tree : 2 * draft_tree]
@@ -136,7 +136,7 @@
         lax.all_gather(w_out, "col", axis=1, tiled=True),
         preferred_element_type=jnp.float32,
     )
-    return row_reduce(partial_out, "row").astype(jnp.bfloat16)
+    return row_reduce(partial_out, "row", jnp.bfloat16).astype(jnp.bfloat16)
 
 
 def solution(mesh):

time: 165 us -> 172 us (1.042)
  waiting for transfers between devices: 33.2 us -> 41.3 us
  blocking collectives: 78.9 us -> 75.3 us
  other arithmetic: 7.3 us -> 10.2 us
    all_gather x1, waiting for transfers between devices: 0.02 us -> 25.7 us  [shards(): lax.all_gather(w_out, 'col', axis=1, tiled=True)]
    all_to_all x1, waiting for transfers between devices: 20.1 us -> 0.01 us  [row_reduce(): received = lax.all_to_all(pieces, axis_name, 0, 0)]
    all_to_all x1, blocking collectives: 15.9 us -> 13.1 us  [row_reduce(): received = lax.all_to_all(pieces, axis_name, 0, 0)]
    all_to_all x1, waiting for transfers between devices: 5.91 us -> 8.38 us  [shards(): gathered = lax.all_to_all(packed, 'row', 1, 1).astype(jnp.float32)]
    unnamed x13 -> x17, local copies, waits for them, and re-layouts: 4.22 us -> 2.09 us
  transfers between devices with their start and end apart: 4 -> 4, of which waited for: 3 -> 3; matrix products, arithmetic and copies ran while one was open for 11% -> 7% of each run, Pallas kernels for 0% -> 0%
where the time goes in v2:
time: 172 us; the launch traced here: 171 us
  blocking collectives  75.3 us (44%)
  waiting for transfers between devices  41.3 us (24%)
  between operations  14.3 us (8%)
  starting transfers between devices  12.9 us (8%)
  other arithmetic  10.2 us (6%)
  local copies, waits for them, and re-layouts  9.9 us (6%)
  matrix products  7.1 us (4%)
    psum x1, blocking collectives, shards(): squares = lax.psum(jnp.sum(features * features, axis=1), 'row')  37.7 us
    all_gather x1, waiting for transfers between devices, shards(): lax.all_gather(w_out, 'col', axis=1, tiled=True)  25.7 us
    all_gather x1, blocking collectives, shards(): projected_output = lax.all_gather(summed, 'row', axis=1, tiled=True)  24.5 us
    all_to_all x1, blocking collectives, row_reduce(): received = lax.all_to_all(pieces, axis_name, 0, 0)  13.1 us
    all_to_all x1, waiting for transfers between devices, shards(): gathered = lax.all_to_all(packed, 'row', 1, 1).astype(jnp.float32)  8.38 us
    all_to_all x1, starting transfers between devices, row_reduce(): received = lax.all_to_all(pieces, axis_name, 0, 0)  7.4 us
    all_gather x1, waiting for transfers between devices, shards(): lax.all_gather(w_qkv, 'col', axis=1, tiled=True)  5.77 us
    all_to_all x1, starting transfers between devices, shards(): gathered = lax.all_to_all(packed, 'row', 1, 1).astype(jnp.float32)  5.41 us
  transfers between devices with their start and end apart: 4, of which 3 were waited for; matrix products, arithmetic and copies ran while one was open for 7% of the time, Pallas kernels for 0%

profile of v2, /device:TPU:2, one launch (start us, length us, event | category | flops | bytes accessed | tf_op | source)
XLA Modules:
  0.0 170.9 jit_solution(12436564671525383123)
XLA Ops:
  6.5 0.7 all-gather.3.cloned.1.call-update
  7.3 0.7 all-gather.5.cloned.1.call-update
  8.0 0.7 convert_element_type.135
  8.7 0.9 fusion.24
  9.5 37.7 %psum.7 = f32[64]{0:T(128)S(1)} all-reduce(f32[64]{0:T(128)S(1)} %fusion.24), channel_id=1, replica_groups=mesh['row'=16,'col'=16] {'row'}, use_global_device_ids=true, to_apply=%region_1.0 | all-reduce | flops 64 | bytes 512 | tf_op jit(solution)/shard_map/psum | solution.py:45
  47.2 5.8 %all-gather.3.cloned.1.call-done = bf16[256,6144]{1,0:T(8,128)(2,1)} async-done(((bf16[256,384]{1,0:T(8,128)(2,1)}), bf16[256,6144]{1,0:T(8,128)(2,1)}) %all-gather.3.cloned.1.call-update) | async-done | bytes 3145744 | tf_op jit(solution)/shard_map/all_gather | solution.py:51
  53.0 2.6 %fusion.30 = f32[64,6144]{1,0:T(8,128)S(1)} fusion(bf16[256,6144]{1,0:T(8,128)(2,1)} %all-gather.3.cloned.1.call-done, bf16[64,256]{1,0:T(8,128)(2,1)} %param.8, f32[256]{0:T(256)S(1)} %convert_element_type.135, f32[64]{0:T(128)S(1)} %add_rsqrt_fusion), kind=kOutput, calls=%fused_computation.53 | convolution fusion | flops 201392128 | bytes 4752640 | tf_op jit(solution)/shard_map/dot_general | solution.py:50
  55.6 1.3 copy.93
  56.9 7.4 %all-to-all-start = ((f32[16,64,384]{2,1,0:T(8,128)}), f32[16,64,384]{2,1,0:T(8,128)}, u32[]{:S(2)}, u32[]{:S(2)}) async-start(f32[16,64,384]{2,1,0:T(8,128)} %bitcast.98), calls=%async_computation | async-start | bytes 3145728 | tf_op jit(solution)/shard_map/all_to_all | solution.py:30
  65.0 0.9 copy.70
  65.9 0.9 copy.71
  67.0 0.2 convolution_compare_fusion.5
  67.9 25.7 %all-gather.5.cloned.1.call-done = bf16[256,4096]{1,0:T(8,128)(2,1)} async-done(((bf16[256,256]{1,0:T(8,128)(2,1)}), bf16[256,4096]{1,0:T(8,128)(2,1)}) %all-gather.5.cloned.1.call-update) | async-done | bytes 2097168 | tf_op jit(solution)/shard_map/all_gather | solution.py:136
  93.7 3.3 %copy.58 = bf16[4096,256]{1,0:T(8,128)(2,1)S(1)} copy(bf16[4096,256]{0,1:T(8,128)(2,1)} %bitcast.102) | data formatting | bytes 4194304 | tf_op jit(solution)/shard_map/dot_general | solution.py:134
  96.9 1.5 reduce_sum.68
  98.4 24.5 %all_gather.10 = bf16[64,6144]{1,0:T(8,128)(2,1)S(1)} all-gather(bf16[64,384]{1,0:T(8,128)(2,1)S(1)} %reduce_sum.68), channel_id=1, replica_groups=mesh['row'=16,'col'=16] {'row'}, dimensions={1}, use_global_device_ids=true | all-gather | bytes 835584 | tf_op jit(solution)/shard_map/all_gather | solution.py:54
  123.1 1.2 squeeze.24
  124.2 1.9 %bitcast_reduce_fusion = (bf16[8,4,64]{2,1,0:T(4,128)(2,1)S(1)}, f32[8,64,4,256]{3,1,2,0:T(8,128)S(1)}) fusion(pred[256]{0:T(512)(128)(4,1)S(1)} %add_compare_fusion, bf16[256,8,128,1]{2,1,0,3:T(8,128)(2,1)} %bitcast.109, bf16[64,8,4,128]{3,2,1,0:T(4,128)(2,1)} %squeeze.24), kind=kOutput, calls=%fused_computation.1 | convolution fusion | flops 135788544 | bytes 3150080 | tf_op jit(solution)/shard_map/while/body/eval_jaxpr/tkgd,pkd->kgtp/dot_general | solution.py:72
  126.1 0.9 fusion.2
  127.1 0.7 convolution_convert_fusion
  127.8 0.5 copy.47
  128.4 1.5 pad_maximum_fusion
  129.9 5.4 %all-to-all-start.1 = ((bf16[1,16,2,65,128]{4,2,3,0,1:T(2,128)(2,1)}), bf16[1,16,2,65,128]{4,2,3,0,1:T(2,128)(2,1)}, u32[]{:S(2)}, u32[]{:S(2)}) async-start(bf16[1,16,2,65,128]{4,2,3,0,1:T(2,128)(2,1)} %pad_maximum_fusion), calls=%async_computation.1 | async-start | bytes 1064960 | tf_op jit(solution)/shard_map/all_to_all | solution.py:98
  135.6 0.2 fusion.52
  135.8 8.4 %all-to-all-done.1 = bf16[1,16,2,65,128]{4,2,3,0,1:T(2,128)(2,1)} async-done(((bf16[1,16,2,65,128]{4,2,3,0,1:T(2,128)(2,1)}), bf16[1,16,2,65,128]{4,2,3,0,1:T(2,128)(2,1)}, u32[]{:S(2)}, u32[]{:S(2)}) %all-to-all-start.1) | async-done | bytes 532512 | tf_op jit(solution)/shard_map/all_to_all | solution.py:98
  144.2 1.4 convert_element_type.142
  145.8 1.0 copy.53
  146.8 2.2 %fusion.13 = f32[2,64,128]{2,0,1:T(2,128)S(1)} fusion(f32[1,16,2,65,128]{4,2,3,0,1:T(2,128)S(1)} %convert_element_type.142, f32[16,2,64]{1,2,0:T(8,128)} %copy.53), kind=kLoop, calls=%fused_computation.27 | loop fusion | flops 507904 | bytes 1122304 | tf_op jit(solution)/shard_map/reduce_sum | solution.py:130
  149.2 0.2 fusion.9
  149.5 0.7 fusion.4
  150.3 13.1 %all_to_all.15 = bf16[16,64,256]{2,1,0:T(8,128)(2,1)S(1)} all-to-all(bf16[16,64,256]{2,1,0:T(8,128)(2,1)S(1)} %fusion.4), channel_id=1, replica_groups=mesh['row'=16,'col'=16] {'row'}, dimensions={0} | all-to-all | bytes 1048576 | tf_op jit(solution)/shard_map/all_to_all | solution.py:30
  163.4 0.7 reduce_sum.73
  (41 shorter events, 1.9 us)
Async XLA Ops:
  6.5 46.5 %all-gather.3.cloned.1.call-start = ((), (), s32[]{:S(2)}) async-start(), calls=%async_computation.3 | async-start | bytes 3342336 | tf_op jit(solution)/shard_map/all_gather | solution.py:51
  7.3 86.4 %all-gather.5.cloned.1.call-start = ((), (), s32[]{:S(2)}) async-start(), calls=%async_computation.4 | async-start | bytes 2228224 | tf_op jit(solution)/shard_map/all_gather | solution.py:136
  56.9 8.1 %copy-start = (bf16[1,256,1024]{2,1,0:T(8,128)(2,1)S(1)}, bf16[1,256,1024]{2,1,0:T(8,128)(2,1)}, u32[]{:S(2)}) copy-start(bf16[1,256,1024]{2,1,0:T(8,128)(2,1)} %param.12) | copy-start | bytes 1572868
  56.9 9.0 %copy-start.1 = (bf16[1,256,1024]{2,1,0:T(8,128)(2,1)S(1)}, bf16[1,256,1024]{2,1,0:T(8,128)(2,1)}, u32[]{:S(2)}) copy-start(bf16[1,256,1024]{2,1,0:T(8,128)(2,1)} %param.13) | copy-start | bytes 1572868
  56.9 9.9 %copy-start.5 = (s32[1,64]{1,0:T(1,128)S(1)}, s32[1,64]{1,0:T(1,128)}, u32[]{:S(2)}) copy-start(s32[1,64]{1,0:T(1,128)} %param.15) | copy-start | bytes 772
  56.9 40.0 %all-to-all-start = ((f32[16,64,384]{2,1,0:T(8,128)}), f32[16,64,384]{2,1,0:T(8,128)}, u32[]{:S(2)}, u32[]{:S(2)}) async-start(f32[16,64,384]{2,1,0:T(8,128)} %bitcast.98), calls=%async_computation | async-start | bytes 3145728 | tf_op jit(solution)/shard_map/all_to_all | solution.py:30
  67.9 67.9 %copy-start.3 = (pred[64,64]{0,1:T(8,128)(4,1)}, pred[64,64]{0,1:T(8,128)(4,1)S(1)}, u32[]{:S(2)}) copy-start(pred[64,64]{0,1:T(8,128)(4,1)S(1)} %copy.50) | copy-start | bytes 12292
  124.2 2.8 %copy-start.2 = (bf16[32,8,8,128]{3,2,1,0:T(8,128)(2,1)S(1)}, bf16[32,8,8,128]{3,2,1,0:T(8,128)(2,1)}, u32[]{:S(2)}) copy-start(bf16[32,8,8,128]{3,2,1,0:T(8,128)(2,1)} %copy.71) | copy-start | bytes 1572868
  129.9 14.3 %all-to-all-start.1 = ((bf16[1,16,2,65,128]{4,2,3,0,1:T(2,128)(2,1)}), bf16[1,16,2,65,128]{4,2,3,0,1:T(2,128)(2,1)}, u32[]{:S(2)}, u32[]{:S(2)}) async-start(bf16[1,16,2,65,128]{4,2,3,0,1:T(2,128)(2,1)} %pad_maximum_fusion), calls=%async_computation.1 | async-start | bytes 1064960 | tf_op jit(solution)/shard_map/all_to_all | solution.py:98
  135.8 13.4 %copy-start.4 = (pred[64,64]{0,1:T(8,128)(4,1)S(1)}, pred[64,64]{0,1:T(8,128)(4,1)}, u32[]{:S(2)}) copy-start(pred[64,64]{0,1:T(8,128)(4,1)} %copy-done.3) | copy-start | bytes 12292
Sparse Core Ops, SparseCore 0:
  9.1 43.8 all-gather.2
  54.7 38.8 all-gather.4

commit v3 on v2

--- a/solution.py
+++ b/solution.py
@@ -31,6 +31,12 @@
     return jnp.sum(received.astype(jnp.float32), axis=0)
 
 
+def row_gather(value, axis_name):
+    count = lax.axis_size(axis_name)
+    copies = jnp.broadcast_to(value[None], (count,) + value.shape)
+    return lax.all_to_all(copies, axis_name, 0, 0)
+
+
 def shards(hidden_in, norm_gain, w_qkv, w_out, cache_k, value_cache, cache_len, parents):
     rows_here = hidden_in.shape[0]
     request_list = cache_k.shape[0]
@@ -42,7 +48,7 @@
     row_index = lax.axis_index("row")
     score_scale = HEAD_SIZE ** (-0.5)
     features = hidden_in.astype(jnp.float32)
-    squares = lax.psum(jnp.sum(features * features, axis=1), "row")
+    squares = jnp.sum(row_gather(jnp.sum(features * features, axis=1), "row"), axis=0)
     row_scale = lax.rsqrt(squares / D + 1e-05)
     normed = (features * row_scale[:, None] * norm_gain.astype(jnp.float32)[None, :]).astype(
         jnp.bfloat16
@@ -51,7 +57,7 @@
         normed, lax.all_gather(w_qkv, "col", axis=1, tiled=True), preferred_element_type=jnp.float32
     )
     summed = row_reduce(partial_value, "row").astype(jnp.bfloat16)
-    projected_output = lax.all_gather(summed, "row", axis=1, tiled=True)
+    projected_output = row_gather(summed, "row").transpose(1, 0, 2).reshape(rows_here, -1)
     query_block = projected_output[:, : QUERY_HEADS * HEAD_SIZE].reshape(
         request_list, draft_tree, KEY_VALUE_HEADS, head_groups, HEAD_SIZE
     )

time: 172 us -> 156 us (0.907)
  blocking collectives: 75.3 us -> 13.1 us
  waiting for transfers between devices: 41.3 us -> 73 us
  starting transfers between devices: 12.9 us -> 27.3 us
    psum x1 -> x0, blocking collectives: 37.7 us -> none  [shards(): squares = lax.psum(jnp.sum(features * features, axis=1), 'row')]
    all_gather x1, waiting for transfers between devices: 25.7 us -> 0.02 us  [shards(): lax.all_gather(w_out, 'col', axis=1, tiled=True)]
    all_gather x1 -> x0, blocking collectives: 24.5 us -> none  [shards(): projected_output = lax.all_gather(summed, 'row', axis=1, tiled=True)]
    all_gather x1, waiting for transfers between devices: 5.77 us -> 29.9 us  [shards(): lax.all_gather(w_qkv, 'col', axis=1, tiled=True)]
    all_to_all x1, waiting for transfers between devices: 0.01 us -> 21.7 us  [row_reduce(): received = lax.all_to_all(pieces, axis_name, 0, 0)]
    all_to_all x0 -> x2, starting transfers between devices: none -> 14.4 us  [row_gather(): return lax.all_to_all(copies, axis_name, 0, 0)]
    all_to_all x0 -> x2, waiting for transfers between devices: none -> 11.5 us  [row_gather(): return lax.all_to_all(copies, axis_name, 0, 0)]
  transfers between devices with their start and end apart: 4 -> 6, of which waited for: 3 -> 5; matrix products, arithmetic and copies ran while one was open for 7% -> 9% of each run, Pallas kernels for 0% -> 0%
where the time goes in v3:
time: 156 us; the launch traced here: 155 us
  waiting for transfers between devices  73 us (47%)
  starting transfers between devices  27.3 us (18%)
  between operations  14.3 us (9%)
  blocking collectives  13.1 us (8%)
  local copies, waits for them, and re-layouts  11.6 us (7%)
  other arithmetic  8.84 us (6%)
  matrix products  7.09 us (5%)
    all_gather x1, waiting for transfers between devices, shards(): lax.all_gather(w_qkv, 'col', axis=1, tiled=True)  29.9 us
    all_to_all x1, waiting for transfers between devices, row_reduce(): received = lax.all_to_all(pieces, axis_name, 0, 0)  21.7 us
    all_to_all x2, starting transfers between devices, row_gather(): return lax.all_to_all(copies, axis_name, 0, 0)  14.4 us
    all_to_all x1, blocking collectives, row_reduce(): received = lax.all_to_all(pieces, axis_name, 0, 0)  13.1 us
    all_to_all x2, waiting for transfers between devices, row_gather(): return lax.all_to_all(copies, axis_name, 0, 0)  11.5 us
    all_to_all x1, waiting for transfers between devices, shards(): gathered = lax.all_to_all(packed, 'row', 1, 1).astype(jnp.float32)  8.54 us
    all_to_all x1, starting transfers between devices, row_reduce(): received = lax.all_to_all(pieces, axis_name, 0, 0)  7.4 us
    all_to_all x1, starting transfers between devices, shards(): gathered = lax.all_to_all(packed, 'row', 1, 1).astype(jnp.float32)  5.5 us
  transfers between devices with their start and end apart: 6, of which 5 were waited for; matrix products, arithmetic and copies ran while one was open for 9% of the time, Pallas kernels for 0%

profile of v3, /device:TPU:2, one launch (start us, length us, event | category | flops | bytes accessed | tf_op | source)
XLA Modules:
  0.0 155.3 jit_solution(15210442583625811994)
XLA Ops:
  6.5 0.7 all-gather.3.cloned.1.call-update
  7.3 0.7 all-gather.5.cloned.1.call-update
  8.0 0.9 fusion.24
  8.9 0.6 broadcast_in_dim.88
  9.5 7.5 %all-to-all-start = ((f32[16,1,64]{2,1,0:T(1,128)}), f32[16,1,64]{2,1,0:T(1,128)S(1)}, u32[]{:S(2)}, u32[]{:S(2)}) async-start(f32[16,1,64]{2,1,0:T(1,128)} %broadcast_in_dim.88), calls=%async_computation | async-start | bytes 16384 | tf_op jit(solution)/shard_map/all_to_all | solution.py:37
  17.0 0.7 convert_element_type.139
  17.6 5.5 %all-to-all-done = f32[16,1,64]{2,1,0:T(1,128)S(1)} async-done(((f32[16,1,64]{2,1,0:T(1,128)}), f32[16,1,64]{2,1,0:T(1,128)S(1)}, u32[]{:S(2)}, u32[]{:S(2)}) %all-to-all-start) | async-done | bytes 4128 | tf_op jit(solution)/shard_map/all_to_all | solution.py:37
  23.1 29.9 %all-gather.3.cloned.1.call-done = bf16[256,6144]{1,0:T(8,128)(2,1)} async-done(((bf16[256,384]{1,0:T(8,128)(2,1)}), bf16[256,6144]{1,0:T(8,128)(2,1)}) %all-gather.3.cloned.1.call-update) | async-done | bytes 3145744 | tf_op jit(solution)/shard_map/all_gather | solution.py:57
  53.0 2.6 %fusion.30 = f32[64,6144]{1,0:T(8,128)S(1)} fusion(bf16[256,6144]{1,0:T(8,128)(2,1)} %all-gather.3.cloned.1.call-done, bf16[64,256]{1,0:T(8,128)(2,1)} %param.8, f32[256]{0:T(256)S(1)} %convert_element_type.139, f32[64]{0:T(128)S(1)} %add_rsqrt_fusion), kind=kOutput, calls=%fused_computation.53 | convolution fusion | flops 201392128 | bytes 4752640 | tf_op jit(solution)/shard_map/dot_general | solution.py:56
  55.6 1.3 copy.131
  56.9 7.4 %all-to-all-start.1 = ((f32[16,64,384]{2,1,0:T(8,128)}), f32[16,64,384]{2,1,0:T(8,128)S(1)}, u32[]{:S(2)}, u32[]{:S(2)}) async-start(f32[16,64,384]{2,1,0:T(8,128)} %bitcast.102), calls=%async_computation.1 | async-start | bytes 3145728 | tf_op jit(solution)/shard_map/all_to_all | solution.py:30
  64.5 21.7 %all-to-all-done.1 = f32[16,64,384]{2,1,0:T(8,128)S(1)} async-done(((f32[16,64,384]{2,1,0:T(8,128)}), f32[16,64,384]{2,1,0:T(8,128)S(1)}, u32[]{:S(2)}, u32[]{:S(2)}) %all-to-all-start.1) | async-done | bytes 1572896 | tf_op jit(solution)/shard_map/all_to_all | solution.py:30
  86.3 1.0 broadcast_in_dim.89
  87.3 6.9 %all-to-all-start.2 = ((bf16[16,64,384]{2,1,0:T(8,128)(2,1)}), bf16[16,64,384]{2,1,0:T(8,128)(2,1)S(1)}, u32[]{:S(2)}, u32[]{:S(2)}) async-start(bf16[16,64,384]{2,1,0:T(8,128)(2,1)} %broadcast_in_dim.89), calls=%async_computation.2 | async-start | bytes 1572864 | tf_op jit(solution)/shard_map/all_to_all | solution.py:37
  95.1 0.9 copy.108
  96.0 0.9 copy.109
  97.7 3.3 %copy.95 = bf16[4096,256]{1,0:T(8,128)(2,1)S(1)} copy(bf16[4096,256]{0,1:T(8,128)(2,1)} %bitcast.109) | data formatting | bytes 4194304 | tf_op jit(solution)/shard_map/dot_general | solution.py:140
  101.0 6.0 %all-to-all-done.2 = bf16[16,64,384]{2,1,0:T(8,128)(2,1)S(1)} async-done(((bf16[16,64,384]{2,1,0:T(8,128)(2,1)}), bf16[16,64,384]{2,1,0:T(8,128)(2,1)S(1)}, u32[]{:S(2)}, u32[]{:S(2)}) %all-to-all-start.2) | async-done | bytes 786464 | tf_op jit(solution)/shard_map/all_to_all | solution.py:37
  107.2 1.2 squeeze.24
  108.4 1.9 %bitcast_reduce_fusion = (bf16[8,4,64]{2,1,0:T(4,128)(2,1)S(1)}, f32[8,64,4,256]{3,1,2,0:T(8,128)S(1)}) fusion(pred[256]{0:T(512)(128)(4,1)S(1)} %add_compare_fusion, bf16[256,8,128,1]{2,1,0,3:T(8,128)(2,1)} %bitcast.116, bf16[64,8,4,128]{3,2,1,0:T(4,128)(2,1)} %squeeze.24), kind=kOutput, calls=%fused_computation.1 | convolution fusion | flops 135788544 | bytes 3150080 | tf_op jit(solution)/shard_map/while/body/eval_jaxpr/tkgd,pkd->kgtp/dot_general | solution.py:78
  110.3 0.9 fusion.2
  111.2 0.7 convolution_convert_fusion
  111.9 0.5 copy.84
  112.5 1.5 pad_maximum_fusion
  114.1 5.5 %all-to-all-start.3 = ((bf16[1,16,2,65,128]{4,2,3,0,1:T(2,128)(2,1)}), bf16[1,16,2,65,128]{4,2,3,0,1:T(2,128)(2,1)}, u32[]{:S(2)}, u32[]{:S(2)}) async-start(bf16[1,16,2,65,128]{4,2,3,0,1:T(2,128)(2,1)} %pad_maximum_fusion), calls=%async_computation.3 | async-start | bytes 1064960 | tf_op jit(solution)/shard_map/all_to_all | solution.py:104
  120.1 8.5 %all-to-all-done.3 = bf16[1,16,2,65,128]{4,2,3,0,1:T(2,128)(2,1)} async-done(((bf16[1,16,2,65,128]{4,2,3,0,1:T(2,128)(2,1)}), bf16[1,16,2,65,128]{4,2,3,0,1:T(2,128)(2,1)}, u32[]{:S(2)}, u32[]{:S(2)}) %all-to-all-start.3) | async-done | bytes 532512 | tf_op jit(solution)/shard_map/all_to_all | solution.py:104
  128.6 1.4 convert_element_type.146
  130.2 1.0 copy.90
  131.3 2.2 %fusion.13 = f32[2,64,128]{2,0,1:T(2,128)S(1)} fusion(f32[1,16,2,65,128]{4,2,3,0,1:T(2,128)S(1)} %convert_element_type.146, f32[16,2,64]{1,2,0:T(8,128)} %copy.90), kind=kLoop, calls=%fused_computation.27 | loop fusion | flops 507904 | bytes 1122304 | tf_op jit(solution)/shard_map/reduce_sum | solution.py:136
  133.9 0.8 fusion.4
  134.7 13.1 %all_to_all.26 = bf16[16,64,256]{2,1,0:T(8,128)(2,1)S(1)} all-to-all(bf16[16,64,256]{2,1,0:T(8,128)(2,1)S(1)} %fusion.4), channel_id=1, replica_groups=mesh['row'=16,'col'=16] {'row'}, dimensions={0} | all-to-all | bytes 1048576 | tf_op jit(solution)/shard_map/all_to_all | solution.py:30
  147.8 0.7 reduce_sum.83
  (47 shorter events, 2.7 us)
Async XLA Ops:
  6.5 46.5 %all-gather.3.cloned.1.call-start = ((), (), s32[]{:S(2)}) async-start(), calls=%async_computation.5 | async-start | bytes 3342336 | tf_op jit(solution)/shard_map/all_gather | solution.py:57
  7.3 90.5 %all-gather.5.cloned.1.call-start = ((), (), s32[]{:S(2)}) async-start(), calls=%async_computation.6 | async-start | bytes 2228224 | tf_op jit(solution)/shard_map/all_gather | solution.py:142
  9.5 13.6 %all-to-all-start = ((f32[16,1,64]{2,1,0:T(1,128)}), f32[16,1,64]{2,1,0:T(1,128)S(1)}, u32[]{:S(2)}, u32[]{:S(2)}) async-start(f32[16,1,64]{2,1,0:T(1,128)} %broadcast_in_dim.88), calls=%async_computation | async-start | bytes 16384 | tf_op jit(solution)/shard_map/all_to_all | solution.py:37
  56.9 7.4 %copy-start.5 = (s32[1,64]{1,0:T(1,128)S(1)}, s32[1,64]{1,0:T(1,128)}, u32[]{:S(2)}) copy-start(s32[1,64]{1,0:T(1,128)} %param.15) | copy-start | bytes 772
  56.9 29.3 %all-to-all-start.1 = ((f32[16,64,384]{2,1,0:T(8,128)}), f32[16,64,384]{2,1,0:T(8,128)S(1)}, u32[]{:S(2)}, u32[]{:S(2)}) async-start(f32[16,64,384]{2,1,0:T(8,128)} %bitcast.102), calls=%async_computation.1 | async-start | bytes 3145728 | tf_op jit(solution)/shard_map/all_to_all | solution.py:30
  64.3 30.7 %copy-start = (bf16[1,256,1024]{2,1,0:T(8,128)(2,1)S(1)}, bf16[1,256,1024]{2,1,0:T(8,128)(2,1)}, u32[]{:S(2)}) copy-start(bf16[1,256,1024]{2,1,0:T(8,128)(2,1)} %param.12) | copy-start | bytes 1572868
  86.3 9.7 %copy-start.1 = (bf16[1,256,1024]{2,1,0:T(8,128)(2,1)S(1)}, bf16[1,256,1024]{2,1,0:T(8,128)(2,1)}, u32[]{:S(2)}) copy-start(bf16[1,256,1024]{2,1,0:T(8,128)(2,1)} %param.13) | copy-start | bytes 1572868
  87.3 19.7 %all-to-all-start.2 = ((bf16[16,64,384]{2,1,0:T(8,128)(2,1)}), bf16[16,64,384]{2,1,0:T(8,128)(2,1)S(1)}, u32[]{:S(2)}, u32[]{:S(2)}) async-start(bf16[16,64,384]{2,1,0:T(8,128)(2,1)} %broadcast_in_dim.89), calls=%async_computation.2 | async-start | bytes 1572864 | tf_op jit(solution)/shard_map/all_to_all | solution.py:37
  97.7 22.4 %copy-start.3 = (pred[64,64]{0,1:T(8,128)(4,1)}, pred[64,64]{0,1:T(8,128)(4,1)S(1)}, u32[]{:S(2)}) copy-start(pred[64,64]{0,1:T(8,128)(4,1)S(1)} %copy.87) | copy-start | bytes 12292
  108.4 2.8 %copy-start.2 = (bf16[32,8,8,128]{3,2,1,0:T(8,128)(2,1)S(1)}, bf16[32,8,8,128]{3,2,1,0:T(8,128)(2,1)}, u32[]{:S(2)}) copy-start(bf16[32,8,8,128]{3,2,1,0:T(8,128)(2,1)} %copy.109) | copy-start | bytes 1572868
  114.1 14.6 %all-to-all-start.3 = ((bf16[1,16,2,65,128]{4,2,3,0,1:T(2,128)(2,1)}), bf16[1,16,2,65,128]{4,2,3,0,1:T(2,128)(2,1)}, u32[]{:S(2)}, u32[]{:S(2)}) async-start(bf16[1,16,2,65,128]{4,2,3,0,1:T(2,128)(2,1)} %pad_maximum_fusion), calls=%async_computation.3 | async-start | bytes 1064960 | tf_op jit(solution)/shard_map/all_to_all | solution.py:104
  120.1 13.5 %copy-start.4 = (pred[64,64]{0,1:T(8,128)(4,1)S(1)}, pred[64,64]{0,1:T(8,128)(4,1)}, u32[]{:S(2)}) copy-start(pred[64,64]{0,1:T(8,128)(4,1)} %copy-done.3) | copy-start | bytes 12292
Sparse Core Ops, SparseCore 0:
  9.1 43.8 all-gather.2
  54.7 38.8 all-gather.4

commit v4 on v3

--- a/solution.py
+++ b/solution.py
@@ -53,10 +53,17 @@
     normed = (features * row_scale[:, None] * norm_gain.astype(jnp.float32)[None, :]).astype(
         jnp.bfloat16
     )
-    partial_value = jnp.dot(
-        normed, lax.all_gather(w_qkv, "col", axis=1, tiled=True), preferred_element_type=jnp.float32
+    col_count = lax.axis_size("col")
+    all_tokens = row_gather(normed, "col").reshape(col_count * rows_here, -1)
+    partial_value = jnp.dot(all_tokens, w_qkv, preferred_element_type=jnp.float32)
+    received = lax.all_to_all(
+        partial_value.reshape(col_count, rows_here, -1), "row", 0, 0
     )
-    summed = row_reduce(partial_value, "row").astype(jnp.bfloat16)
+    summed = jnp.sum(received, axis=0).astype(jnp.bfloat16)
+    transpose = [
+        (r * col_count + c, c * col_count + r) for r in range(row_count) for c in range(col_count)
+    ]
+    summed = lax.ppermute(summed, ("row", "col"), transpose)
     projected_output = row_gather(summed, "row").transpose(1, 0, 2).reshape(rows_here, -1)
     query_block = projected_output[:, : QUERY_HEADS * HEAD_SIZE].reshape(
         request_list, draft_tree, KEY_VALUE_HEADS, head_groups, HEAD_SIZE

time: 156 us -> 160 us (1.026)
  waiting for transfers between devices: 73 us -> 48.5 us
  blocking collectives: 13.1 us -> 37.5 us
  starting transfers between devices: 27.3 us -> 37.1 us
  local copies, waits for them, and re-layouts: 11.6 us -> 7.92 us
    all_gather x1 -> x0, waiting for transfers between devices: 29.9 us -> none  [shards(): lax.all_gather(w_qkv, 'col', axis=1, tiled=True)]
    all_to_all x0 -> x1, blocking collectives: none -> 24.3 us  [row_gather(): return lax.all_to_all(copies, axis_name, 0, 0)]
    ppermute x0 -> x1, starting transfers between devices: none -> 6.68 us  [shards(): summed = lax.ppermute(summed, ('row', 'col'), transpose)]
    all_to_all x2, starting transfers between devices: 14.4 us -> 20.5 us  [row_gather(): return lax.all_to_all(copies, axis_name, 0, 0)]
    all_to_all x2, waiting for transfers between devices: 11.5 us -> 15.6 us  [row_gather(): return lax.all_to_all(copies, axis_name, 0, 0)]
    all_to_all x1, starting transfers between devices: 7.4 us -> 5.09 us  [shards(): lax.all_to_all(partial_value.reshape(col_count, rows_here, -1), 'row', 0, 0)]
    ppermute x0 -> x1, waiting for transfers between devices: none -> 2.3 us  [shards(): summed = lax.ppermute(summed, ('row', 'col'), transpose)]
    unnamed x17 -> x13, local copies, waits for them, and re-layouts: 2.1 us -> 0.46 us
  transfers between devices with their start and end apart: 6 -> 6, of which waited for: 5 -> 5; matrix products, arithmetic and copies ran while one was open for 9% -> 8% of each run, Pallas kernels for 0% -> 0%
where the time goes in v4:
time: 160 us; the launch traced here: 159 us
  waiting for transfers between devices  48.5 us (30%)
  blocking collectives  37.5 us (23%)
  starting transfers between devices  37.1 us (23%)
  between operations  14.4 us (9%)
  local copies, waits for them, and re-layouts  7.92 us (5%)
  other arithmetic  7.72 us (5%)
  matrix products  5.85 us (4%)
    all_to_all x1, blocking collectives, row_gather(): return lax.all_to_all(copies, axis_name, 0, 0)  24.3 us
    all_to_all x1, waiting for transfers between devices, shards(): lax.all_to_all(partial_value.reshape(col_count, rows_here, -1), 'row', 0, 0)  21.6 us
    all_to_all x2, starting transfers between devices, row_gather(): return lax.all_to_all(copies, axis_name, 0, 0)  20.5 us
    all_to_all x2, waiting for transfers between devices, row_gather(): return lax.all_to_all(copies, axis_name, 0, 0)  15.6 us
    all_to_all x1, blocking collectives, row_reduce(): received = lax.all_to_all(pieces, axis_name, 0, 0)  13.2 us
    all_to_all x1, waiting for transfers between devices, shards(): gathered = lax.all_to_all(packed, 'row', 1, 1).astype(jnp.float32)  8.31 us
    ppermute x1, starting transfers between devices, shards(): summed = lax.ppermute(summed, ('row', 'col'), transpose)  6.68 us
    all_to_all x1, starting transfers between devices, shards(): lax.all_to_all(partial_value.reshape(col_count, rows_here, -1), 'row', 0, 0)  5.09 us
  transfers between devices with their start and end apart: 6, of which 5 were waited for; matrix products, arithmetic and copies ran while one was open for 8% of the time, Pallas kernels for 0%

profile of v4, /device:TPU:2, one launch (start us, length us, event | category | flops | bytes accessed | tf_op | source)
XLA Modules:
  0.0 159.0 jit_solution(2020960412234748342)
XLA Ops:
  6.5 0.9 fusion.26
  7.4 0.6 broadcast_in_dim.94
  8.1 7.5 %all-to-all-start = ((f32[16,1,64]{2,1,0:T(1,128)}), f32[16,1,64]{2,1,0:T(1,128)S(1)}, u32[]{:S(2)}, u32[]{:S(2)}) async-start(f32[16,1,64]{2,1,0:T(1,128)} %broadcast_in_dim.94), calls=%async_computation | async-start | bytes 16384 | tf_op jit(solution)/shard_map/all_to_all | solution.py:37
  15.5 0.7 convert_element_type.135
  16.2 5.5 %all-to-all-done = f32[16,1,64]{2,1,0:T(1,128)S(1)} async-done(((f32[16,1,64]{2,1,0:T(1,128)}), f32[16,1,64]{2,1,0:T(1,128)S(1)}, u32[]{:S(2)}, u32[]{:S(2)}) %all-to-all-start) | async-done | bytes 4128 | tf_op jit(solution)/shard_map/all_to_all | solution.py:37
  21.7 0.8 fusion.28
  22.6 24.3 %all_to_all.31 = bf16[16,64,256]{2,1,0:T(8,128)(2,1)S(1)} all-to-all(bf16[16,64,256]{2,1,0:T(8,128)(2,1)S(1)} %broadcast_in_dim.95), channel_id=1, replica_groups=mesh['row'=16,'col'=16] {'col'}, dimensions={0} | all-to-all | bytes 1048576 | tf_op jit(solution)/shard_map/all_to_all | solution.py:37
  46.9 1.6 fusion.24
  48.5 5.1 %all-to-all-start.2 = ((f32[16,64,384]{2,1,0:T(8,128)}), f32[16,64,384]{2,1,0:T(8,128)S(1)}, u32[]{:S(2)}, u32[]{:S(2)}) async-start(f32[16,64,384]{2,1,0:T(8,128)} %fusion.24), calls=%async_computation.2 | async-start | bytes 3145728 | tf_op jit(solution)/shard_map/all_to_all | solution.py:59
  53.6 0.7 all-gather.2.cloned.1.call-update
  54.3 21.6 %all-to-all-done.2 = f32[16,64,384]{2,1,0:T(8,128)S(1)} async-done(((f32[16,64,384]{2,1,0:T(8,128)}), f32[16,64,384]{2,1,0:T(8,128)S(1)}, u32[]{:S(2)}, u32[]{:S(2)}) %all-to-all-start.2) | async-done | bytes 1572896 | tf_op jit(solution)/shard_map/all_to_all | solution.py:59
  76.0 6.7 %collective-permute-start = (bf16[64,384]{1,0:T(8,128)(2,1)S(1)}, bf16[64,384]{1,0:T(8,128)(2,1)S(1)}, u32[]{:S(2)}, u32[]{:S(2)}) collective-permute-start(bf16[64,384]{1,0:T(8,128)(2,1)S(1)} %reduce_sum.78), channel_id=1, source_target_pairs={{0,0},{1,16},{2,32},{3,48},{4,64},{5,80},{6,96},{7,112},{8,128},{9... | collective-permute-start | bytes 147464 | tf_op jit(solution)/shard_map/ppermute | solution.py:66
  82.8 2.3 %collective-permute-done = bf16[64,384]{1,0:T(8,128)(2,1)S(1)} collective-permute-done((bf16[64,384]{1,0:T(8,128)(2,1)S(1)}, bf16[64,384]{1,0:T(8,128)(2,1)S(1)}, u32[]{:S(2)}, u32[]{:S(2)}) %collective-permute-start) | collective-permute-done | bytes 49184 | tf_op jit(solution)/shard_map/ppermute | solution.py:66
  85.1 1.0 broadcast_in_dim.96
  86.2 13.0 %all-to-all-start.3 = ((bf16[16,64,384]{2,1,0:T(8,128)(2,1)}), bf16[16,64,384]{2,1,0:T(8,128)(2,1)S(1)}, u32[]{:S(2)}, u32[]{:S(2)}) async-start(bf16[16,64,384]{2,1,0:T(8,128)(2,1)} %broadcast_in_dim.96), calls=%async_computation.3 | async-start | bytes 1572864 | tf_op jit(solution)/shard_map/all_to_all | solution.py:37
  101.0 10.2 %all-to-all-done.3 = bf16[16,64,384]{2,1,0:T(8,128)(2,1)S(1)} async-done(((bf16[16,64,384]{2,1,0:T(8,128)(2,1)}), bf16[16,64,384]{2,1,0:T(8,128)(2,1)S(1)}, u32[]{:S(2)}, u32[]{:S(2)}) %all-to-all-start.3) | async-done | bytes 786464 | tf_op jit(solution)/shard_map/all_to_all | solution.py:37
  111.4 1.2 squeeze.24
  112.6 1.7 %bitcast_reduce_fusion = (bf16[8,4,64]{2,1,0:T(4,128)(2,1)S(1)}, f32[8,64,4,256]{3,1,2,0:T(8,128)S(1)}) fusion(pred[256]{0:T(512)(128)(4,1)S(1)} %add_compare_fusion, bf16[256,8,128,1]{2,1,0,3:T(8,128)(2,1)S(1)} %bitcast.111, bf16[64,8,4,128]{3,2,1,0:T(4,128)(2,1)} %squeeze.24), kind=kOutput, calls=%fused_computation.1 | convolution fusion | flops 135788544 | bytes 3150080 | tf_op jit(solution)/shard_map/while/body/eval_jaxpr/tkgd,pkd->kgtp/dot_general | solution.py:85
  114.3 0.7 convolution_convert_fusion
  115.0 0.5 copy.80
  115.5 0.9 fusion.2
  116.5 1.5 pad_maximum_fusion
  118.0 4.8 %all-to-all-start.4 = ((bf16[1,16,2,65,128]{4,2,3,0,1:T(2,128)(2,1)}), bf16[1,16,2,65,128]{4,2,3,0,1:T(2,128)(2,1)S(1)}, u32[]{:S(2)}, u32[]{:S(2)}) async-start(bf16[1,16,2,65,128]{4,2,3,0,1:T(2,128)(2,1)} %pad_maximum_fusion), calls=%async_computation.4 | async-start | bytes 1064960 | tf_op jit(solution)/shard_map/all_to_all | solution.py:111
  123.4 8.3 %all-to-all-done.4 = bf16[1,16,2,65,128]{4,2,3,0,1:T(2,128)(2,1)S(1)} async-done(((bf16[1,16,2,65,128]{4,2,3,0,1:T(2,128)(2,1)}), bf16[1,16,2,65,128]{4,2,3,0,1:T(2,128)(2,1)S(1)}, u32[]{:S(2)}, u32[]{:S(2)}) %all-to-all-start.4) | async-done | bytes 532512 | tf_op jit(solution)/shard_map/all_to_all | solution.py:111
  131.7 0.4 convert_element_type.142
  132.2 0.2 copy.86
  132.5 1.3 fusion.13
  133.9 0.2 fusion.9
  134.3 3.3 %copy.91 = bf16[4096,256]{1,0:T(8,128)(2,1)S(1)} copy(bf16[4096,256]{0,1:T(8,128)(2,1)} %bitcast.104) | data formatting | bytes 4194304 | tf_op jit(solution)/shard_map/dot_general | solution.py:147
  137.5 0.8 fusion.4
  138.3 13.2 %all_to_all.32 = bf16[16,64,256]{2,1,0:T(8,128)(2,1)S(1)} all-to-all(bf16[16,64,256]{2,1,0:T(8,128)(2,1)S(1)} %fusion.4), channel_id=1, replica_groups=mesh['row'=16,'col'=16] {'row'}, dimensions={0} | all-to-all | bytes 1048576 | tf_op jit(solution)/shard_map/all_to_all | solution.py:30
  151.5 0.7 reduce_sum.83
  (44 shorter events, 2.6 us)
Async XLA Ops:
  6.5 40.4 %copy-start = (bf16[256,384]{1,0:T(8,128)(2,1)S(1)}, bf16[256,384]{1,0:T(8,128)(2,1)}, u32[]{:S(2)}) copy-start(bf16[256,384]{1,0:T(8,128)(2,1)} %param.10) | copy-start | bytes 589828
  8.1 13.6 %all-to-all-start = ((f32[16,1,64]{2,1,0:T(1,128)}), f32[16,1,64]{2,1,0:T(1,128)S(1)}, u32[]{:S(2)}, u32[]{:S(2)}) async-start(f32[16,1,64]{2,1,0:T(1,128)} %broadcast_in_dim.94), calls=%async_computation | async-start | bytes 16384 | tf_op jit(solution)/shard_map/all_to_all | solution.py:37
  48.5 34.2 %copy-start.3 = (s32[1,64]{1,0:T(1,128)S(1)}, s32[1,64]{1,0:T(1,128)}, u32[]{:S(2)}) copy-start(s32[1,64]{1,0:T(1,128)} %param.15) | copy-start | bytes 772
  48.5 27.4 %all-to-all-start.2 = ((f32[16,64,384]{2,1,0:T(8,128)}), f32[16,64,384]{2,1,0:T(8,128)S(1)}, u32[]{:S(2)}, u32[]{:S(2)}) async-start(f32[16,64,384]{2,1,0:T(8,128)} %fusion.24), calls=%async_computation.2 | async-start | bytes 3145728 | tf_op jit(solution)/shard_map/all_to_all | solution.py:59
  53.6 80.7 %all-gather.2.cloned.1.call-start = ((), (), s32[]{:S(2)}) async-start(), calls=%async_computation.6 | async-start | bytes 2228224 | tf_op jit(solution)/shard_map/all_gather | solution.py:149
  54.3 46.0 %copy-start.1 = (bf16[1,256,1024]{2,1,0:T(8,128)(2,1)S(1)}, bf16[1,256,1024]{2,1,0:T(8,128)(2,1)}, u32[]{:S(2)}) copy-start(bf16[1,256,1024]{2,1,0:T(8,128)(2,1)} %param.12) | copy-start | bytes 1572868
  76.0 24.4 %copy-start.2 = (bf16[1,256,1024]{2,1,0:T(8,128)(2,1)S(1)}, bf16[1,256,1024]{2,1,0:T(8,128)(2,1)}, u32[]{:S(2)}) copy-start(bf16[1,256,1024]{2,1,0:T(8,128)(2,1)} %param.13) | copy-start | bytes 1572868
  76.0 9.1 %collective-permute-start = (bf16[64,384]{1,0:T(8,128)(2,1)S(1)}, bf16[64,384]{1,0:T(8,128)(2,1)S(1)}, u32[]{:S(2)}, u32[]{:S(2)}) collective-permute-start(bf16[64,384]{1,0:T(8,128)(2,1)S(1)} %reduce_sum.78), channel_id=1, source_target_pairs={{0,0},{1,16},{2,32},{3,48},{4,64},{5,80},{6,96},{7,112},{8,128},{9... | collective-permute-start | bytes 147464 | tf_op jit(solution)/shard_map/ppermute | solution.py:66
  86.2 25.0 %all-to-all-start.3 = ((bf16[16,64,384]{2,1,0:T(8,128)(2,1)}), bf16[16,64,384]{2,1,0:T(8,128)(2,1)S(1)}, u32[]{:S(2)}, u32[]{:S(2)}) async-start(bf16[16,64,384]{2,1,0:T(8,128)(2,1)} %broadcast_in_dim.96), calls=%async_computation.3 | async-start | bytes 1572864 | tf_op jit(solution)/shard_map/all_to_all | solution.py:37
  118.0 13.7 %all-to-all-start.4 = ((bf16[1,16,2,65,128]{4,2,3,0,1:T(2,128)(2,1)}), bf16[1,16,2,65,128]{4,2,3,0,1:T(2,128)(2,1)S(1)}, u32[]{:S(2)}, u32[]{:S(2)}) async-start(bf16[1,16,2,65,128]{4,2,3,0,1:T(2,128)(2,1)} %pad_maximum_fusion), calls=%async_computation.4 | async-start | bytes 1064960 | tf_op jit(solution)/shard_map/all_to_all | solution.py:111
Sparse Core Ops, SparseCore 0:
  56.2 42.2 all-gather.1

commit v5 on v4

--- a/solution.py
+++ b/solution.py
@@ -54,7 +54,8 @@
         jnp.bfloat16
     )
     col_count = lax.axis_size("col")
-    all_tokens = row_gather(normed, "col").reshape(col_count * rows_here, -1)
+    all_tokens = lax.all_gather(normed, "col", axis=0, tiled=True)
+    w_out, all_tokens = lax.optimization_barrier((w_out, all_tokens))
     partial_value = jnp.dot(all_tokens, w_qkv, preferred_element_type=jnp.float32)
     received = lax.all_to_all(
         partial_value.reshape(col_count, rows_here, -1), "row", 0, 0

time: 160 us -> 162 us (1.012)
  blocking collectives: 37.5 us -> 65.4 us
  waiting for transfers between devices: 48.5 us -> 32.9 us
  starting transfers between devices: 37.1 us -> 27.9 us
    all_to_all x1 -> x0, waiting for transfers between devices: 21.6 us -> none  [shards(): lax.all_to_all(partial_value.reshape(col_count, rows_here, -1), 'row', 0, 0)]
    all_gather x0 -> x1, blocking collectives: none -> 21.4 us  [shards(): all_tokens = lax.all_gather(normed, 'col', axis=0, tiled=True)]
    all_gather x1, waiting for transfers between devices: 0.02 us -> 5.86 us  [shards(): lax.all_gather(w_out, 'col', axis=1, tiled=True)]
    all_to_all x1 -> x0, starting transfers between devices: 5.09 us -> none  [shards(): lax.all_to_all(partial_value.reshape(col_count, rows_here, -1), 'row', 0, 0)]
    ppermute x1, starting transfers between devices: 6.68 us -> 2.05 us  [shards(): summed = lax.ppermute(summed, ('row', 'col'), transpose)]
    all_to_all x1, blocking collectives: 13.2 us -> 17.6 us  [row_reduce(): received = lax.all_to_all(pieces, axis_name, 0, 0)]
    all_to_all x1, blocking collectives: 24.3 us -> 26.4 us  [shards(): lax.all_to_all(partial_value.reshape(col_count, rows_here, -1), 'row', 0, 0)]
  transfers between devices with their start and end apart: 6 -> 5, of which waited for: 5 -> 5; matrix products, arithmetic and copies ran while one was open for 8% -> 7% of each run, Pallas kernels for 0% -> 0%
where the time goes in v5:
time: 162 us; the launch traced here: 161 us
  blocking collectives  65.4 us (40%)
  waiting for transfers between devices  32.9 us (20%)
  starting transfers between devices  27.9 us (17%)
  between operations  14.3 us (9%)
  local copies, waits for them, and re-layouts  7.86 us (5%)
  other arithmetic  7.71 us (5%)
  matrix products  4.7 us (3%)
    all_to_all x1, blocking collectives, shards(): lax.all_to_all(partial_value.reshape(col_count, rows_here, -1), 'row', 0, 0)  26.4 us
    all_gather x1, blocking collectives, shards(): all_tokens = lax.all_gather(normed, 'col', axis=0, tiled=True)  21.4 us
    all_to_all x2, starting transfers between devices, row_gather(): return lax.all_to_all(copies, axis_name, 0, 0)  21 us
    all_to_all x1, blocking collectives, row_reduce(): received = lax.all_to_all(pieces, axis_name, 0, 0)  17.6 us
    all_to_all x2, waiting for transfers between devices, row_gather(): return lax.all_to_all(copies, axis_name, 0, 0)  14.9 us
    all_to_all x1, waiting for transfers between devices, shards(): gathered = lax.all_to_all(packed, 'row', 1, 1).astype(jnp.float32)  8.36 us
    all_gather x1, waiting for transfers between devices, shards(): lax.all_gather(w_out, 'col', axis=1, tiled=True)  5.86 us
    all_to_all x1, starting transfers between devices, shards(): gathered = lax.all_to_all(packed, 'row', 1, 1).astype(jnp.float32)  4.83 us
  transfers between devices with their start and end apart: 5, of which 5 were waited for; matrix products, arithmetic and copies ran while one was open for 7% of the time, Pallas kernels for 0%

profile of v5, /device:TPU:2, one launch (start us, length us, event | category | flops | bytes accessed | tf_op | source)
XLA Modules:
  0.0 160.8 jit_solution(3334781279495029768)
XLA Ops:
  6.5 0.9 fusion.24
  7.4 0.6 broadcast_in_dim.88
  8.1 7.5 %all-to-all-start = ((f32[16,1,64]{2,1,0:T(1,128)}), f32[16,1,64]{2,1,0:T(1,128)S(1)}, u32[]{:S(2)}, u32[]{:S(2)}) async-start(f32[16,1,64]{2,1,0:T(1,128)} %broadcast_in_dim.88), calls=%async_computation | async-start | bytes 16384 | tf_op jit(solution)/shard_map/all_to_all | solution.py:37
  15.5 0.7 convert_element_type.135
  16.2 5.5 %all-to-all-done = f32[16,1,64]{2,1,0:T(1,128)S(1)} async-done(((f32[16,1,64]{2,1,0:T(1,128)}), f32[16,1,64]{2,1,0:T(1,128)S(1)}, u32[]{:S(2)}, u32[]{:S(2)}) %all-to-all-start) | async-done | bytes 4128 | tf_op jit(solution)/shard_map/all_to_all | solution.py:37
  21.7 0.8 fusion.26
  22.6 21.4 %all_gather.6 = bf16[1024,256]{1,0:T(8,128)(2,1)S(1)} all-gather(bf16[64,256]{1,0:T(8,128)(2,1)S(1)} %fusion.26), channel_id=1, replica_groups=mesh['row'=16,'col'=16] {'col'}, dimensions={0}, use_global_device_ids=true | all-gather | bytes 557056 | tf_op jit(solution)/shard_map/all_gather | solution.py:57
  44.0 0.4 fusion.49
  44.4 26.4 %all_to_all.26 = f32[16,64,384]{2,1,0:T(8,128)S(1)} all-to-all(f32[16,64,384]{2,1,0:T(8,128)S(1)} %bitcast.100), channel_id=1, replica_groups=mesh['row'=16,'col'=16] {'row'}, dimensions={0} | all-to-all | bytes 3145728 | tf_op jit(solution)/shard_map/all_to_all | solution.py:60
  70.9 2.1 %collective-permute-start = (bf16[64,384]{1,0:T(8,128)(2,1)S(1)}, bf16[64,384]{1,0:T(8,128)(2,1)S(1)}, u32[]{:S(2)}, u32[]{:S(2)}) collective-permute-start(bf16[64,384]{1,0:T(8,128)(2,1)S(1)} %reduce_sum.78), channel_id=1, source_target_pairs={{0,0},{1,16},{2,32},{3,48},{4,64},{5,80},{6,96},{7,112},{8,128},{9... | collective-permute-start | bytes 147464 | tf_op jit(solution)/shard_map/ppermute | solution.py:67
  73.1 3.3 %collective-permute-done = bf16[64,384]{1,0:T(8,128)(2,1)S(1)} collective-permute-done((bf16[64,384]{1,0:T(8,128)(2,1)S(1)}, bf16[64,384]{1,0:T(8,128)(2,1)S(1)}, u32[]{:S(2)}, u32[]{:S(2)}) %collective-permute-start) | collective-permute-done | bytes 49184 | tf_op jit(solution)/shard_map/ppermute | solution.py:67
  76.4 1.0 broadcast_in_dim.89
  77.4 13.5 %all-to-all-start.2 = ((bf16[16,64,384]{2,1,0:T(8,128)(2,1)}), bf16[16,64,384]{2,1,0:T(8,128)(2,1)S(1)}, u32[]{:S(2)}, u32[]{:S(2)}) async-start(bf16[16,64,384]{2,1,0:T(8,128)(2,1)} %broadcast_in_dim.89), calls=%async_computation.2 | async-start | bytes 1572864 | tf_op jit(solution)/shard_map/all_to_all | solution.py:37
  91.3 0.4 all-gather.2.cloned.1.call-update
  93.2 9.5 %all-to-all-done.2 = bf16[16,64,384]{2,1,0:T(8,128)(2,1)S(1)} async-done(((bf16[16,64,384]{2,1,0:T(8,128)(2,1)}), bf16[16,64,384]{2,1,0:T(8,128)(2,1)S(1)}, u32[]{:S(2)}, u32[]{:S(2)}) %all-to-all-start.2) | async-done | bytes 786464 | tf_op jit(solution)/shard_map/all_to_all | solution.py:37
  102.9 1.2 squeeze.24
  104.1 1.7 %bitcast_reduce_fusion = (bf16[8,4,64]{2,1,0:T(4,128)(2,1)S(1)}, f32[8,64,4,256]{3,1,2,0:T(8,128)S(1)}) fusion(pred[256]{0:T(512)(128)(4,1)S(1)} %add_compare_fusion, bf16[256,8,128,1]{2,1,0,3:T(8,128)(2,1)S(1)} %bitcast.111, bf16[64,8,4,128]{3,2,1,0:T(4,128)(2,1)} %squeeze.24), kind=kOutput, calls=%fused_computation.1 | convolution fusion | flops 135788544 | bytes 3150080 | tf_op jit(solution)/shard_map/while/body/eval_jaxpr/tkgd,pkd->kgtp/dot_general | solution.py:86
  105.8 0.7 convolution_convert_fusion
  106.4 0.5 copy.80
  107.0 0.9 fusion.2
  108.0 1.5 pad_maximum_fusion
  109.5 4.8 %all-to-all-start.3 = ((bf16[1,16,2,65,128]{4,2,3,0,1:T(2,128)(2,1)}), bf16[1,16,2,65,128]{4,2,3,0,1:T(2,128)(2,1)S(1)}, u32[]{:S(2)}, u32[]{:S(2)}) async-start(bf16[1,16,2,65,128]{4,2,3,0,1:T(2,128)(2,1)} %pad_maximum_fusion), calls=%async_computation.3 | async-start | bytes 1064960 | tf_op jit(solution)/shard_map/all_to_all | solution.py:112
  114.9 8.4 %all-to-all-done.3 = bf16[1,16,2,65,128]{4,2,3,0,1:T(2,128)(2,1)S(1)} async-done(((bf16[1,16,2,65,128]{4,2,3,0,1:T(2,128)(2,1)}), bf16[1,16,2,65,128]{4,2,3,0,1:T(2,128)(2,1)S(1)}, u32[]{:S(2)}, u32[]{:S(2)}) %all-to-all-start.3) | async-done | bytes 532512 | tf_op jit(solution)/shard_map/all_to_all | solution.py:112
  123.2 0.4 convert_element_type.142
  123.7 0.2 copy.86
  124.0 1.3 fusion.13
  125.4 0.2 fusion.9
  125.7 5.9 %all-gather.2.cloned.1.call-done = bf16[256,4096]{1,0:T(8,128)(2,1)} async-done(((bf16[256,256]{1,0:T(8,128)(2,1)}), bf16[256,4096]{1,0:T(8,128)(2,1)}) %all-gather.2.cloned.1.call-update) | async-done | bytes 2097168 | tf_op jit(solution)/shard_map/all_gather | solution.py:150
  131.6 3.3 %copy.91 = bf16[4096,256]{1,0:T(8,128)(2,1)S(1)} copy(bf16[4096,256]{0,1:T(8,128)(2,1)} %bitcast.104) | data formatting | bytes 4194304 | tf_op jit(solution)/shard_map/dot_general | solution.py:148
  134.9 0.8 fusion.4
  135.6 17.6 %all_to_all.27 = bf16[16,64,256]{2,1,0:T(8,128)(2,1)S(1)} all-to-all(bf16[16,64,256]{2,1,0:T(8,128)(2,1)S(1)} %fusion.4), channel_id=1, replica_groups=mesh['row'=16,'col'=16] {'row'}, dimensions={0} | all-to-all | bytes 1048576 | tf_op jit(solution)/shard_map/all_to_all | solution.py:30
  153.2 0.7 reduce_sum.83
  (42 shorter events, 2.6 us)
Async XLA Ops:
  6.5 37.4 %copy-start = (bf16[256,384]{1,0:T(8,128)(2,1)S(1)}, bf16[256,384]{1,0:T(8,128)(2,1)}, u32[]{:S(2)}) copy-start(bf16[256,384]{1,0:T(8,128)(2,1)} %param.10) | copy-start | bytes 589828
  8.1 13.6 %all-to-all-start = ((f32[16,1,64]{2,1,0:T(1,128)}), f32[16,1,64]{2,1,0:T(1,128)S(1)}, u32[]{:S(2)}, u32[]{:S(2)}) async-start(f32[16,1,64]{2,1,0:T(1,128)} %broadcast_in_dim.88), calls=%async_computation | async-start | bytes 16384 | tf_op jit(solution)/shard_map/all_to_all | solution.py:37
  44.4 28.5 %copy-start.3 = (s32[1,64]{1,0:T(1,128)S(1)}, s32[1,64]{1,0:T(1,128)}, u32[]{:S(2)}) copy-start(s32[1,64]{1,0:T(1,128)} %param.15) | copy-start | bytes 772
  70.8 21.7 %copy-start.1 = (bf16[1,256,1024]{2,1,0:T(8,128)(2,1)S(1)}, bf16[1,256,1024]{2,1,0:T(8,128)(2,1)}, u32[]{:S(2)}) copy-start(bf16[1,256,1024]{2,1,0:T(8,128)(2,1)} %param.12) | copy-start | bytes 1572868
  70.9 21.7 %copy-start.2 = (bf16[1,256,1024]{2,1,0:T(8,128)(2,1)S(1)}, bf16[1,256,1024]{2,1,0:T(8,128)(2,1)}, u32[]{:S(2)}) copy-start(bf16[1,256,1024]{2,1,0:T(8,128)(2,1)} %param.13) | copy-start | bytes 1572868
  70.9 5.5 %collective-permute-start = (bf16[64,384]{1,0:T(8,128)(2,1)S(1)}, bf16[64,384]{1,0:T(8,128)(2,1)S(1)}, u32[]{:S(2)}, u32[]{:S(2)}) collective-permute-start(bf16[64,384]{1,0:T(8,128)(2,1)S(1)} %reduce_sum.78), channel_id=1, source_target_pairs={{0,0},{1,16},{2,32},{3,48},{4,64},{5,80},{6,96},{7,112},{8,128},{9... | collective-permute-start | bytes 147464 | tf_op jit(solution)/shard_map/ppermute | solution.py:67
  77.4 25.3 %all-to-all-start.2 = ((bf16[16,64,384]{2,1,0:T(8,128)(2,1)}), bf16[16,64,384]{2,1,0:T(8,128)(2,1)S(1)}, u32[]{:S(2)}, u32[]{:S(2)}) async-start(bf16[16,64,384]{2,1,0:T(8,128)(2,1)} %broadcast_in_dim.89), calls=%async_computation.2 | async-start | bytes 1572864 | tf_op jit(solution)/shard_map/all_to_all | solution.py:37
  90.9 40.7 %all-gather.2.cloned.1.call-start = ((), (), s32[]{:S(2)}) async-start(), calls=%async_computation.5 | async-start | bytes 2228224 | tf_op jit(solution)/shard_map/all_gather | solution.py:150
  109.5 13.7 %all-to-all-start.3 = ((bf16[1,16,2,65,128]{4,2,3,0,1:T(2,128)(2,1)}), bf16[1,16,2,65,128]{4,2,3,0,1:T(2,128)(2,1)S(1)}, u32[]{:S(2)}, u32[]{:S(2)}) async-start(bf16[1,16,2,65,128]{4,2,3,0,1:T(2,128)(2,1)} %pad_maximum_fusion), calls=%async_computation.3 | async-start | bytes 1064960 | tf_op jit(solution)/shard_map/all_to_all | solution.py:112
Sparse Core Ops, SparseCore 0:
  93.5 38.0 all-gather.1

commit v6 on v3

--- a/solution.py
+++ b/solution.py
@@ -82,7 +82,7 @@
         )
         visible = (slot_ids < length)[None, None, None, :]
         scores = jnp.where(visible, scores, masked_score)
-        highest = jnp.max(scores, axis=-1).astype(jnp.bfloat16).astype(jnp.float32)
+        highest = jnp.max(scores, axis=-1)
         weights = jnp.where(visible, jnp.exp(scores - highest[..., None]), 0.0)
         totals = jnp.sum(weights, axis=-1)
         blended = jnp.einsum(
@@ -91,19 +91,29 @@
             value_row_block,
             preferred_element_type=jnp.float32,
         )
-        stats = jnp.concatenate(
-            [highest.reshape(QUERY_HEADS, draft_tree), totals.reshape(QUERY_HEADS, draft_tree)],
-            axis=-1,
+        highest = highest.reshape(QUERY_HEADS, draft_tree)
+        max_hi = highest.astype(jnp.bfloat16)
+        rest = highest - max_hi.astype(jnp.float32)
+        max_mid = rest.astype(jnp.bfloat16)
+        max_lo = (rest - max_mid.astype(jnp.float32)).astype(jnp.bfloat16)
+        stats = jnp.stack(
+            [
+                jnp.concatenate([max_hi, totals.reshape(QUERY_HEADS, draft_tree).astype(jnp.bfloat16)], axis=-1),
+                jnp.concatenate([max_mid, max_lo], axis=-1),
+            ],
+            axis=1,
         )
         return jnp.concatenate(
-            [blended.reshape(QUERY_HEADS, draft_tree, HEAD_SIZE), stats[:, None, :]], axis=1
-        ).astype(jnp.bfloat16)
+            [blended.reshape(QUERY_HEADS, draft_tree, HEAD_SIZE).astype(jnp.bfloat16), stats], axis=1
+        )
 
     packed = lax.map(cache_part, (query_block, cache_k, value_cache, cache_len))
-    packed = packed.reshape(request_list, row_count, heads_dev, draft_tree + 1, HEAD_SIZE)
+    packed = packed.reshape(request_list, row_count, heads_dev, draft_tree + 2, HEAD_SIZE)
     gathered = lax.all_to_all(packed, "row", 1, 1).astype(jnp.float32)
     block_blend = gathered[:, :, :, :draft_tree, :]
-    block_max = gathered[:, :, :, draft_tree, :draft_tree]
+    block_max = (
+        gathered[:, :, :, draft_tree, :draft_tree] + gathered[:, :, :, draft_tree + 1, :draft_tree]
+    ) + gathered[:, :, :, draft_tree + 1, draft_tree : 2 * draft_tree]
     block_total = gathered[:, :, :, draft_tree, draft_tree : 2 * draft_tree]
     allowed = ancestors(parents)[:, None, :, :]
     query_heads = projected_output[:, : QUERY_HEADS * HEAD_SIZE].reshape(

time: 156 us -> 155 us (level)
  other arithmetic: 8.84 us -> 6.84 us
    unnamed x17 -> x15, local copies, waits for them, and re-layouts: 2.1 us -> 3.98 us
    reduce_sum x1, other arithmetic: 2.23 us -> 0.37 us  [shards(): jnp.sum(block_blend * block_scale[..., None], axis=1)]
where the time goes in v6:
time: 155 us; the launch traced here: 154 us
  waiting for transfers between devices  73.1 us (47%)
  starting transfers between devices  27.3 us (18%)
  between operations  14.3 us (9%)
  blocking collectives  13.1 us (8%)
  local copies, waits for them, and re-layouts  12.5 us (8%)
  matrix products  7.05 us (5%)
  other arithmetic  6.84 us (4%)
    all_gather x1, waiting for transfers between devices, shards(): lax.all_gather(w_qkv, 'col', axis=1, tiled=True)  29.9 us
    all_to_all x1, waiting for transfers between devices, row_reduce(): received = lax.all_to_all(pieces, axis_name, 0, 0)  21.7 us
    all_to_all x2, starting transfers between devices, row_gather(): return lax.all_to_all(copies, axis_name, 0, 0)  14.4 us
    all_to_all x1, blocking collectives, row_reduce(): received = lax.all_to_all(pieces, axis_name, 0, 0)  13.1 us
    all_to_all x2, waiting for transfers between devices, row_gather(): return lax.all_to_all(copies, axis_name, 0, 0)  11.5 us
    all_to_all x1, waiting for transfers between devices, shards(): gathered = lax.all_to_all(packed, 'row', 1, 1).astype(jnp.float32)  8.64 us
    all_to_all x1, starting transfers between devices, row_reduce(): received = lax.all_to_all(pieces, axis_name, 0, 0)  7.4 us
    all_to_all x1, starting transfers between devices, shards(): gathered = lax.all_to_all(packed, 'row', 1, 1).astype(jnp.float32)  5.48 us
  transfers between devices with their start and end apart: 6, of which 5 were waited for; matrix products, arithmetic and copies ran while one was open for 9% of the time, Pallas kernels for 0%

profile of v6, /device:TPU:2, one launch (start us, length us, event | category | flops | bytes accessed | tf_op | source)
XLA Modules:
  0.0 154.3 jit_solution(13833110814464951637)
XLA Ops:
  6.5 0.7 all-gather.3.cloned.1.call-update
  7.3 0.7 all-gather.5.cloned.1.call-update
  8.0 0.9 fusion.24
  8.9 0.6 broadcast_in_dim.86
  9.5 7.5 %all-to-all-start = ((f32[16,1,64]{2,1,0:T(1,128)}), f32[16,1,64]{2,1,0:T(1,128)S(1)}, u32[]{:S(2)}, u32[]{:S(2)}) async-start(f32[16,1,64]{2,1,0:T(1,128)} %broadcast_in_dim.86), calls=%async_computation | async-start | bytes 16384 | tf_op jit(solution)/shard_map/all_to_all | solution.py:37
  17.0 0.7 convert_element_type.181
  17.6 5.5 %all-to-all-done = f32[16,1,64]{2,1,0:T(1,128)S(1)} async-done(((f32[16,1,64]{2,1,0:T(1,128)}), f32[16,1,64]{2,1,0:T(1,128)S(1)}, u32[]{:S(2)}, u32[]{:S(2)}) %all-to-all-start) | async-done | bytes 4128 | tf_op jit(solution)/shard_map/all_to_all | solution.py:37
  23.1 29.9 %all-gather.3.cloned.1.call-done = bf16[256,6144]{1,0:T(8,128)(2,1)} async-done(((bf16[256,384]{1,0:T(8,128)(2,1)}), bf16[256,6144]{1,0:T(8,128)(2,1)}) %all-gather.3.cloned.1.call-update) | async-done | bytes 3145744 | tf_op jit(solution)/shard_map/all_gather | solution.py:57
  53.0 2.6 %fusion.30 = f32[64,6144]{1,0:T(8,128)S(1)} fusion(bf16[256,6144]{1,0:T(8,128)(2,1)} %all-gather.3.cloned.1.call-done, bf16[64,256]{1,0:T(8,128)(2,1)} %param.8, f32[256]{0:T(256)S(1)} %convert_element_type.181, f32[64]{0:T(128)S(1)} %add_rsqrt_fusion), kind=kOutput, calls=%fused_computation.54 | convolution fusion | flops 201392128 | bytes 4752640 | tf_op jit(solution)/shard_map/dot_general | solution.py:56
  55.6 1.3 copy.175
  56.9 7.4 %all-to-all-start.1 = ((f32[16,64,384]{2,1,0:T(8,128)}), f32[16,64,384]{2,1,0:T(8,128)S(1)}, u32[]{:S(2)}, u32[]{:S(2)}) async-start(f32[16,64,384]{2,1,0:T(8,128)} %bitcast.117), calls=%async_computation.1 | async-start | bytes 3145728 | tf_op jit(solution)/shard_map/all_to_all | solution.py:30
  64.5 21.7 %all-to-all-done.1 = f32[16,64,384]{2,1,0:T(8,128)S(1)} async-done(((f32[16,64,384]{2,1,0:T(8,128)}), f32[16,64,384]{2,1,0:T(8,128)S(1)}, u32[]{:S(2)}, u32[]{:S(2)}) %all-to-all-start.1) | async-done | bytes 1572896 | tf_op jit(solution)/shard_map/all_to_all | solution.py:30
  86.3 1.0 broadcast_in_dim.87
  87.3 6.9 %all-to-all-start.2 = ((bf16[16,64,384]{2,1,0:T(8,128)(2,1)}), bf16[16,64,384]{2,1,0:T(8,128)(2,1)S(1)}, u32[]{:S(2)}, u32[]{:S(2)}) async-start(bf16[16,64,384]{2,1,0:T(8,128)(2,1)} %broadcast_in_dim.87), calls=%async_computation.2 | async-start | bytes 1572864 | tf_op jit(solution)/shard_map/all_to_all | solution.py:37
  95.1 0.9 copy.152
  96.0 0.9 copy.153
  97.7 3.3 %copy.136 = bf16[4096,256]{1,0:T(8,128)(2,1)S(1)} copy(bf16[4096,256]{0,1:T(8,128)(2,1)} %bitcast.124) | data formatting | bytes 4194304 | tf_op jit(solution)/shard_map/dot_general | solution.py:150
  101.0 6.0 %all-to-all-done.2 = bf16[16,64,384]{2,1,0:T(8,128)(2,1)S(1)} async-done(((bf16[16,64,384]{2,1,0:T(8,128)(2,1)}), bf16[16,64,384]{2,1,0:T(8,128)(2,1)S(1)}, u32[]{:S(2)}, u32[]{:S(2)}) %all-to-all-start.2) | async-done | bytes 786464 | tf_op jit(solution)/shard_map/all_to_all | solution.py:37
  107.1 0.9 copy-done
  108.1 1.2 squeeze.22
  109.3 1.8 %bitcast_reduce_fusion = (f32[8,4,64]{2,1,0:T(4,128)S(1)}, f32[8,64,4,256]{3,1,2,0:T(8,128)S(1)}) fusion(pred[256]{0:T(512)(128)(4,1)S(1)} %add_compare_fusion, bf16[256,8,128,1]{2,1,0,3:T(8,128)(2,1)} %bitcast.131, bf16[64,8,4,128]{3,2,1,0:T(4,128)(2,1)} %squeeze.22), kind=kOutput, calls=%fused_computation.1 | convolution fusion | flops 135788544 | bytes 3154176 | tf_op jit(solution)/shard_map/while/body/eval_jaxpr/tkgd,pkd->kgtp/dot_general | solution.py:78
  111.2 1.0 slice_bitcast_fusion
  112.2 0.9 fusion.2
  113.1 0.7 convolution_convert_fusion
  113.8 0.5 copy.120
  114.5 1.6 %pad_maximum_fusion = bf16[1,16,2,66,128]{4,2,3,0,1:T(2,128)(2,1)} fusion(bf16[1,16,2,1,128]{4,2,3,0,1:T(2,128)(2,1)S(1)} %get-tuple-element.41, bf16[1,16,2,1,128]{4,2,3,0,1:T(2,128)(2,1)S(1)} %get-tuple-element.40, bf16[1,16,2,64,128]{4,2,3,0,1:T(2,128)(2,1)S(1)} %copy.120), kind=kLoop, calls=%fused_computation.34 | loop fusion | flops 540672 | bytes 1081344 | tf_op jit(solution)/shard_map/while/body/eval_jaxpr/concatenate | solution.py:106
  116.1 5.5 %all-to-all-start.3 = ((bf16[1,16,2,66,128]{4,2,3,0,1:T(2,128)(2,1)}), bf16[1,16,2,66,128]{4,2,3,0,1:T(2,128)(2,1)}, u32[]{:S(2)}, u32[]{:S(2)}) async-start(bf16[1,16,2,66,128]{4,2,3,0,1:T(2,128)(2,1)} %pad_maximum_fusion), calls=%async_computation.3 | async-start | bytes 1081344 | tf_op jit(solution)/shard_map/all_to_all | solution.py:112
  122.1 8.6 %all-to-all-done.3 = bf16[1,16,2,66,128]{4,2,3,0,1:T(2,128)(2,1)} async-done(((bf16[1,16,2,66,128]{4,2,3,0,1:T(2,128)(2,1)}), bf16[1,16,2,66,128]{4,2,3,0,1:T(2,128)(2,1)}, u32[]{:S(2)}, u32[]{:S(2)}) %all-to-all-start.3) | async-done | bytes 540704 | tf_op jit(solution)/shard_map/all_to_all | solution.py:112
  130.7 1.1 copy_convert_fusion
  132.9 0.8 fusion.4
  133.7 13.1 %all_to_all.26 = bf16[16,64,256]{2,1,0:T(8,128)(2,1)S(1)} all-to-all(bf16[16,64,256]{2,1,0:T(8,128)(2,1)S(1)} %fusion.4), channel_id=1, replica_groups=mesh['row'=16,'col'=16] {'row'}, dimensions={0} | all-to-all | bytes 1048576 | tf_op jit(solution)/shard_map/all_to_all | solution.py:30
  146.7 0.7 reduce_sum.83
  (46 shorter events, 3.1 us)
Async XLA Ops:
  6.5 46.5 %all-gather.3.cloned.1.call-start = ((), (), s32[]{:S(2)}) async-start(), calls=%async_computation.5 | async-start | bytes 3342336 | tf_op jit(solution)/shard_map/all_gather | solution.py:57
  7.3 90.5 %all-gather.5.cloned.1.call-start = ((), (), s32[]{:S(2)}) async-start(), calls=%async_computation.6 | async-start | bytes 2228224 | tf_op jit(solution)/shard_map/all_gather | solution.py:152
  9.5 13.6 %all-to-all-start = ((f32[16,1,64]{2,1,0:T(1,128)}), f32[16,1,64]{2,1,0:T(1,128)S(1)}, u32[]{:S(2)}, u32[]{:S(2)}) async-start(f32[16,1,64]{2,1,0:T(1,128)} %broadcast_in_dim.86), calls=%async_computation | async-start | bytes 16384 | tf_op jit(solution)/shard_map/all_to_all | solution.py:37
  56.9 7.4 %copy-start.4 = (s32[1,64]{1,0:T(1,128)S(1)}, s32[1,64]{1,0:T(1,128)}, u32[]{:S(2)}) copy-start(s32[1,64]{1,0:T(1,128)} %param.15) | copy-start | bytes 772
  56.9 29.3 %all-to-all-start.1 = ((f32[16,64,384]{2,1,0:T(8,128)}), f32[16,64,384]{2,1,0:T(8,128)S(1)}, u32[]{:S(2)}, u32[]{:S(2)}) async-start(f32[16,64,384]{2,1,0:T(8,128)} %bitcast.117), calls=%async_computation.1 | async-start | bytes 3145728 | tf_op jit(solution)/shard_map/all_to_all | solution.py:30
  64.3 30.7 %copy-start.1 = (bf16[1,256,1024]{2,1,0:T(8,128)(2,1)S(1)}, bf16[1,256,1024]{2,1,0:T(8,128)(2,1)}, u32[]{:S(2)}) copy-start(bf16[1,256,1024]{2,1,0:T(8,128)(2,1)} %param.12) | copy-start | bytes 1572868
  86.3 9.7 %copy-start.2 = (bf16[1,256,1024]{2,1,0:T(8,128)(2,1)S(1)}, bf16[1,256,1024]{2,1,0:T(8,128)(2,1)}, u32[]{:S(2)}) copy-start(bf16[1,256,1024]{2,1,0:T(8,128)(2,1)} %param.13) | copy-start | bytes 1572868
  87.3 19.7 %all-to-all-start.2 = ((bf16[16,64,384]{2,1,0:T(8,128)(2,1)}), bf16[16,64,384]{2,1,0:T(8,128)(2,1)S(1)}, u32[]{:S(2)}, u32[]{:S(2)}) async-start(bf16[16,64,384]{2,1,0:T(8,128)(2,1)} %broadcast_in_dim.87), calls=%async_computation.2 | async-start | bytes 1572864 | tf_op jit(solution)/shard_map/all_to_all | solution.py:37
  107.1 0.9 copy-start
  111.1 2.0 %copy-start.3 = (bf16[32,8,8,128]{3,2,1,0:T(8,128)(2,1)S(1)}, bf16[32,8,8,128]{3,2,1,0:T(8,128)(2,1)}, u32[]{:S(2)}) copy-start(bf16[32,8,8,128]{3,2,1,0:T(8,128)(2,1)} %copy.153) | copy-start | bytes 1572868
  116.1 14.7 %all-to-all-start.3 = ((bf16[1,16,2,66,128]{4,2,3,0,1:T(2,128)(2,1)}), bf16[1,16,2,66,128]{4,2,3,0,1:T(2,128)(2,1)}, u32[]{:S(2)}, u32[]{:S(2)}) async-start(bf16[1,16,2,66,128]{4,2,3,0,1:T(2,128)(2,1)} %pad_maximum_fusion), calls=%async_computation.3 | async-start | bytes 1081344 | tf_op jit(solution)/shard_map/all_to_all | solution.py:112
Sparse Core Ops, SparseCore 0:
  9.1 43.8 all-gather.2
  54.7 38.8 all-gather.4

commit v7 on v3

--- a/solution.py
+++ b/solution.py
@@ -82,7 +82,7 @@
         )
         visible = (slot_ids < length)[None, None, None, :]
         scores = jnp.where(visible, scores, masked_score)
-        highest = jnp.max(scores, axis=-1).astype(jnp.bfloat16).astype(jnp.float32)
+        highest = jnp.max(scores, axis=-1)
         weights = jnp.where(visible, jnp.exp(scores - highest[..., None]), 0.0)
         totals = jnp.sum(weights, axis=-1)
         blended = jnp.einsum(
@@ -97,11 +97,11 @@
         )
         return jnp.concatenate(
             [blended.reshape(QUERY_HEADS, draft_tree, HEAD_SIZE), stats[:, None, :]], axis=1
-        ).astype(jnp.bfloat16)
+        )
 
     packed = lax.map(cache_part, (query_block, cache_k, value_cache, cache_len))
     packed = packed.reshape(request_list, row_count, heads_dev, draft_tree + 1, HEAD_SIZE)
-    gathered = lax.all_to_all(packed, "row", 1, 1).astype(jnp.float32)
+    gathered = lax.all_to_all(packed, "row", 1, 1)
     block_blend = gathered[:, :, :, :draft_tree, :]
     block_max = gathered[:, :, :, draft_tree, :draft_tree]
     block_total = gathered[:, :, :, draft_tree, draft_tree : 2 * draft_tree]

time: 156 us -> 162 us (1.038)
  waiting for transfers between devices: 73 us -> 78.7 us
    all_to_all x2, waiting for transfers between devices: 11.5 us -> 16.8 us  [row_gather(): return lax.all_to_all(copies, axis_name, 0, 0)]
    unnamed x17 -> x13, local copies, waits for them, and re-layouts: 2.1 us -> 4.21 us
  transfers between devices with their start and end apart: 6 -> 6, of which waited for: 5 -> 5; matrix products, arithmetic and copies ran while one was open for 9% -> 13% of each run, Pallas kernels for 0% -> 0%
where the time goes in v7:
time: 162 us; the launch traced here: 161 us
  waiting for transfers between devices  78.7 us (49%)
  starting transfers between devices  26.9 us (17%)
  blocking collectives  14.3 us (9%)
  between operations  14.3 us (9%)
  local copies, waits for them, and re-layouts  13.2 us (8%)
  other arithmetic  7.34 us (5%)
  matrix products  5.84 us (4%)
    all_gather x1, waiting for transfers between devices, shards(): lax.all_gather(w_qkv, 'col', axis=1, tiled=True)  30.6 us
    all_to_all x1, waiting for transfers between devices, row_reduce(): received = lax.all_to_all(pieces, axis_name, 0, 0)  20.9 us
    all_to_all x2, waiting for transfers between devices, row_gather(): return lax.all_to_all(copies, axis_name, 0, 0)  16.8 us
    all_to_all x2, starting transfers between devices, row_gather(): return lax.all_to_all(copies, axis_name, 0, 0)  14.4 us
    all_to_all x1, blocking collectives, row_reduce(): received = lax.all_to_all(pieces, axis_name, 0, 0)  14.3 us
    all_to_all x1, waiting for transfers between devices, shards(): gathered = lax.all_to_all(packed, 'row', 1, 1)  9.09 us
    all_to_all x1, starting transfers between devices, row_reduce(): received = lax.all_to_all(pieces, axis_name, 0, 0)  7.4 us
    all_to_all x1, starting transfers between devices, shards(): gathered = lax.all_to_all(packed, 'row', 1, 1)  5.03 us
  transfers between devices with their start and end apart: 6, of which 5 were waited for; matrix products, arithmetic and copies ran while one was open for 13% of the time, Pallas kernels for 0%

profile of v7, /device:TPU:2, one launch (start us, length us, event | category | flops | bytes accessed | tf_op | source)
XLA Modules:
  0.0 160.5 jit_solution(2738622934716406521)
XLA Ops:
  6.5 0.7 all-gather.3.cloned.1.call-update
  7.3 0.9 fusion.25
  8.1 0.6 broadcast_in_dim.88
  8.7 7.5 %all-to-all-start = ((f32[16,1,64]{2,1,0:T(1,128)}), f32[16,1,64]{2,1,0:T(1,128)S(1)}, u32[]{:S(2)}, u32[]{:S(2)}) async-start(f32[16,1,64]{2,1,0:T(1,128)} %broadcast_in_dim.88), calls=%async_computation | async-start | bytes 16384 | tf_op jit(solution)/shard_map/all_to_all | solution.py:37
  16.3 0.7 all-gather.5.cloned.1.call-update
  17.0 0.7 convert_element_type.95
  17.6 4.7 %all-to-all-done = f32[16,1,64]{2,1,0:T(1,128)S(1)} async-done(((f32[16,1,64]{2,1,0:T(1,128)}), f32[16,1,64]{2,1,0:T(1,128)S(1)}, u32[]{:S(2)}, u32[]{:S(2)}) %all-to-all-start) | async-done | bytes 4128 | tf_op jit(solution)/shard_map/all_to_all | solution.py:37
  22.4 30.6 %all-gather.3.cloned.1.call-done = bf16[256,6144]{1,0:T(8,128)(2,1)} async-done(((bf16[256,384]{1,0:T(8,128)(2,1)}), bf16[256,6144]{1,0:T(8,128)(2,1)}) %all-gather.3.cloned.1.call-update) | async-done | bytes 3145744 | tf_op jit(solution)/shard_map/all_gather | solution.py:57
  53.0 2.6 %fusion.31 = f32[64,6144]{1,0:T(8,128)S(1)} fusion(bf16[256,6144]{1,0:T(8,128)(2,1)} %all-gather.3.cloned.1.call-done, bf16[64,256]{1,0:T(8,128)(2,1)} %param.8, f32[256]{0:T(256)S(1)} %convert_element_type.95, f32[64]{0:T(128)S(1)} %add_rsqrt_fusion), kind=kOutput, calls=%fused_computation.53 | convolution fusion | flops 201392128 | bytes 4752640 | tf_op jit(solution)/shard_map/dot_general | solution.py:56
  55.6 1.3 copy.127
  56.9 7.4 %all-to-all-start.1 = ((f32[16,64,384]{2,1,0:T(8,128)}), f32[16,64,384]{2,1,0:T(8,128)S(1)}, u32[]{:S(2)}, u32[]{:S(2)}) async-start(f32[16,64,384]{2,1,0:T(8,128)} %bitcast.100), calls=%async_computation.1 | async-start | bytes 3145728 | tf_op jit(solution)/shard_map/all_to_all | solution.py:30
  65.4 20.9 %all-to-all-done.1 = f32[16,64,384]{2,1,0:T(8,128)S(1)} async-done(((f32[16,64,384]{2,1,0:T(8,128)}), f32[16,64,384]{2,1,0:T(8,128)S(1)}, u32[]{:S(2)}, u32[]{:S(2)}) %all-to-all-start.1) | async-done | bytes 1572896 | tf_op jit(solution)/shard_map/all_to_all | solution.py:30
  86.3 1.0 broadcast_in_dim.89
  87.3 6.9 %all-to-all-start.2 = ((bf16[16,64,384]{2,1,0:T(8,128)(2,1)}), bf16[16,64,384]{2,1,0:T(8,128)(2,1)S(1)}, u32[]{:S(2)}, u32[]{:S(2)}) async-start(bf16[16,64,384]{2,1,0:T(8,128)(2,1)} %broadcast_in_dim.89), calls=%async_computation.2 | async-start | bytes 1572864 | tf_op jit(solution)/shard_map/all_to_all | solution.py:37
  94.9 12.0 %all-to-all-done.2 = bf16[16,64,384]{2,1,0:T(8,128)(2,1)S(1)} async-done(((bf16[16,64,384]{2,1,0:T(8,128)(2,1)}), bf16[16,64,384]{2,1,0:T(8,128)(2,1)S(1)}, u32[]{:S(2)}, u32[]{:S(2)}) %all-to-all-start.2) | async-done | bytes 786464 | tf_op jit(solution)/shard_map/all_to_all | solution.py:37
  107.1 0.9 copy-done
  108.0 1.0 slice_bitcast_fusion.3
  109.3 0.6 bitcast_reduce_fusion
  110.0 0.7 fusion.12
  110.6 0.8 copy.81
  111.4 0.9 fusion.2
  112.4 1.5 maximum_maximum_fusion
  113.9 5.0 %all-to-all-start.3 = ((f32[1,16,2,65,128]{4,2,3,0,1:T(2,128)}), f32[1,16,2,65,128]{4,2,3,0,1:T(2,128)S(1)}, u32[]{:S(2)}, u32[]{:S(2)}) async-start(f32[1,16,2,65,128]{4,2,3,0,1:T(2,128)} %maximum_maximum_fusion), calls=%async_computation.3 | async-start | bytes 2129920 | tf_op jit(solution)/shard_map/all_to_all | solution.py:104
  119.2 3.3 %copy.91 = bf16[4096,256]{1,0:T(8,128)(2,1)S(1)} copy(bf16[4096,256]{0,1:T(8,128)(2,1)} %bitcast.107) | data formatting | bytes 4194304 | tf_op jit(solution)/shard_map/dot_general | solution.py:140
  122.4 1.1 copy.106
  123.6 1.0 slice_bitcast_fusion
  125.0 9.1 %all-to-all-done.3 = f32[1,16,2,65,128]{4,2,3,0,1:T(2,128)S(1)} async-done(((f32[1,16,2,65,128]{4,2,3,0,1:T(2,128)}), f32[1,16,2,65,128]{4,2,3,0,1:T(2,128)S(1)}, u32[]{:S(2)}, u32[]{:S(2)}) %all-to-all-start.3) | async-done | bytes 1064992 | tf_op jit(solution)/shard_map/all_to_all | solution.py:104
  134.2 1.0 copy.86
  135.3 2.2 %fusion.14 = f32[2,64,128]{2,0,1:T(2,128)S(1)} fusion(f32[1,16,2,65,128]{4,2,3,0,1:T(2,128)S(1)} %all-to-all-done.3, f32[16,2,64]{1,2,0:T(8,128)} %copy.86), kind=kLoop, calls=%fused_computation.28 | loop fusion | flops 507904 | bytes 1122304 | tf_op jit(solution)/shard_map/reduce_sum | solution.py:136
  138.0 0.8 fusion.4
  138.7 14.3 %all_to_all.26 = bf16[16,64,256]{2,1,0:T(8,128)(2,1)S(1)} all-to-all(bf16[16,64,256]{2,1,0:T(8,128)(2,1)S(1)} %fusion.4), channel_id=1, replica_groups=mesh['row'=16,'col'=16] {'row'}, dimensions={0} | all-to-all | bytes 1048576 | tf_op jit(solution)/shard_map/all_to_all | solution.py:30
  153.0 0.7 reduce_sum.83
  (40 shorter events, 2.8 us)
Async XLA Ops:
  6.5 46.5 %all-gather.3.cloned.1.call-start = ((), (), s32[]{:S(2)}) async-start(), calls=%async_computation.5 | async-start | bytes 3342336 | tf_op jit(solution)/shard_map/all_gather | solution.py:57
  8.7 13.6 %all-to-all-start = ((f32[16,1,64]{2,1,0:T(1,128)}), f32[16,1,64]{2,1,0:T(1,128)S(1)}, u32[]{:S(2)}, u32[]{:S(2)}) async-start(f32[16,1,64]{2,1,0:T(1,128)} %broadcast_in_dim.88), calls=%async_computation | async-start | bytes 16384 | tf_op jit(solution)/shard_map/all_to_all | solution.py:37
  16.2 102.9 %all-gather.5.cloned.1.call-start = ((), (), s32[]{:S(2)}) async-start(), calls=%async_computation.6 | async-start | bytes 2228224 | tf_op jit(solution)/shard_map/all_gather | solution.py:142
  56.9 8.1 %copy-start.1 = (bf16[1,256,1024]{2,1,0:T(8,128)(2,1)S(1)}, bf16[1,256,1024]{2,1,0:T(8,128)(2,1)}, u32[]{:S(2)}) copy-start(bf16[1,256,1024]{2,1,0:T(8,128)(2,1)} %param.12) | copy-start | bytes 1572868
  56.9 8.2 %copy-start.2 = (bf16[1,256,1024]{2,1,0:T(8,128)(2,1)S(1)}, bf16[1,256,1024]{2,1,0:T(8,128)(2,1)}, u32[]{:S(2)}) copy-start(bf16[1,256,1024]{2,1,0:T(8,128)(2,1)} %param.13) | copy-start | bytes 1572868
  56.9 8.3 %copy-start.3 = (s32[1,64]{1,0:T(1,128)S(1)}, s32[1,64]{1,0:T(1,128)}, u32[]{:S(2)}) copy-start(s32[1,64]{1,0:T(1,128)} %param.15) | copy-start | bytes 772
  56.9 29.3 %all-to-all-start.1 = ((f32[16,64,384]{2,1,0:T(8,128)}), f32[16,64,384]{2,1,0:T(8,128)S(1)}, u32[]{:S(2)}, u32[]{:S(2)}) async-start(f32[16,64,384]{2,1,0:T(8,128)} %bitcast.100), calls=%async_computation.1 | async-start | bytes 3145728 | tf_op jit(solution)/shard_map/all_to_all | solution.py:30
  87.3 19.7 %all-to-all-start.2 = ((bf16[16,64,384]{2,1,0:T(8,128)(2,1)}), bf16[16,64,384]{2,1,0:T(8,128)(2,1)S(1)}, u32[]{:S(2)}, u32[]{:S(2)}) async-start(bf16[16,64,384]{2,1,0:T(8,128)(2,1)} %broadcast_in_dim.89), calls=%async_computation.2 | async-start | bytes 1572864 | tf_op jit(solution)/shard_map/all_to_all | solution.py:37
  107.1 0.9 copy-start
  113.9 20.2 %all-to-all-start.3 = ((f32[1,16,2,65,128]{4,2,3,0,1:T(2,128)}), f32[1,16,2,65,128]{4,2,3,0,1:T(2,128)S(1)}, u32[]{:S(2)}, u32[]{:S(2)}) async-start(f32[1,16,2,65,128]{4,2,3,0,1:T(2,128)} %maximum_maximum_fusion), calls=%async_computation.3 | async-start | bytes 2129920 | tf_op jit(solution)/shard_map/all_to_all | solution.py:104
Sparse Core Ops, SparseCore 0:
  9.1 43.8 all-gather.2
  54.7 38.8 all-gather.4

commit v8 on v7

--- a/solution.py
+++ b/solution.py
@@ -53,10 +53,14 @@
     normed = (features * row_scale[:, None] * norm_gain.astype(jnp.float32)[None, :]).astype(
         jnp.bfloat16
     )
-    partial_value = jnp.dot(
-        normed, lax.all_gather(w_qkv, "col", axis=1, tiled=True), preferred_element_type=jnp.float32
-    )
-    summed = row_reduce(partial_value, "row").astype(jnp.bfloat16)
+    half = w_qkv.shape[1] // 2
+    halves = []
+    for part in (w_qkv[:, :half], w_qkv[:, half:]):
+        partial_value = jnp.dot(
+            normed, lax.all_gather(part, "col", axis=1, tiled=True), preferred_element_type=jnp.float32
+        )
+        halves.append(row_reduce(partial_value, "row"))
+    summed = jnp.concatenate(halves, axis=1).astype(jnp.bfloat16)
     projected_output = row_gather(summed, "row").transpose(1, 0, 2).reshape(rows_here, -1)
     query_block = projected_output[:, : QUERY_HEADS * HEAD_SIZE].reshape(
         request_list, draft_tree, KEY_VALUE_HEADS, head_groups, HEAD_SIZE

time: 162 us -> 191 us (1.18)
  waiting for transfers between devices: 78.7 us -> 95.8 us
  local copies, waits for them, and re-layouts: 13.2 us -> 19.3 us
  starting transfers between devices: 26.9 us -> 32.6 us
    all_gather x1 -> x2, waiting for transfers between devices: 30.6 us -> 54.6 us  [shards(): lax.all_gather(part, 'col', axis=1, tiled=True)]
    all_to_all x1 -> x2, starting transfers between devices: 7.4 us -> 14.8 us  [row_reduce(): received = lax.all_to_all(pieces, axis_name, 0, 0)]
    all_to_all x1 -> x2, waiting for transfers between devices: 20.9 us -> 14.3 us  [row_reduce(): received = lax.all_to_all(pieces, axis_name, 0, 0)]
    reshape x1 -> x4, local copies, waits for them, and re-layouts: 1.32 us -> 4.12 us  [row_reduce(): partial.reshape(rows, count, cols // count).transpose(1, 0, 2).astype(sent)]
    unnamed x13 -> x19, local copies, waits for them, and re-layouts: 4.21 us -> 6.45 us
    dot_general x1 -> x2, matrix products: 2.61 us -> 4.02 us  [shards(): jnp.dot(normed, lax.all_gather(part, 'col', axis=1, tiled=True), preferre...]
  transfers between devices with their start and end apart: 6 -> 8, of which waited for: 5 -> 6; matrix products, arithmetic and copies ran while one was open for 13% -> 14% of each run, Pallas kernels for 0% -> 0%
where the time goes in v8:
time: 191 us; the launch traced here: 190 us
  waiting for transfers between devices  95.8 us (50%)
  starting transfers between devices  32.6 us (17%)
  local copies, waits for them, and re-layouts  19.3 us (10%)
  between operations  14 us (7%)
  blocking collectives  13.8 us (7%)
  other arithmetic  7.5 us (4%)
  matrix products  7.28 us (4%)
    all_gather x2, waiting for transfers between devices, shards(): lax.all_gather(part, 'col', axis=1, tiled=True)  54.6 us
    all_to_all x2, waiting for transfers between devices, row_gather(): return lax.all_to_all(copies, axis_name, 0, 0)  17 us
    all_to_all x2, starting transfers between devices, row_reduce(): received = lax.all_to_all(pieces, axis_name, 0, 0)  14.8 us
    all_to_all x2, waiting for transfers between devices, row_reduce(): received = lax.all_to_all(pieces, axis_name, 0, 0)  14.3 us
    all_to_all x1, blocking collectives, row_reduce(): received = lax.all_to_all(pieces, axis_name, 0, 0)  13.8 us
    all_to_all x2, starting transfers between devices, row_gather(): return lax.all_to_all(copies, axis_name, 0, 0)  12.6 us
    all_to_all x1, waiting for transfers between devices, shards(): gathered = lax.all_to_all(packed, 'row', 1, 1)  9.17 us
    unnamed x19, local copies, waits for them, and re-layouts  6.45 us
  transfers between devices with their start and end apart: 8, of which 6 were waited for; matrix products, arithmetic and copies ran while one was open for 14% of the time, Pallas kernels for 0%

profile of v8, /device:TPU:2, one launch (start us, length us, event | category | flops | bytes accessed | tf_op | source)
XLA Modules:
  0.0 190.4 jit_solution(11534638111007706878)
XLA Ops:
  6.5 1.1 fusion.53
  8.4 0.7 copy.111
  9.2 0.9 fusion.25
  10.7 7.5 %all-to-all-start = ((f32[16,1,64]{2,1,0:T(1,128)}), f32[16,1,64]{2,1,0:T(1,128)S(1)}, u32[]{:S(2)}, u32[]{:S(2)}) async-start(f32[16,1,64]{2,1,0:T(1,128)} %broadcast_in_dim.88), calls=%async_computation | async-start | bytes 16384 | tf_op jit(solution)/shard_map/all_to_all | solution.py:37
  19.6 4.8 %all-to-all-done = f32[16,1,64]{2,1,0:T(1,128)S(1)} async-done(((f32[16,1,64]{2,1,0:T(1,128)}), f32[16,1,64]{2,1,0:T(1,128)S(1)}, u32[]{:S(2)}, u32[]{:S(2)}) %all-to-all-start) | async-done | bytes 4128 | tf_op jit(solution)/shard_map/all_to_all | solution.py:37
  24.3 26.7 %all-gather.6.cloned.1.call-done = bf16[256,3072]{0,1:T(8,128)(2,1)} async-done(((bf16[256,192]{0,1:T(8,128)(2,1)}), bf16[256,3072]{0,1:T(8,128)(2,1)}) %all-gather.6.cloned.1.call-update) | async-done | bytes 1572880 | tf_op jit(solution)/shard_map/all_gather | solution.py:60
  51.0 2.0 %fusion.43 = f32[64,3072]{1,0:T(8,128)S(1)} fusion(bf16[256,3072]{0,1:T(8,128)(2,1)} %all-gather.6.cloned.1.call-done, bf16[64,256]{1,0:T(8,128)(2,1)} %param.8, f32[256]{0:T(256)S(1)} %convert_element_type.93, f32[64]{0:T(128)S(1)} %add_rsqrt_fusion), kind=kOutput, calls=%fused_computation.71 | convolution fusion | flops 100728832 | bytes 2393344 | tf_op jit(solution)/shard_map/dot_general | solution.py:59
  53.6 1.6 copy.141
  55.1 7.4 %all-to-all-start.2 = ((f32[16,64,192]{2,1,0:T(8,128)}), f32[16,64,192]{2,1,0:T(8,128)S(1)}, u32[]{:S(2)}, u32[]{:S(2)}) async-start(f32[16,64,192]{2,1,0:T(8,128)} %bitcast.99), calls=%async_computation.2 | async-start | bytes 2097152 | tf_op jit(solution)/shard_map/all_to_all | solution.py:30
  62.5 27.9 %all-gather.4.cloned.1.call-done = bf16[256,3072]{0,1:T(8,128)(2,1)} async-done(((bf16[256,192]{0,1:T(8,128)(2,1)}), bf16[256,3072]{0,1:T(8,128)(2,1)}) %all-gather.4.cloned.1.call-update) | async-done | bytes 1572880 | tf_op jit(solution)/shard_map/all_gather | solution.py:60
  90.5 2.0 %fusion.45 = f32[64,3072]{1,0:T(8,128)S(1)} fusion(bf16[256,3072]{0,1:T(8,128)(2,1)} %all-gather.4.cloned.1.call-done, bf16[64,256]{1,0:T(8,128)(2,1)S(1)} %copy-done.4, f32[256]{0:T(256)S(1)} %convert_element_type.93, f32[64]{0:T(128)S(1)} %add_rsqrt_fusion), kind=kOutput, calls=%fused_computation.72 | convolution fusion | flops 100728832 | bytes 2393344 | tf_op jit(solution)/shard_map/dot_general | solution.py:59
  93.0 1.6 copy.142
  94.6 7.4 %all-to-all-start.1 = ((f32[16,64,192]{2,1,0:T(8,128)}), f32[16,64,192]{2,1,0:T(8,128)S(1)}, u32[]{:S(2)}, u32[]{:S(2)}) async-start(f32[16,64,192]{2,1,0:T(8,128)} %bitcast.100), calls=%async_computation.1 | async-start | bytes 2097152 | tf_op jit(solution)/shard_map/all_to_all | solution.py:30
  102.7 0.9 copy.117
  103.9 14.3 %all-to-all-done.1 = f32[16,64,192]{2,1,0:T(8,128)S(1)} async-done(((f32[16,64,192]{2,1,0:T(8,128)}), f32[16,64,192]{2,1,0:T(8,128)S(1)}, u32[]{:S(2)}, u32[]{:S(2)}) %all-to-all-start.1) | async-done | bytes 786464 | tf_op jit(solution)/shard_map/all_to_all | solution.py:30
  118.3 1.0 broadcast_in_dim.89
  119.3 5.2 %all-to-all-start.3 = ((bf16[16,64,384]{2,1,0:T(8,128)(2,1)}), bf16[16,64,384]{2,1,0:T(8,128)(2,1)S(1)}, u32[]{:S(2)}, u32[]{:S(2)}) async-start(bf16[16,64,384]{2,1,0:T(8,128)(2,1)} %broadcast_in_dim.89), calls=%async_computation.3 | async-start | bytes 1572864 | tf_op jit(solution)/shard_map/all_to_all | solution.py:37
  125.2 12.2 %all-to-all-done.3 = bf16[16,64,384]{2,1,0:T(8,128)(2,1)S(1)} async-done(((bf16[16,64,384]{2,1,0:T(8,128)(2,1)}), bf16[16,64,384]{2,1,0:T(8,128)(2,1)S(1)}, u32[]{:S(2)}, u32[]{:S(2)}) %all-to-all-start.3) | async-done | bytes 786464 | tf_op jit(solution)/shard_map/all_to_all | solution.py:37
  137.6 0.9 copy-done
  138.4 1.0 slice_bitcast_fusion.3
  141.1 0.8 copy.93
  141.9 0.9 fusion.2
  142.8 1.5 maximum_maximum_fusion
  144.3 5.1 %all-to-all-start.4 = ((f32[1,16,2,65,128]{4,2,3,0,1:T(2,128)}), f32[1,16,2,65,128]{4,2,3,0,1:T(2,128)S(1)}, u32[]{:S(2)}, u32[]{:S(2)}) async-start(f32[1,16,2,65,128]{4,2,3,0,1:T(2,128)} %maximum_maximum_fusion), calls=%async_computation.4 | async-start | bytes 2129920 | tf_op jit(solution)/shard_map/all_to_all | solution.py:108
  149.7 3.3 %copy.103 = bf16[4096,256]{1,0:T(8,128)(2,1)S(1)} copy(bf16[4096,256]{0,1:T(8,128)(2,1)} %bitcast.106) | data formatting | bytes 4194304 | tf_op jit(solution)/shard_map/dot_general | solution.py:144
  153.0 1.1 copy.119
  154.2 1.0 slice_bitcast_fusion
  155.6 9.2 %all-to-all-done.4 = f32[1,16,2,65,128]{4,2,3,0,1:T(2,128)S(1)} async-done(((f32[1,16,2,65,128]{4,2,3,0,1:T(2,128)}), f32[1,16,2,65,128]{4,2,3,0,1:T(2,128)S(1)}, u32[]{:S(2)}, u32[]{:S(2)}) %all-to-all-start.4) | async-done | bytes 1064992 | tf_op jit(solution)/shard_map/all_to_all | solution.py:108
  164.8 1.0 copy.98
  165.9 2.2 %fusion.14 = f32[2,64,128]{2,0,1:T(2,128)S(1)} fusion(f32[1,16,2,65,128]{4,2,3,0,1:T(2,128)S(1)} %all-to-all-done.4, f32[16,2,64]{1,2,0:T(8,128)} %copy.98), kind=kLoop, calls=%fused_computation.27 | loop fusion | flops 507904 | bytes 1122304 | tf_op jit(solution)/shard_map/reduce_sum | solution.py:140
  168.6 0.8 fusion.4
  169.3 13.8 %all_to_all.31 = bf16[16,64,256]{2,1,0:T(8,128)(2,1)S(1)} all-to-all(bf16[16,64,256]{2,1,0:T(8,128)(2,1)S(1)} %fusion.4), channel_id=1, replica_groups=mesh['row'=16,'col'=16] {'row'}, dimensions={0} | all-to-all | bytes 1048576 | tf_op jit(solution)/shard_map/all_to_all | solution.py:30
  (58 shorter events, 8.6 us)
Async XLA Ops:
  6.5 44.5 %all-gather.6.cloned.1.call-start = ((), (), s32[]{:S(2)}) async-start(), calls=%async_computation.7 | async-start | bytes 1671168 | tf_op jit(solution)/shard_map/all_gather | solution.py:60
  8.4 82.1 %all-gather.4.cloned.1.call-start = ((), (), s32[]{:S(2)}) async-start(), calls=%async_computation.6 | async-start | bytes 1671168 | tf_op jit(solution)/shard_map/all_gather | solution.py:60
  10.7 13.6 %all-to-all-start = ((f32[16,1,64]{2,1,0:T(1,128)}), f32[16,1,64]{2,1,0:T(1,128)S(1)}, u32[]{:S(2)}, u32[]{:S(2)}) async-start(f32[16,1,64]{2,1,0:T(1,128)} %broadcast_in_dim.88), calls=%async_computation | async-start | bytes 16384 | tf_op jit(solution)/shard_map/all_to_all | solution.py:37
  18.2 131.5 %all-gather.8.cloned.1.call-start = ((), (), s32[]{:S(2)}) async-start(), calls=%async_computation.8 | async-start | bytes 2228224 | tf_op jit(solution)/shard_map/all_gather | solution.py:146
  53.5 36.9 %copy-start.4 = (bf16[64,256]{1,0:T(8,128)(2,1)S(1)}, bf16[64,256]{1,0:T(8,128)(2,1)}, u32[]{:S(2)}) copy-start(bf16[64,256]{1,0:T(8,128)(2,1)} %param.8) | copy-start | bytes 98308
  55.1 39.4 %all-to-all-start.2 = ((f32[16,64,192]{2,1,0:T(8,128)}), f32[16,64,192]{2,1,0:T(8,128)S(1)}, u32[]{:S(2)}, u32[]{:S(2)}) async-start(f32[16,64,192]{2,1,0:T(8,128)} %bitcast.99), calls=%async_computation.2 | async-start | bytes 2097152 | tf_op jit(solution)/shard_map/all_to_all | solution.py:30
  93.0 9.7 %copy-start.1 = (bf16[1,256,1024]{2,1,0:T(8,128)(2,1)S(1)}, bf16[1,256,1024]{2,1,0:T(8,128)(2,1)}, u32[]{:S(2)}) copy-start(bf16[1,256,1024]{2,1,0:T(8,128)(2,1)} %param.12) | copy-start | bytes 1572868
  94.6 9.0 %copy-start.2 = (bf16[1,256,1024]{2,1,0:T(8,128)(2,1)S(1)}, bf16[1,256,1024]{2,1,0:T(8,128)(2,1)}, u32[]{:S(2)}) copy-start(bf16[1,256,1024]{2,1,0:T(8,128)(2,1)} %param.13) | copy-start | bytes 1572868
  94.6 9.1 %copy-start.5 = (s32[1,64]{1,0:T(1,128)S(1)}, s32[1,64]{1,0:T(1,128)}, u32[]{:S(2)}) copy-start(s32[1,64]{1,0:T(1,128)} %param.15) | copy-start | bytes 772
  94.6 23.6 %all-to-all-start.1 = ((f32[16,64,192]{2,1,0:T(8,128)}), f32[16,64,192]{2,1,0:T(8,128)S(1)}, u32[]{:S(2)}, u32[]{:S(2)}) async-start(f32[16,64,192]{2,1,0:T(8,128)} %bitcast.100), calls=%async_computation.1 | async-start | bytes 2097152 | tf_op jit(solution)/shard_map/all_to_all | solution.py:30
  119.3 18.1 %all-to-all-start.3 = ((bf16[16,64,384]{2,1,0:T(8,128)(2,1)}), bf16[16,64,384]{2,1,0:T(8,128)(2,1)S(1)}, u32[]{:S(2)}, u32[]{:S(2)}) async-start(bf16[16,64,384]{2,1,0:T(8,128)(2,1)} %broadcast_in_dim.89), calls=%async_computation.3 | async-start | bytes 1572864 | tf_op jit(solution)/shard_map/all_to_all | solution.py:37
  137.5 2.3 %copy-start.3 = (bf16[32,8,8,128]{3,2,1,0:T(8,128)(2,1)S(1)}, bf16[32,8,8,128]{3,2,1,0:T(8,128)(2,1)}, u32[]{:S(2)}) copy-start(bf16[32,8,8,128]{3,2,1,0:T(8,128)(2,1)} %copy.117) | copy-start | bytes 1572868
  137.6 0.9 copy-start
  144.3 20.4 %all-to-all-start.4 = ((f32[1,16,2,65,128]{4,2,3,0,1:T(2,128)}), f32[1,16,2,65,128]{4,2,3,0,1:T(2,128)S(1)}, u32[]{:S(2)}, u32[]{:S(2)}) async-start(f32[1,16,2,65,128]{4,2,3,0,1:T(2,128)} %maximum_maximum_fusion), calls=%async_computation.4 | async-start | bytes 2129920 | tf_op jit(solution)/shard_map/all_to_all | solution.py:108
Sparse Core Ops, SparseCore 0:
  9.2 41.8 all-gather.5
  52.9 37.5 all-gather.3
  92.2 39.2 all-gather.7

commit v9 on v7

--- a/solution.py
+++ b/solution.py
@@ -56,16 +56,26 @@
     partial_value = jnp.dot(
         normed, lax.all_gather(w_qkv, "col", axis=1, tiled=True), preferred_element_type=jnp.float32
     )
-    summed = row_reduce(partial_value, "row").astype(jnp.bfloat16)
-    projected_output = row_gather(summed, "row").transpose(1, 0, 2).reshape(rows_here, -1)
-    query_block = projected_output[:, : QUERY_HEADS * HEAD_SIZE].reshape(
+    query_cols = QUERY_HEADS * HEAD_SIZE
+    query_part = partial_value[:, :query_cols].reshape(rows_here, row_count, -1)
+    pair_part = (
+        partial_value[:, query_cols:]
+        .reshape(rows_here, 2, KEY_VALUE_HEADS, HEAD_SIZE)
+        .transpose(0, 2, 1, 3)
+        .reshape(rows_here, row_count, -1)
+    )
+    owned = jnp.concatenate([query_part, pair_part], axis=2).transpose(1, 0, 2)
+    summed = jnp.sum(lax.all_to_all(owned, "row", 0, 0), axis=0).astype(jnp.bfloat16)
+    query_mine = summed[:, : heads_dev * HEAD_SIZE]
+    pair_mine = summed[:, heads_dev * HEAD_SIZE :]
+    partner = [(i, i ^ 1) for i in range(row_count)]
+    pair_theirs = lax.ppermute(pair_mine, "row", partner)
+    is_key = row_index % 2 == 0
+    key_mine = jnp.where(is_key, pair_mine, pair_theirs)
+    value_mine = jnp.where(is_key, pair_theirs, pair_mine)
+    all_queries = row_gather(query_mine, "row").transpose(1, 0, 2).reshape(rows_here, -1)
+    query_block = all_queries.reshape(
         request_list, draft_tree, KEY_VALUE_HEADS, head_groups, HEAD_SIZE
-    )
-    new_key_block = projected_output[
-        :, QUERY_HEADS * HEAD_SIZE : (QUERY_HEADS + KEY_VALUE_HEADS) * HEAD_SIZE
-    ].reshape(request_list, draft_tree, KEY_VALUE_HEADS, HEAD_SIZE)
-    new_value_block = projected_output[:, (QUERY_HEADS + KEY_VALUE_HEADS) * HEAD_SIZE :].reshape(
-        request_list, draft_tree, KEY_VALUE_HEADS, HEAD_SIZE
     )
     first_slot = row_index * token_positions
     slot_ids = first_slot + jnp.arange(token_positions, dtype=jnp.int32)
@@ -106,15 +116,14 @@
     block_max = gathered[:, :, :, draft_tree, :draft_tree]
     block_total = gathered[:, :, :, draft_tree, draft_tree : 2 * draft_tree]
     allowed = ancestors(parents)[:, None, :, :]
-    query_heads = projected_output[:, : QUERY_HEADS * HEAD_SIZE].reshape(
-        request_list, draft_tree, QUERY_HEADS, HEAD_SIZE
+    query_own = query_mine.reshape(request_list, draft_tree, heads_dev, HEAD_SIZE)
+    key_own = jnp.broadcast_to(
+        key_mine.reshape(request_list, draft_tree, 1, HEAD_SIZE),
+        (request_list, draft_tree, heads_dev, HEAD_SIZE),
     )
-    query_own = lax.dynamic_slice_in_dim(query_heads, row_index * heads_dev, heads_dev, 2)
-    key_own = lax.dynamic_slice_in_dim(
-        jnp.repeat(new_key_block, head_groups, axis=2), row_index * heads_dev, heads_dev, 2
-    )
-    value_own = lax.dynamic_slice_in_dim(
-        jnp.repeat(new_value_block, head_groups, axis=2), row_index * heads_dev, heads_dev, 2
+    value_own = jnp.broadcast_to(
+        value_mine.reshape(request_list, draft_tree, 1, HEAD_SIZE),
+        (request_list, draft_tree, heads_dev, HEAD_SIZE),
     )
     tree_scores = (
         jnp.einsum("rthd,rshd->rhts", query_own, key_own, preferred_element_type=jnp.float32)

time: 162 us -> 151 us (0.932)
  blocking collectives: 14.3 us -> 41.7 us
  waiting for transfers between devices: 78.7 us -> 55.8 us
  starting transfers between devices: 26.9 us -> 17.5 us
  local copies, waits for them, and re-layouts: 13.2 us -> 7.85 us
    all_to_all x0 -> x1, blocking collectives: none -> 28.9 us  [shards(): lax.all_to_all(owned, 'row', 0, 0)]
    all_to_all x1 -> x0, waiting for transfers between devices: 20.9 us -> none  [row_reduce(): received = lax.all_to_all(pieces, axis_name, 0, 0)]
    all_to_all x1 -> x0, starting transfers between devices: 7.4 us -> none  [row_reduce(): received = lax.all_to_all(pieces, axis_name, 0, 0)]
    ppermute x0 -> x1, waiting for transfers between devices: none -> 6.86 us  [shards(): pair_theirs = lax.ppermute(pair_mine, 'row', partner)]
    all_to_all x1, waiting for transfers between devices: 9.09 us -> 3.91 us  [shards(): gathered = lax.all_to_all(packed, 'row', 1, 1)]
    unnamed x13 -> x11, local copies, waits for them, and re-layouts: 4.21 us -> 0.34 us
    all_to_all x2, waiting for transfers between devices: 16.8 us -> 13 us  [row_gather(): return lax.all_to_all(copies, axis_name, 0, 0)]
    all_to_all x2, starting transfers between devices: 14.4 us -> 12.3 us  [row_gather(): return lax.all_to_all(copies, axis_name, 0, 0)]
  transfers between devices with their start and end apart: 6 -> 6, of which waited for: 5 -> 5; matrix products, arithmetic and copies ran while one was open for 13% -> 11% of each run, Pallas kernels for 0% -> 0%
where the time goes in v9:
time: 151 us; the launch traced here: 150 us
  waiting for transfers between devices  55.8 us (37%)
  blocking collectives  41.7 us (28%)
  starting transfers between devices  17.5 us (12%)
  between operations  14.3 us (9%)
  local copies, waits for them, and re-layouts  7.85 us (5%)
  other arithmetic  7.46 us (5%)
  matrix products  5.84 us (4%)
    all_gather x1, waiting for transfers between devices, shards(): lax.all_gather(w_qkv, 'col', axis=1, tiled=True)  30.6 us
    all_to_all x1, blocking collectives, shards(): lax.all_to_all(owned, 'row', 0, 0)  28.9 us
    all_to_all x2, waiting for transfers between devices, row_gather(): return lax.all_to_all(copies, axis_name, 0, 0)  13 us
    all_to_all x1, blocking collectives, row_reduce(): received = lax.all_to_all(pieces, axis_name, 0, 0)  12.8 us
    all_to_all x2, starting transfers between devices, row_gather(): return lax.all_to_all(copies, axis_name, 0, 0)  12.3 us
    ppermute x1, waiting for transfers between devices, shards(): pair_theirs = lax.ppermute(pair_mine, 'row', partner)  6.86 us
    all_to_all x1, starting transfers between devices, shards(): gathered = lax.all_to_all(packed, 'row', 1, 1)  4.9 us
    all_to_all x1, waiting for transfers between devices, shards(): gathered = lax.all_to_all(packed, 'row', 1, 1)  3.91 us
  transfers between devices with their start and end apart: 6, of which 5 were waited for; matrix products, arithmetic and copies ran while one was open for 11% of the time, Pallas kernels for 0%

profile of v9, /device:TPU:2, one launch (start us, length us, event | category | flops | bytes accessed | tf_op | source)
XLA Modules:
  0.0 150.4 jit_solution(1550734635356049737)
XLA Ops:
  6.5 0.7 all-gather.3.cloned.1.call-update
  7.3 0.9 fusion.25
  8.1 0.6 broadcast_in_dim.88
  8.7 7.5 %all-to-all-start = ((f32[16,1,64]{2,1,0:T(1,128)}), f32[16,1,64]{2,1,0:T(1,128)S(1)}, u32[]{:S(2)}, u32[]{:S(2)}) async-start(f32[16,1,64]{2,1,0:T(1,128)} %broadcast_in_dim.88), calls=%async_computation | async-start | bytes 16384 | tf_op jit(solution)/shard_map/all_to_all | solution.py:37
  16.3 0.7 all-gather.5.cloned.1.call-update
  17.0 0.7 convert_element_type.91
  17.6 4.7 %all-to-all-done = f32[16,1,64]{2,1,0:T(1,128)S(1)} async-done(((f32[16,1,64]{2,1,0:T(1,128)}), f32[16,1,64]{2,1,0:T(1,128)S(1)}, u32[]{:S(2)}, u32[]{:S(2)}) %all-to-all-start) | async-done | bytes 4128 | tf_op jit(solution)/shard_map/all_to_all | solution.py:37
  22.4 30.6 %all-gather.3.cloned.1.call-done = bf16[256,6144]{1,0:T(8,128)(2,1)} async-done(((bf16[256,384]{1,0:T(8,128)(2,1)}), bf16[256,6144]{1,0:T(8,128)(2,1)}) %all-gather.3.cloned.1.call-update) | async-done | bytes 3145744 | tf_op jit(solution)/shard_map/all_gather | solution.py:57
  53.0 2.6 %fusion.31 = f32[64,6144]{1,0:T(8,128)S(1)} fusion(bf16[256,6144]{1,0:T(8,128)(2,1)} %all-gather.3.cloned.1.call-done, bf16[64,256]{1,0:T(8,128)(2,1)} %param.8, f32[256]{0:T(256)S(1)} %convert_element_type.91, f32[64]{0:T(128)S(1)} %add_rsqrt_fusion), kind=kOutput, calls=%fused_computation.51 | convolution fusion | flops 201392128 | bytes 4752640 | tf_op jit(solution)/shard_map/dot_general | solution.py:56
  55.9 0.2 copy.73
  56.3 28.9 %all_to_all.26 = f32[16,64,384]{2,1,0:T(8,128)S(1)} all-to-all(f32[16,64,384]{2,1,0:T(8,128)S(1)} %maximum_bitcast_fusion), channel_id=1, replica_groups=mesh['row'=16,'col'=16] {'row'}, dimensions={0} | all-to-all | bytes 3145728 | tf_op jit(solution)/shard_map/all_to_all | solution.py:68
  85.2 0.8 broadcast_in_dim.89
  86.1 4.8 %all-to-all-start.2 = ((bf16[16,64,256]{2,1,0:T(8,128)(2,1)}), bf16[16,64,256]{2,1,0:T(8,128)(2,1)S(1)}, u32[]{:S(2)}, u32[]{:S(2)}) async-start(bf16[16,64,256]{2,1,0:T(8,128)(2,1)} %broadcast_in_dim.89), calls=%async_computation.2 | async-start | bytes 1048576 | tf_op jit(solution)/shard_map/all_to_all | solution.py:37
  91.9 0.2 convolution_compare_fusion.5
  92.2 8.2 %all-to-all-done.2 = bf16[16,64,256]{2,1,0:T(8,128)(2,1)S(1)} async-done(((bf16[16,64,256]{2,1,0:T(8,128)(2,1)}), bf16[16,64,256]{2,1,0:T(8,128)(2,1)S(1)}, u32[]{:S(2)}, u32[]{:S(2)}) %all-to-all-start.2) | async-done | bytes 524320 | tf_op jit(solution)/shard_map/all_to_all | solution.py:37
  100.5 0.3 copy.75
  100.9 0.6 bitcast_reduce_fusion
  101.5 0.7 fusion.12
  102.2 0.8 copy.79
  103.0 0.9 fusion.2
  103.9 1.5 maximum_maximum_fusion
  105.4 4.9 %all-to-all-start.3 = ((f32[1,16,2,65,128]{4,2,3,0,1:T(2,128)}), f32[1,16,2,65,128]{4,2,3,0,1:T(2,128)S(1)}, u32[]{:S(2)}, u32[]{:S(2)}) async-start(f32[1,16,2,65,128]{4,2,3,0,1:T(2,128)} %maximum_maximum_fusion), calls=%async_computation.3 | async-start | bytes 2129920 | tf_op jit(solution)/shard_map/all_to_all | solution.py:114
  110.7 0.3 collective-permute-start
  111.3 3.3 %copy.87 = bf16[4096,256]{1,0:T(8,128)(2,1)S(1)} copy(bf16[4096,256]{0,1:T(8,128)(2,1)} %bitcast.97) | data formatting | bytes 4194304 | tf_op jit(solution)/shard_map/dot_general | solution.py:149
  114.6 6.9 %collective-permute-done = bf16[64,128]{1,0:T(8,128)(2,1)S(1)} collective-permute-done((bf16[64,128]{1,0:T(8,128)(2,1)S(1)}, bf16[64,128]{1,0:T(8,128)(2,1)S(1)}, u32[]{:S(2)}, u32[]{:S(2)}) %collective-permute-start) | collective-permute-done | bytes 16416 | tf_op jit(solution)/shard_map/ppermute | solution.py:72
  121.6 3.9 %all-to-all-done.3 = f32[1,16,2,65,128]{4,2,3,0,1:T(2,128)S(1)} async-done(((f32[1,16,2,65,128]{4,2,3,0,1:T(2,128)}), f32[1,16,2,65,128]{4,2,3,0,1:T(2,128)S(1)}, u32[]{:S(2)}, u32[]{:S(2)}) %all-to-all-start.3) | async-done | bytes 1064992 | tf_op jit(solution)/shard_map/all_to_all | solution.py:114
  125.6 1.0 copy.83
  126.8 2.2 %fusion.14 = f32[2,64,128]{2,0,1:T(2,128)S(1)} fusion(f32[1,16,2,65,128]{4,2,3,0,1:T(2,128)S(1)} %all-to-all-done.3, f32[16,2,64]{1,2,0:T(8,128)} %copy.83), kind=kLoop, calls=%fused_computation.29 | loop fusion | flops 507904 | bytes 1122304 | tf_op jit(solution)/shard_map/reduce_sum | solution.py:145
  129.0 0.2 fusion.9
  129.3 0.8 fusion.4
  130.0 12.8 %all_to_all.27 = bf16[16,64,256]{2,1,0:T(8,128)(2,1)S(1)} all-to-all(bf16[16,64,256]{2,1,0:T(8,128)(2,1)S(1)} %fusion.4), channel_id=1, replica_groups=mesh['row'=16,'col'=16] {'row'}, dimensions={0} | all-to-all | bytes 1048576 | tf_op jit(solution)/shard_map/all_to_all | solution.py:30
  142.9 0.7 reduce_sum.83
  (40 shorter events, 2.2 us)
Async XLA Ops:
  6.5 46.5 %all-gather.3.cloned.1.call-start = ((), (), s32[]{:S(2)}) async-start(), calls=%async_computation.5 | async-start | bytes 3342336 | tf_op jit(solution)/shard_map/all_gather | solution.py:57
  8.7 13.6 %all-to-all-start = ((f32[16,1,64]{2,1,0:T(1,128)}), f32[16,1,64]{2,1,0:T(1,128)S(1)}, u32[]{:S(2)}, u32[]{:S(2)}) async-start(f32[16,1,64]{2,1,0:T(1,128)} %broadcast_in_dim.88), calls=%async_computation | async-start | bytes 16384 | tf_op jit(solution)/shard_map/all_to_all | solution.py:37
  16.2 95.1 %all-gather.5.cloned.1.call-start = ((), (), s32[]{:S(2)}) async-start(), calls=%async_computation.6 | async-start | bytes 2228224 | tf_op jit(solution)/shard_map/all_gather | solution.py:151
  85.1 5.8 %copy-start.2 = (s32[1,64]{1,0:T(1,128)S(1)}, s32[1,64]{1,0:T(1,128)}, u32[]{:S(2)}) copy-start(s32[1,64]{1,0:T(1,128)} %param.15) | copy-start | bytes 772
  85.1 6.6 %copy-start = (bf16[1,256,1024]{2,1,0:T(8,128)(2,1)S(1)}, bf16[1,256,1024]{2,1,0:T(8,128)(2,1)}, u32[]{:S(2)}) copy-start(bf16[1,256,1024]{2,1,0:T(8,128)(2,1)} %param.12) | copy-start | bytes 1572868
  85.1 6.7 %copy-start.1 = (bf16[1,256,1024]{2,1,0:T(8,128)(2,1)S(1)}, bf16[1,256,1024]{2,1,0:T(8,128)(2,1)}, u32[]{:S(2)}) copy-start(bf16[1,256,1024]{2,1,0:T(8,128)(2,1)} %param.13) | copy-start | bytes 1572868
  86.1 14.4 %all-to-all-start.2 = ((bf16[16,64,256]{2,1,0:T(8,128)(2,1)}), bf16[16,64,256]{2,1,0:T(8,128)(2,1)S(1)}, u32[]{:S(2)}, u32[]{:S(2)}) async-start(bf16[16,64,256]{2,1,0:T(8,128)(2,1)} %broadcast_in_dim.89), calls=%async_computation.2 | async-start | bytes 1048576 | tf_op jit(solution)/shard_map/all_to_all | solution.py:37
  105.4 20.1 %all-to-all-start.3 = ((f32[1,16,2,65,128]{4,2,3,0,1:T(2,128)}), f32[1,16,2,65,128]{4,2,3,0,1:T(2,128)S(1)}, u32[]{:S(2)}, u32[]{:S(2)}) async-start(f32[1,16,2,65,128]{4,2,3,0,1:T(2,128)} %maximum_maximum_fusion), calls=%async_computation.3 | async-start | bytes 2129920 | tf_op jit(solution)/shard_map/all_to_all | solution.py:114
  110.7 10.7 %collective-permute-start = (bf16[64,128]{1,0:T(8,128)(2,1)S(1)}, bf16[64,128]{1,0:T(8,128)(2,1)S(1)}, u32[]{:S(2)}, u32[]{:S(2)}) collective-permute-start(bf16[64,128]{1,0:T(8,128)(2,1)S(1)} %slice.33), channel_id=1, source_target_pairs={{0,16},{16,0},{32,48},{48,32},{64,80},{80,64},{96,112},{112,96},{1... | collective-permute-start | bytes 49160 | tf_op jit(solution)/shard_map/ppermute | solution.py:72
Sparse Core Ops, SparseCore 0:
  9.1 43.8 all-gather.2
  54.7 38.7 all-gather.4

commit v10 on v9

--- a/solution.py
+++ b/solution.py
@@ -70,6 +70,7 @@
     pair_mine = summed[:, heads_dev * HEAD_SIZE :]
     partner = [(i, i ^ 1) for i in range(row_count)]
     pair_theirs = lax.ppermute(pair_mine, "row", partner)
+    query_mine, pair_theirs = lax.optimization_barrier((query_mine, pair_theirs))
     is_key = row_index % 2 == 0
     key_mine = jnp.where(is_key, pair_mine, pair_theirs)
     value_mine = jnp.where(is_key, pair_theirs, pair_mine)

time: 151 us -> 153 us (1.013)
    all_to_all x1, waiting for transfers between devices: 3.91 us -> 10.1 us  [shards(): gathered = lax.all_to_all(packed, 'row', 1, 1)]
    ppermute x1, waiting for transfers between devices: 6.86 us -> 2.27 us  [shards(): pair_theirs = lax.ppermute(pair_mine, 'row', partner)]
  transfers between devices with their start and end apart: 6 -> 6, of which waited for: 5 -> 5; matrix products, arithmetic and copies ran while one was open for 11% -> 10% of each run, Pallas kernels for 0% -> 0%
where the time goes in v10:
time: 153 us
  waiting for transfers between devices  56.6 us (37%)
  blocking collectives  42.1 us (28%)
  starting transfers between devices  18.8 us (12%)
  between operations  14.3 us (9%)
  local copies, waits for them, and re-layouts  7.85 us (5%)
  other arithmetic  7.46 us (5%)
  matrix products  5.85 us (4%)
    all_gather x1, waiting for transfers between devices, shards(): lax.all_gather(w_qkv, 'col', axis=1, tiled=True)  30.6 us
    all_to_all x1, blocking collectives, shards(): lax.all_to_all(owned, 'row', 0, 0)  28.9 us
    all_to_all x1, blocking collectives, row_reduce(): received = lax.all_to_all(pieces, axis_name, 0, 0)  13.2 us
    all_to_all x2, starting transfers between devices, row_gather(): return lax.all_to_all(copies, axis_name, 0, 0)  12.3 us
    all_to_all x2, waiting for transfers between devices, row_gather(): return lax.all_to_all(copies, axis_name, 0, 0)  12.2 us
    all_to_all x1, waiting for transfers between devices, shards(): gathered = lax.all_to_all(packed, 'row', 1, 1)  10.1 us
    all_to_all x1, starting transfers between devices, shards(): gathered = lax.all_to_all(packed, 'row', 1, 1)  4.94 us
    dot_general x1, local copies, waits for them, and re-layouts, shards(): jnp.dot(attended, lax.all_gather(w_out, 'col', axis=1, tiled=True), prefe...  3.28 us
  transfers between devices with their start and end apart: 6, of which 5 were waited for; matrix products, arithmetic and copies ran while one was open for 10% of the time, Pallas kernels for 0%

profile of v10, /device:TPU:2, one launch (start us, length us, event | category | flops | bytes accessed | tf_op | source)
XLA Modules:
  0.0 152.9 jit_solution(357476080769653371)
XLA Ops:
  6.5 0.7 all-gather.3.cloned.1.call-update
  7.3 0.9 fusion.25
  8.1 0.6 broadcast_in_dim.88
  8.7 7.5 %all-to-all-start = ((f32[16,1,64]{2,1,0:T(1,128)}), f32[16,1,64]{2,1,0:T(1,128)S(1)}, u32[]{:S(2)}, u32[]{:S(2)}) async-start(f32[16,1,64]{2,1,0:T(1,128)} %broadcast_in_dim.88), calls=%async_computation | async-start | bytes 16384 | tf_op jit(solution)/shard_map/all_to_all | solution.py:37
  16.3 0.7 all-gather.5.cloned.1.call-update
  17.0 0.7 convert_element_type.91
  17.6 4.7 %all-to-all-done = f32[16,1,64]{2,1,0:T(1,128)S(1)} async-done(((f32[16,1,64]{2,1,0:T(1,128)}), f32[16,1,64]{2,1,0:T(1,128)S(1)}, u32[]{:S(2)}, u32[]{:S(2)}) %all-to-all-start) | async-done | bytes 4128 | tf_op jit(solution)/shard_map/all_to_all | solution.py:37
  22.4 30.6 %all-gather.3.cloned.1.call-done = bf16[256,6144]{1,0:T(8,128)(2,1)} async-done(((bf16[256,384]{1,0:T(8,128)(2,1)}), bf16[256,6144]{1,0:T(8,128)(2,1)}) %all-gather.3.cloned.1.call-update) | async-done | bytes 3145744 | tf_op jit(solution)/shard_map/all_gather | solution.py:57
  53.0 2.6 %fusion.31 = f32[64,6144]{1,0:T(8,128)S(1)} fusion(bf16[256,6144]{1,0:T(8,128)(2,1)} %all-gather.3.cloned.1.call-done, bf16[64,256]{1,0:T(8,128)(2,1)} %param.8, f32[256]{0:T(256)S(1)} %convert_element_type.91, f32[64]{0:T(128)S(1)} %add_rsqrt_fusion), kind=kOutput, calls=%fused_computation.51 | convolution fusion | flops 201392128 | bytes 4752640 | tf_op jit(solution)/shard_map/dot_general | solution.py:56
  56.0 0.2 copy.73
  56.3 28.9 %all_to_all.26 = f32[16,64,384]{2,1,0:T(8,128)S(1)} all-to-all(f32[16,64,384]{2,1,0:T(8,128)S(1)} %maximum_bitcast_fusion), channel_id=1, replica_groups=mesh['row'=16,'col'=16] {'row'}, dimensions={0} | all-to-all | bytes 3145728 | tf_op jit(solution)/shard_map/all_to_all | solution.py:68
  85.2 1.5 %collective-permute-start = (bf16[64,128]{1,0:T(8,128)(2,1)S(1)}, bf16[64,128]{1,0:T(8,128)(2,1)S(1)}, u32[]{:S(2)}, u32[]{:S(2)}) collective-permute-start(bf16[64,128]{1,0:T(8,128)(2,1)S(1)} %slice.31), channel_id=1, source_target_pairs={{0,16},{16,0},{32,48},{48,32},{64,80},{80,64},{96,112},{112,96},{1... | collective-permute-start | bytes 49160 | tf_op jit(solution)/shard_map/ppermute | solution.py:72
  86.8 2.3 %collective-permute-done = bf16[64,128]{1,0:T(8,128)(2,1)S(1)} collective-permute-done((bf16[64,128]{1,0:T(8,128)(2,1)S(1)}, bf16[64,128]{1,0:T(8,128)(2,1)S(1)}, u32[]{:S(2)}, u32[]{:S(2)}) %collective-permute-start) | collective-permute-done | bytes 16416 | tf_op jit(solution)/shard_map/ppermute | solution.py:72
  89.0 0.8 broadcast_in_dim.89
  89.9 4.8 %all-to-all-start.2 = ((bf16[16,64,256]{2,1,0:T(8,128)(2,1)}), bf16[16,64,256]{2,1,0:T(8,128)(2,1)S(1)}, u32[]{:S(2)}, u32[]{:S(2)}) async-start(bf16[16,64,256]{2,1,0:T(8,128)(2,1)} %broadcast_in_dim.89), calls=%async_computation.2 | async-start | bytes 1048576 | tf_op jit(solution)/shard_map/all_to_all | solution.py:37
  95.7 0.2 convolution_compare_fusion.5
  96.1 7.5 %all-to-all-done.2 = bf16[16,64,256]{2,1,0:T(8,128)(2,1)S(1)} async-done(((bf16[16,64,256]{2,1,0:T(8,128)(2,1)}), bf16[16,64,256]{2,1,0:T(8,128)(2,1)S(1)}, u32[]{:S(2)}, u32[]{:S(2)}) %all-to-all-start.2) | async-done | bytes 524320 | tf_op jit(solution)/shard_map/all_to_all | solution.py:37
  103.5 0.3 copy.75
  104.0 0.6 bitcast_reduce_fusion
  104.6 0.7 fusion.12
  105.3 0.8 copy.79
  106.1 0.9 fusion.2
  107.0 1.5 maximum_maximum_fusion
  108.5 4.9 %all-to-all-start.3 = ((f32[1,16,2,65,128]{4,2,3,0,1:T(2,128)}), f32[1,16,2,65,128]{4,2,3,0,1:T(2,128)S(1)}, u32[]{:S(2)}, u32[]{:S(2)}) async-start(f32[1,16,2,65,128]{4,2,3,0,1:T(2,128)} %maximum_maximum_fusion), calls=%async_computation.3 | async-start | bytes 2129920 | tf_op jit(solution)/shard_map/all_to_all | solution.py:115
  114.1 3.3 %copy.87 = bf16[4096,256]{1,0:T(8,128)(2,1)S(1)} copy(bf16[4096,256]{0,1:T(8,128)(2,1)} %bitcast.99) | data formatting | bytes 4194304 | tf_op jit(solution)/shard_map/dot_general | solution.py:150
  117.6 10.1 %all-to-all-done.3 = f32[1,16,2,65,128]{4,2,3,0,1:T(2,128)S(1)} async-done(((f32[1,16,2,65,128]{4,2,3,0,1:T(2,128)}), f32[1,16,2,65,128]{4,2,3,0,1:T(2,128)S(1)}, u32[]{:S(2)}, u32[]{:S(2)}) %all-to-all-start.3) | async-done | bytes 1064992 | tf_op jit(solution)/shard_map/all_to_all | solution.py:115
  127.7 1.0 copy.83
  128.9 2.2 %fusion.14 = f32[2,64,128]{2,0,1:T(2,128)S(1)} fusion(f32[1,16,2,65,128]{4,2,3,0,1:T(2,128)S(1)} %all-to-all-done.3, f32[16,2,64]{1,2,0:T(8,128)} %copy.83), kind=kLoop, calls=%fused_computation.29 | loop fusion | flops 507904 | bytes 1122304 | tf_op jit(solution)/shard_map/reduce_sum | solution.py:146
  131.1 0.2 fusion.9
  131.4 0.8 fusion.4
  132.2 13.2 %all_to_all.27 = bf16[16,64,256]{2,1,0:T(8,128)(2,1)S(1)} all-to-all(bf16[16,64,256]{2,1,0:T(8,128)(2,1)S(1)} %fusion.4), channel_id=1, replica_groups=mesh['row'=16,'col'=16] {'row'}, dimensions={0} | all-to-all | bytes 1048576 | tf_op jit(solution)/shard_map/all_to_all | solution.py:30
  145.4 0.7 reduce_sum.83
  (40 shorter events, 2.3 us)
Async XLA Ops:
  6.5 46.5 %all-gather.3.cloned.1.call-start = ((), (), s32[]{:S(2)}) async-start(), calls=%async_computation.5 | async-start | bytes 3342336 | tf_op jit(solution)/shard_map/all_gather | solution.py:57
  8.7 13.6 %all-to-all-start = ((f32[16,1,64]{2,1,0:T(1,128)}), f32[16,1,64]{2,1,0:T(1,128)S(1)}, u32[]{:S(2)}, u32[]{:S(2)}) async-start(f32[16,1,64]{2,1,0:T(1,128)} %broadcast_in_dim.88), calls=%async_computation | async-start | bytes 16384 | tf_op jit(solution)/shard_map/all_to_all | solution.py:37
  16.2 97.9 %all-gather.5.cloned.1.call-start = ((), (), s32[]{:S(2)}) async-start(), calls=%async_computation.6 | async-start | bytes 2228224 | tf_op jit(solution)/shard_map/all_gather | solution.py:152
  85.1 9.6 %copy-start.2 = (s32[1,64]{1,0:T(1,128)S(1)}, s32[1,64]{1,0:T(1,128)}, u32[]{:S(2)}) copy-start(s32[1,64]{1,0:T(1,128)} %param.15) | copy-start | bytes 772
  85.1 10.4 %copy-start = (bf16[1,256,1024]{2,1,0:T(8,128)(2,1)S(1)}, bf16[1,256,1024]{2,1,0:T(8,128)(2,1)}, u32[]{:S(2)}) copy-start(bf16[1,256,1024]{2,1,0:T(8,128)(2,1)} %param.12) | copy-start | bytes 1572868
  85.1 10.5 %copy-start.1 = (bf16[1,256,1024]{2,1,0:T(8,128)(2,1)S(1)}, bf16[1,256,1024]{2,1,0:T(8,128)(2,1)}, u32[]{:S(2)}) copy-start(bf16[1,256,1024]{2,1,0:T(8,128)(2,1)} %param.13) | copy-start | bytes 1572868
  85.2 3.8 %collective-permute-start = (bf16[64,128]{1,0:T(8,128)(2,1)S(1)}, bf16[64,128]{1,0:T(8,128)(2,1)S(1)}, u32[]{:S(2)}, u32[]{:S(2)}) collective-permute-start(bf16[64,128]{1,0:T(8,128)(2,1)S(1)} %slice.31), channel_id=1, source_target_pairs={{0,16},{16,0},{32,48},{48,32},{64,80},{80,64},{96,112},{112,96},{1... | collective-permute-start | bytes 49160 | tf_op jit(solution)/shard_map/ppermute | solution.py:72
  89.9 13.7 %all-to-all-start.2 = ((bf16[16,64,256]{2,1,0:T(8,128)(2,1)}), bf16[16,64,256]{2,1,0:T(8,128)(2,1)S(1)}, u32[]{:S(2)}, u32[]{:S(2)}) async-start(bf16[16,64,256]{2,1,0:T(8,128)(2,1)} %broadcast_in_dim.89), calls=%async_computation.2 | async-start | bytes 1048576 | tf_op jit(solution)/shard_map/all_to_all | solution.py:37
  108.5 19.2 %all-to-all-start.3 = ((f32[1,16,2,65,128]{4,2,3,0,1:T(2,128)}), f32[1,16,2,65,128]{4,2,3,0,1:T(2,128)S(1)}, u32[]{:S(2)}, u32[]{:S(2)}) async-start(f32[1,16,2,65,128]{4,2,3,0,1:T(2,128)} %maximum_maximum_fusion), calls=%async_computation.3 | async-start | bytes 2129920 | tf_op jit(solution)/shard_map/all_to_all | solution.py:115
Sparse Core Ops, SparseCore 0:
  9.1 43.8 all-gather.2
  54.7 38.7 all-gather.4

commit v11 on v9

--- a/solution.py
+++ b/solution.py
@@ -105,16 +105,15 @@
             [highest.reshape(QUERY_HEADS, draft_tree), totals.reshape(QUERY_HEADS, draft_tree)],
             axis=-1,
         )
-        return jnp.concatenate(
-            [blended.reshape(QUERY_HEADS, draft_tree, HEAD_SIZE), stats[:, None, :]], axis=1
-        )
+        return blended.reshape(QUERY_HEADS, draft_tree, HEAD_SIZE).astype(jnp.bfloat16), stats
 
-    packed = lax.map(cache_part, (query_block, cache_k, value_cache, cache_len))
-    packed = packed.reshape(request_list, row_count, heads_dev, draft_tree + 1, HEAD_SIZE)
-    gathered = lax.all_to_all(packed, "row", 1, 1)
-    block_blend = gathered[:, :, :, :draft_tree, :]
-    block_max = gathered[:, :, :, draft_tree, :draft_tree]
-    block_total = gathered[:, :, :, draft_tree, draft_tree : 2 * draft_tree]
+    blends, stats = lax.map(cache_part, (query_block, cache_k, value_cache, cache_len))
+    blends = blends.reshape(request_list, row_count, heads_dev, draft_tree, HEAD_SIZE)
+    stats = stats.reshape(request_list, row_count, heads_dev, 2 * draft_tree)
+    block_blend = lax.all_to_all(blends, "row", 1, 1).astype(jnp.float32)
+    stats = lax.all_to_all(stats, "row", 1, 1)
+    block_max = stats[..., :draft_tree]
+    block_total = stats[..., draft_tree:]
     allowed = ancestors(parents)[:, None, :, :]
     query_own = query_mine.reshape(request_list, draft_tree, heads_dev, HEAD_SIZE)
     key_own = jnp.broadcast_to(

time: 151 us -> 158 us (1.046)
  blocking collectives: 41.7 us -> 13.1 us
  waiting for transfers between devices: 55.8 us -> 72.8 us
  starting transfers between devices: 17.5 us -> 32.4 us
  matrix products: 5.84 us -> 9.47 us
  local copies, waits for them, and re-layouts: 7.85 us -> 9.75 us
    all_to_all x1 -> x0, blocking collectives: 28.9 us -> none  [shards(): lax.all_to_all(owned, 'row', 0, 0)]
    all_to_all x1 -> x3, waiting for transfers between devices: 3.91 us -> 32.1 us  [the longest x1 20.2 us: shards(): lax.all_to_all(owned, 'row', 0, 0)]
    all_to_all x1 -> x3, starting transfers between devices: 4.9 us -> 17 us  [the longest x1 7.4 us: shards(): lax.all_to_all(owned, 'row', 0, 0)]
    ppermute x1, waiting for transfers between devices: 6.86 us -> 0.01 us  [shards(): pair_theirs = lax.ppermute(pair_mine, 'row', partner)]
    all_to_all x2, waiting for transfers between devices: 13 us -> 9.43 us  [row_gather(): return lax.all_to_all(copies, axis_name, 0, 0)]
    ppermute x1, starting transfers between devices: 0.28 us -> 3.62 us  [shards(): pair_theirs = lax.ppermute(pair_mine, 'row', partner)]
    unnamed x11 -> x15, local copies, waits for them, and re-layouts: 0.34 us -> 3.31 us
    dot_general x1, matrix products: 0.66 us -> 3.04 us  [cache_part(): jnp.einsum('kgtp,pkd->kgtd', weights.astype(jnp.bfloat16), value_row_bloc...]
  transfers between devices with their start and end apart: 6 -> 8, of which waited for: 5 -> 6; matrix products, arithmetic and copies ran while one was open for 11% -> 11% of each run, Pallas kernels for 0% -> 0%
where the time goes in v11:
time: 158 us
  waiting for transfers between devices  72.8 us (46%)
  starting transfers between devices  32.4 us (21%)
  between operations  14.3 us (9%)
  blocking collectives  13.1 us (8%)
  local copies, waits for them, and re-layouts  9.75 us (6%)
  matrix products  9.47 us (6%)
  other arithmetic  5.9 us (4%)
    all_gather x1, waiting for transfers between devices, shards(): lax.all_gather(w_qkv, 'col', axis=1, tiled=True)  29.9 us
    all_to_all x1, waiting for transfers between devices, shards(): lax.all_to_all(owned, 'row', 0, 0)  20.2 us
    all_to_all x1, blocking collectives, row_reduce(): received = lax.all_to_all(pieces, axis_name, 0, 0)  13.1 us
    all_to_all x2, starting transfers between devices, row_gather(): return lax.all_to_all(copies, axis_name, 0, 0)  11.8 us
    all_to_all x2, waiting for transfers between devices, row_gather(): return lax.all_to_all(copies, axis_name, 0, 0)  9.43 us
    all_to_all x1, waiting for transfers between devices, shards(): block_blend = lax.all_to_all(blends, 'row', 1, 1).astype(jnp.float32)  8.69 us
    all_to_all x1, starting transfers between devices, shards(): lax.all_to_all(owned, 'row', 0, 0)  7.4 us
    all_to_all x1, starting transfers between devices, shards(): block_blend = lax.all_to_all(blends, 'row', 1, 1).astype(jnp.float32)  4.81 us
  transfers between devices with their start and end apart: 8, of which 6 were waited for; matrix products, arithmetic and copies ran while one was open for 11% of the time, Pallas kernels for 0%

profile of v11, /device:TPU:2, one launch (start us, length us, event | category | flops | bytes accessed | tf_op | source)
XLA Modules:
  0.0 157.7 jit_solution(9597442592420979391)
XLA Ops:
  6.5 0.7 all-gather.3.cloned.1.call-update
  7.3 0.7 all-gather.5.cloned.1.call-update
  8.0 0.9 fusion.23
  8.9 0.6 broadcast_in_dim.90
  9.5 7.5 %all-to-all-start = ((f32[16,1,64]{2,1,0:T(1,128)}), f32[16,1,64]{2,1,0:T(1,128)S(1)}, u32[]{:S(2)}, u32[]{:S(2)}) async-start(f32[16,1,64]{2,1,0:T(1,128)} %broadcast_in_dim.90), calls=%async_computation | async-start | bytes 16384 | tf_op jit(solution)/shard_map/all_to_all | solution.py:37
  17.0 0.7 convert_element_type.108
  17.6 5.5 %all-to-all-done = f32[16,1,64]{2,1,0:T(1,128)S(1)} async-done(((f32[16,1,64]{2,1,0:T(1,128)}), f32[16,1,64]{2,1,0:T(1,128)S(1)}, u32[]{:S(2)}, u32[]{:S(2)}) %all-to-all-start) | async-done | bytes 4128 | tf_op jit(solution)/shard_map/all_to_all | solution.py:37
  23.1 29.9 %all-gather.3.cloned.1.call-done = bf16[256,6144]{1,0:T(8,128)(2,1)} async-done(((bf16[256,384]{1,0:T(8,128)(2,1)}), bf16[256,6144]{1,0:T(8,128)(2,1)}) %all-gather.3.cloned.1.call-update) | async-done | bytes 3145744 | tf_op jit(solution)/shard_map/all_gather | solution.py:57
  53.0 2.6 %fusion.29 = f32[64,6144]{1,0:T(8,128)S(1)} fusion(bf16[256,6144]{1,0:T(8,128)(2,1)} %all-gather.3.cloned.1.call-done, bf16[64,256]{1,0:T(8,128)(2,1)} %param.8, f32[256]{0:T(256)S(1)} %convert_element_type.108, f32[64]{0:T(128)S(1)} %add_rsqrt_fusion), kind=kOutput, calls=%fused_computation.49 | convolution fusion | flops 201392128 | bytes 4752640 | tf_op jit(solution)/shard_map/dot_general | solution.py:56
  56.1 1.3 maximum_bitcast_fusion
  57.4 7.4 %all-to-all-start.1 = ((f32[16,64,384]{2,1,0:T(8,128)}), f32[16,64,384]{2,1,0:T(8,128)S(1)}, u32[]{:S(2)}, u32[]{:S(2)}) async-start(f32[16,64,384]{2,1,0:T(8,128)} %maximum_bitcast_fusion), calls=%async_computation.1 | async-start | bytes 3145728 | tf_op jit(solution)/shard_map/all_to_all | solution.py:68
  66.5 20.2 %all-to-all-done.1 = f32[16,64,384]{2,1,0:T(8,128)S(1)} async-done(((f32[16,64,384]{2,1,0:T(8,128)}), f32[16,64,384]{2,1,0:T(8,128)S(1)}, u32[]{:S(2)}, u32[]{:S(2)}) %all-to-all-start.1) | async-done | bytes 1572896 | tf_op jit(solution)/shard_map/all_to_all | solution.py:68
  86.8 3.6 %collective-permute-start = (bf16[64,128]{1,0:T(8,128)(2,1)S(1)}, bf16[64,128]{1,0:T(8,128)(2,1)S(1)}, u32[]{:S(2)}, u32[]{:S(2)}) collective-permute-start(bf16[64,128]{1,0:T(8,128)(2,1)S(1)} %slice.28), channel_id=1, source_target_pairs={{0,16},{16,0},{32,48},{48,32},{64,80},{80,64},{96,112},{112,96},{1... | collective-permute-start | bytes 49160 | tf_op jit(solution)/shard_map/ppermute | solution.py:72
  90.4 0.8 broadcast_in_dim.91
  91.3 4.3 %all-to-all-start.2 = ((bf16[16,64,256]{2,1,0:T(8,128)(2,1)}), bf16[16,64,256]{2,1,0:T(8,128)(2,1)S(1)}, u32[]{:S(2)}, u32[]{:S(2)}) async-start(bf16[16,64,256]{2,1,0:T(8,128)(2,1)} %broadcast_in_dim.91), calls=%async_computation.2 | async-start | bytes 1048576 | tf_op jit(solution)/shard_map/all_to_all | solution.py:37
  95.7 0.9 copy.71
  96.6 0.9 copy.72
  97.5 3.3 %copy.60 = bf16[4096,256]{1,0:T(8,128)(2,1)S(1)} copy(bf16[4096,256]{0,1:T(8,128)(2,1)} %bitcast.81) | data formatting | bytes 4194304 | tf_op jit(solution)/shard_map/dot_general | solution.py:148
  101.0 3.9 %all-to-all-done.2 = bf16[16,64,256]{2,1,0:T(8,128)(2,1)S(1)} async-done(((bf16[16,64,256]{2,1,0:T(8,128)(2,1)}), bf16[16,64,256]{2,1,0:T(8,128)(2,1)S(1)}, u32[]{:S(2)}, u32[]{:S(2)}) %all-to-all-start.2) | async-done | bytes 524320 | tf_op jit(solution)/shard_map/all_to_all | solution.py:37
  105.2 0.9 squeeze.16
  106.2 1.9 %bitcast_reduce_fusion = (f32[8,4,64]{2,1,0:T(4,128)S(1)}, f32[8,64,4,256]{3,1,2,0:T(8,128)S(1)}) fusion(pred[256]{0:T(512)(128)(4,1)S(1)} %add_compare_fusion, bf16[256,8,128,1]{2,1,0,3:T(8,128)(2,1)} %bitcast.88, bf16[64,8,4,128]{3,2,1,0:T(4,128)(2,1)} %squeeze.16), kind=kOutput, calls=%fused_computation.1 | convolution fusion | flops 135788544 | bytes 3154176 | tf_op jit(solution)/shard_map/while/body/eval_jaxpr/tkgd,pkd->kgtp/dot_general | solution.py:88
  108.0 1.3 copy-done
  109.4 0.9 fusion.2
  110.3 0.7 pad_maximum_fusion
  111.0 4.7 %all-to-all-start.4 = ((f32[1,16,2,128]{3,2,0,1:T(2,128)}), f32[1,16,2,128]{3,2,0,1:T(2,128)S(1)}, u32[]{:S(2)}, u32[]{:S(2)}) async-start(f32[1,16,2,128]{3,2,0,1:T(2,128)} %pad_maximum_fusion), calls=%async_computation.4 | async-start | bytes 32768 | tf_op jit(solution)/shard_map/all_to_all | solution.py:114
  115.8 3.0 %convolution_convert_fusion = bf16[8,4,64,128]{3,2,1,0:T(8,128)(2,1)} fusion(f32[8,64,4,256]{3,1,2,0:T(8,128)} %copy-done, f32[8,4,64]{2,1,0:T(4,128)S(1)} %get-tuple-element.37, pred[256]{0:T(512)(128)(4,1)S(1)} %add_compare_fusion, bf16[256,8,128,1]{2,1,0,3:T(8,128)(2,1)S(1)} %bitcast.87), kind=kOutput, calls=%fused_computation.8 | convolution fusion | flops 137101312 | bytes 3154176 | tf_op jit(solution)/shard_map/while/body/eval_jaxpr/kgtp,pkd->kgtd/dot_general | solution.py:98
  118.8 3.2 %all-to-all-done.4 = f32[1,16,2,128]{3,2,0,1:T(2,128)S(1)} async-done(((f32[1,16,2,128]{3,2,0,1:T(2,128)}), f32[1,16,2,128]{3,2,0,1:T(2,128)S(1)}, u32[]{:S(2)}, u32[]{:S(2)}) %all-to-all-start.4) | async-done | bytes 16416 | tf_op jit(solution)/shard_map/all_to_all | solution.py:114
  122.0 4.8 %all-to-all-start.3 = ((bf16[1,16,2,64,128]{4,3,2,0,1:T(8,128)(2,1)}), bf16[1,16,2,64,128]{4,3,2,0,1:T(8,128)(2,1)S(1)}, u32[]{:S(2)}, u32[]{:S(2)}) async-start(bf16[1,16,2,64,128]{4,3,2,0,1:T(8,128)(2,1)} %bitcast.10), calls=%async_computation.3 | async-start | bytes 1048576 | tf_op jit(solution)/shard_map/all_to_all | solution.py:113
  127.0 8.7 %all-to-all-done.3 = bf16[1,16,2,64,128]{4,3,2,0,1:T(8,128)(2,1)S(1)} async-done(((bf16[1,16,2,64,128]{4,3,2,0,1:T(8,128)(2,1)}), bf16[1,16,2,64,128]{4,3,2,0,1:T(8,128)(2,1)S(1)}, u32[]{:S(2)}, u32[]{:S(2)}) %all-to-all-start.3) | async-done | bytes 524320 | tf_op jit(solution)/shard_map/all_to_all | solution.py:113
  136.4 0.8 fusion.4
  137.1 13.1 %all_to_all.31 = bf16[16,64,256]{2,1,0:T(8,128)(2,1)S(1)} all-to-all(bf16[16,64,256]{2,1,0:T(8,128)(2,1)S(1)} %fusion.4), channel_id=1, replica_groups=mesh['row'=16,'col'=16] {'row'}, dimensions={0} | all-to-all | bytes 1048576 | tf_op jit(solution)/shard_map/all_to_all | solution.py:30
  150.2 0.7 reduce_sum.83
  (44 shorter events, 3.0 us)
Async XLA Ops:
  6.5 46.5 %all-gather.3.cloned.1.call-start = ((), (), s32[]{:S(2)}) async-start(), calls=%async_computation.6 | async-start | bytes 3342336 | tf_op jit(solution)/shard_map/all_gather | solution.py:57
  7.3 90.3 %all-gather.5.cloned.1.call-start = ((), (), s32[]{:S(2)}) async-start(), calls=%async_computation.7 | async-start | bytes 2228224 | tf_op jit(solution)/shard_map/all_gather | solution.py:150
  9.5 13.6 %all-to-all-start = ((f32[16,1,64]{2,1,0:T(1,128)}), f32[16,1,64]{2,1,0:T(1,128)S(1)}, u32[]{:S(2)}, u32[]{:S(2)}) async-start(f32[16,1,64]{2,1,0:T(1,128)} %broadcast_in_dim.90), calls=%async_computation | async-start | bytes 16384 | tf_op jit(solution)/shard_map/all_to_all | solution.py:37
  57.4 8.1 %copy-start.4 = (s32[1,64]{1,0:T(1,128)S(1)}, s32[1,64]{1,0:T(1,128)}, u32[]{:S(2)}) copy-start(s32[1,64]{1,0:T(1,128)} %param.15) | copy-start | bytes 772
  57.4 29.3 %all-to-all-start.1 = ((f32[16,64,384]{2,1,0:T(8,128)}), f32[16,64,384]{2,1,0:T(8,128)S(1)}, u32[]{:S(2)}, u32[]{:S(2)}) async-start(f32[16,64,384]{2,1,0:T(8,128)} %maximum_bitcast_fusion), calls=%async_computation.1 | async-start | bytes 3145728 | tf_op jit(solution)/shard_map/all_to_all | solution.py:68
  64.8 30.9 %copy-start.1 = (bf16[1,256,1024]{2,1,0:T(8,128)(2,1)S(1)}, bf16[1,256,1024]{2,1,0:T(8,128)(2,1)}, u32[]{:S(2)}) copy-start(bf16[1,256,1024]{2,1,0:T(8,128)(2,1)} %param.12) | copy-start | bytes 1572868
  66.5 30.1 %copy-start.2 = (bf16[1,256,1024]{2,1,0:T(8,128)(2,1)S(1)}, bf16[1,256,1024]{2,1,0:T(8,128)(2,1)}, u32[]{:S(2)}) copy-start(bf16[1,256,1024]{2,1,0:T(8,128)(2,1)} %param.13) | copy-start | bytes 1572868
  86.8 14.0 %collective-permute-start = (bf16[64,128]{1,0:T(8,128)(2,1)S(1)}, bf16[64,128]{1,0:T(8,128)(2,1)S(1)}, u32[]{:S(2)}, u32[]{:S(2)}) collective-permute-start(bf16[64,128]{1,0:T(8,128)(2,1)S(1)} %slice.28), channel_id=1, source_target_pairs={{0,16},{16,0},{32,48},{48,32},{64,80},{80,64},{96,112},{112,96},{1... | collective-permute-start | bytes 49160 | tf_op jit(solution)/shard_map/ppermute | solution.py:72
  91.3 13.7 %all-to-all-start.2 = ((bf16[16,64,256]{2,1,0:T(8,128)(2,1)}), bf16[16,64,256]{2,1,0:T(8,128)(2,1)S(1)}, u32[]{:S(2)}, u32[]{:S(2)}) async-start(bf16[16,64,256]{2,1,0:T(8,128)(2,1)} %broadcast_in_dim.91), calls=%async_computation.2 | async-start | bytes 1048576 | tf_op jit(solution)/shard_map/all_to_all | solution.py:37
  106.2 9.6 %copy-start.3 = (bf16[32,8,8,128]{3,2,1,0:T(8,128)(2,1)S(1)}, bf16[32,8,8,128]{3,2,1,0:T(8,128)(2,1)}, u32[]{:S(2)}) copy-start(bf16[32,8,8,128]{3,2,1,0:T(8,128)(2,1)} %copy.72) | copy-start | bytes 1572868
  108.0 1.4 copy-start
  111.0 11.0 %all-to-all-start.4 = ((f32[1,16,2,128]{3,2,0,1:T(2,128)}), f32[1,16,2,128]{3,2,0,1:T(2,128)S(1)}, u32[]{:S(2)}, u32[]{:S(2)}) async-start(f32[1,16,2,128]{3,2,0,1:T(2,128)} %pad_maximum_fusion), calls=%async_computation.4 | async-start | bytes 32768 | tf_op jit(solution)/shard_map/all_to_all | solution.py:114
  122.0 13.7 %all-to-all-start.3 = ((bf16[1,16,2,64,128]{4,3,2,0,1:T(8,128)(2,1)}), bf16[1,16,2,64,128]{4,3,2,0,1:T(8,128)(2,1)S(1)}, u32[]{:S(2)}, u32[]{:S(2)}) async-start(bf16[1,16,2,64,128]{4,3,2,0,1:T(8,128)(2,1)} %bitcast.10), calls=%async_computation.3 | async-start | bytes 1048576 | tf_op jit(solution)/shard_map/all_to_all | solution.py:113
Sparse Core Ops, SparseCore 0:
  9.1 43.8 all-gather.2
  54.7 39.0 all-gather.4

commit v12 on v11

v12 whole, which is shorter than its diff:
```python
import jax
import jax.numpy as jnp
from jax import lax
from jax.sharding import PartitionSpec as P

D = 4096
QUERY_HEADS = 32
KEY_VALUE_HEADS = 8
HEAD_SIZE = 128


masked_score = -1e30


def ancestors(parents):
    draft_tree = parents.shape[1]
    slot_ids = jnp.arange(draft_tree, dtype=jnp.int32)
    parent_links = (parents[:, :, None] == slot_ids[None, None, :]).astype(jnp.float32)
    reachable = parent_links + jnp.eye(draft_tree, dtype=jnp.float32)[None]
    for squaring in range(max(1, (draft_tree - 1).bit_length())):
        product = jnp.einsum("rij,rjk->rik", reachable, reachable, precision=lax.Precision.HIGHEST)
        reachable = (product > 0.5).astype(jnp.float32)
    return reachable > 0.5


def row_reduce(partial, axis_name, sent=jnp.float32):
    count = lax.axis_size(axis_name)
    rows, cols = partial.shape
    pieces = partial.reshape(rows, count, cols // count).transpose(1, 0, 2).astype(sent)
    received = lax.all_to_all(pieces, axis_name, 0, 0)
    return jnp.sum(received.astype(jnp.float32), axis=0)


def row_gather(value, axis_name):
    count = lax.axis_size(axis_name)
    copies = jnp.broadcast_to(value[None], (count,) + value.shape)
    return lax.all_to_all(copies, axis_name, 0, 0)


def shards(hidden_in, norm_gain, w_qkv, w_out, cache_k, value_cache, cache_len, parents):
    rows_here = hidden_in.shape[0]
    request_list = cache_k.shape[0]
    token_positions = cache_k.shape[1]
    draft_tree = parents.shape[1]
    head_groups = QUERY_HEADS // KEY_VALUE_HEADS
    row_count = lax.axis_size("row")
    heads_dev = QUERY_HEADS // row_count
    row_index = lax.axis_index("row")
    score_scale = HEAD_SIZE ** (-0.5)
    features = hidden_in.astype(jnp.float32)
    squares = jnp.sum(row_gather(jnp.sum(features * features, axis=1), "row"), axis=0)
    row_scale = lax.rsqrt(squares / D + 1e-05)
    normed = (features * row_scale[:, None] * norm_gain.astype(jnp.float32)[None, :]).astype(
        jnp.bfloat16
    )
    partial_value = jnp.dot(
        normed, lax.all_gather(w_qkv, "col", axis=1, tiled=True), preferred_element_type=jnp.float32
    )
    query_cols = QUERY_HEADS * HEAD_SIZE
    query_part = partial_value[:, :query_cols].reshape(rows_here, row_count, -1)
    pair_part = (
        partial_value[:, query_cols:]
        .reshape(rows_here, 2, KEY_VALUE_HEADS, HEAD_SIZE)
        .transpose(0, 2, 1, 3)
        .reshape(rows_here, row_count, -1)
    )
    owned = jnp.concatenate([query_part, pair_part], axis=2).transpose(1, 0, 2)
    summed = jnp.sum(lax.all_to_all(owned, "row", 0, 0), axis=0).astype(jnp.bfloat16)
    query_mine = summed[:, : heads_dev * HEAD_SIZE]
    pair_mine = summed[:, heads_dev * HEAD_SIZE :]
    partner = [(i, i ^ 1) for i in range(row_count)]
    pair_theirs = lax.ppermute(pair_mine, "row", partner)
    is_key = row_index % 2 == 0
    key_mine = jnp.where(is_key, pair_mine, pair_theirs)
    value_mine = jnp.where(is_key, pair_theirs, pair_mine)
    def by_head(cache):
        local = cache.reshape(token_positions, KEY_VALUE_HEADS, HEAD_SIZE).transpose(1, 0, 2)
        pieces = jnp.repeat(local, row_count // KEY_VALUE_HEADS, axis=0)
        return lax.all_to_all(pieces, "row", 0, 0).reshape(row_count * token_positions, HEAD_SIZE)

    keys = by_head(cache_k[0])
    values = by_head(value_cache[0])
    window = row_count * token_positions
    query_own = query_mine.reshape(draft_tree, heads_dev, HEAD_SIZE)
    scores = (
        jnp.einsum("thd,pd->htp", query_own, keys, preferred_element_type=jnp.float32)
        * score_scale
    )
    visible = (jnp.arange(window, dtype=jnp.int32) < cache_len[0])[None, None, :]
    scores = jnp.where(visible, scores, masked_score)
    allowed = ancestors(parents)[0][None, :, :]
    tree_scores = (
        jnp.einsum("thd,sd->hts", query_own, key_mine, preferred_element_type=jnp.float32)
        * score_scale
    )
    tree_scores = jnp.where(allowed, tree_scores, masked_score)
    highest = jnp.maximum(jnp.max(scores, axis=-1), jnp.max(tree_scores, axis=-1))
    weights = jnp.where(visible, jnp.exp(scores - highest[..., None]), 0.0)
    tree_weights = jnp.where(allowed, jnp.exp(tree_scores - highest[..., None]), 0.0)
    totals = jnp.sum(weights, axis=-1) + jnp.sum(tree_weights, axis=-1)
    blended = jnp.einsum(
        "htp,pd->htd", weights.astype(jnp.bfloat16), values, preferred_element_type=jnp.float32
    ) + jnp.einsum(
        "hts,sd->htd", tree_weights.astype(jnp.bfloat16), value_mine, preferred_element_type=jnp.float32
    )
    attended = (blended / totals[..., None]).astype(jnp.bfloat16)
    attended = attended.transpose(1, 0, 2).reshape(rows_here, heads_dev * HEAD_SIZE)
    partial_out = jnp.dot(
        attended,
        lax.all_gather(w_out, "col", axis=1, tiled=True),
        preferred_element_type=jnp.float32,
    )
    return row_reduce(partial_out, "row", jnp.bfloat16).astype(jnp.bfloat16)


def solution(mesh):
    placed = (
        P("col", "row"),
        P("row"),
        P("row", "col"),
        P("row", "col"),
        P("col", "row", None),
        P("col", "row", None),
        P("col"),
        P("col", None),
    )
    return jax.shard_map(
        shards, mesh=mesh, in_specs=placed, out_specs=P("col", "row"), check_vma=False
    )
```

time: 158 us -> 137 us (0.87)
  waiting for transfers between devices: 72.8 us -> 59.2 us
  starting transfers between devices: 32.4 us -> 27.8 us
  matrix products: 9.47 us -> 7.46 us
    all_to_all x2, waiting for transfers between devices: 11.9 us -> 3.02 us  [by_head(): lax.all_to_all(pieces, 'row', 0, 0)]
    ppermute x1, waiting for transfers between devices: 0.01 us -> 6.19 us  [shards(): pair_theirs = lax.ppermute(pair_mine, 'row', partner)]
    all_gather x1, waiting for transfers between devices: 29.9 us -> 23.7 us  [shards(): lax.all_gather(w_qkv, 'col', axis=1, tiled=True)]
    all_to_all x2 -> x1, waiting for transfers between devices: 9.43 us -> 4.9 us  [row_gather(): return lax.all_to_all(copies, axis_name, 0, 0)]
    all_to_all x2 -> x1, starting transfers between devices: 11.8 us -> 7.48 us  [row_gather(): return lax.all_to_all(copies, axis_name, 0, 0)]
    ppermute x1, starting transfers between devices: 3.62 us -> 0.37 us  [shards(): pair_theirs = lax.ppermute(pair_mine, 'row', partner)]
    all_to_all x2, starting transfers between devices: 9.55 us -> 12.5 us  [by_head(): lax.all_to_all(pieces, 'row', 0, 0)]
    broadcast_in_dim x0 -> x2, local copies, waits for them, and re-layouts: none -> 2.59 us  [by_head(): pieces = jnp.repeat(local, row_count // KEY_VALUE_HEADS, axis=0)]
  transfers between devices with their start and end apart: 8 -> 7, of which waited for: 6 -> 5; matrix products, arithmetic and copies ran while one was open for 11% -> 12% of each run, Pallas kernels for 0% -> 0%
where the time goes in v12:
time: 137 us; the launch traced here: 136 us
  waiting for transfers between devices  59.2 us (43%)
  starting transfers between devices  27.8 us (20%)
  between operations  14.3 us (10%)
  blocking collectives  13.9 us (10%)
  local copies, waits for them, and re-layouts  8.53 us (6%)
  matrix products  7.46 us (5%)
  other arithmetic  5.08 us (4%)
    all_gather x1, waiting for transfers between devices, shards(): lax.all_gather(w_qkv, 'col', axis=1, tiled=True)  23.7 us
    all_to_all x1, waiting for transfers between devices, shards(): lax.all_to_all(owned, 'row', 0, 0)  19.9 us
    all_to_all x1, blocking collectives, row_reduce(): received = lax.all_to_all(pieces, axis_name, 0, 0)  13.9 us
    all_to_all x2, starting transfers between devices, by_head(): lax.all_to_all(pieces, 'row', 0, 0)  12.5 us
    all_to_all x1, starting transfers between devices, row_gather(): return lax.all_to_all(copies, axis_name, 0, 0)  7.48 us
    all_to_all x1, starting transfers between devices, shards(): lax.all_to_all(owned, 'row', 0, 0)  7.4 us
    ppermute x1, waiting for transfers between devices, shards(): pair_theirs = lax.ppermute(pair_mine, 'row', partner)  6.19 us
    all_to_all x1, waiting for transfers between devices, row_gather(): return lax.all_to_all(copies, axis_name, 0, 0)  4.9 us
  transfers between devices with their start and end apart: 7, of which 5 were waited for; matrix products, arithmetic and copies ran while one was open for 12% of the time, Pallas kernels for 0%

profile of v12, /device:TPU:2, one launch (start us, length us, event | category | flops | bytes accessed | tf_op | source)
XLA Modules:
  0.0 136.2 jit_solution(3213104212025937896)
XLA Ops:
  6.5 0.7 all-gather.3.cloned.1.call-update
  7.3 0.7 all-gather.5.cloned.1.call-update
  8.0 0.9 fusion.17
  8.9 0.6 broadcast_in_dim.61
  9.5 7.5 %all-to-all-start = ((f32[16,1,64]{2,1,0:T(1,128)}), f32[16,1,64]{2,1,0:T(1,128)S(1)}, u32[]{:S(2)}, u32[]{:S(2)}) async-start(f32[16,1,64]{2,1,0:T(1,128)} %broadcast_in_dim.61), calls=%async_computation | async-start | bytes 16384 | tf_op jit(solution)/shard_map/all_to_all | solution.py:37
  17.0 1.1 copy.59
  18.2 4.9 %all-to-all-done = f32[16,1,64]{2,1,0:T(1,128)S(1)} async-done(((f32[16,1,64]{2,1,0:T(1,128)}), f32[16,1,64]{2,1,0:T(1,128)S(1)}, u32[]{:S(2)}, u32[]{:S(2)}) %all-to-all-start) | async-done | bytes 4128 | tf_op jit(solution)/shard_map/all_to_all | solution.py:37
  23.1 1.2 broadcast_in_dim.62
  24.3 4.9 %all-to-all-start.2 = ((bf16[16,256,128]{2,1,0:T(8,128)(2,1)}), bf16[16,256,128]{2,1,0:T(8,128)(2,1)S(1)}, u32[]{:S(2)}, u32[]{:S(2)}) async-start(bf16[16,256,128]{2,1,0:T(8,128)(2,1)} %bitcast.6), calls=%async_computation.2 | async-start | bytes 2097152 | tf_op jit(solution)/shard_map/all_to_all | solution.py:79
  29.3 23.7 %all-gather.3.cloned.1.call-done = bf16[256,6144]{1,0:T(8,128)(2,1)} async-done(((bf16[256,384]{1,0:T(8,128)(2,1)}), bf16[256,6144]{1,0:T(8,128)(2,1)}) %all-gather.3.cloned.1.call-update) | async-done | bytes 3145744 | tf_op jit(solution)/shard_map/all_gather | solution.py:57
  53.0 2.6 %fusion.23 = f32[64,6144]{1,0:T(8,128)S(1)} fusion(bf16[256,6144]{1,0:T(8,128)(2,1)} %all-gather.3.cloned.1.call-done, bf16[64,256]{1,0:T(8,128)(2,1)S(1)} %copy-done.3, f32[256]{0:T(256)S(1)} %convert_element_type.87, f32[64]{0:T(128)S(1)} %add_rsqrt_fusion), kind=kOutput, calls=%fused_computation.40 | convolution fusion | flops 201392128 | bytes 4752640 | tf_op jit(solution)/shard_map/dot_general | solution.py:56
  55.9 0.2 copy.45
  56.1 1.3 maximum_bitcast_fusion
  57.4 7.4 %all-to-all-start.1 = ((f32[16,64,384]{2,1,0:T(8,128)}), f32[16,64,384]{2,1,0:T(8,128)S(1)}, u32[]{:S(2)}, u32[]{:S(2)}) async-start(f32[16,64,384]{2,1,0:T(8,128)} %maximum_bitcast_fusion), calls=%async_computation.1 | async-start | bytes 3145728 | tf_op jit(solution)/shard_map/all_to_all | solution.py:68
  64.9 0.2 convolution_compare_fusion.5
  65.7 0.1 fusion.11
  66.8 19.9 %all-to-all-done.1 = f32[16,64,384]{2,1,0:T(8,128)S(1)} async-done(((f32[16,64,384]{2,1,0:T(8,128)}), f32[16,64,384]{2,1,0:T(8,128)S(1)}, u32[]{:S(2)}, u32[]{:S(2)}) %all-to-all-start.1) | async-done | bytes 1572896 | tf_op jit(solution)/shard_map/all_to_all | solution.py:68
  86.7 1.4 %broadcast_in_dim.67 = bf16[8,2,256,128]{3,2,1,0:T(8,128)(2,1)} broadcast(bf16[8,256,128]{2,1,0:T(8,128)(2,1)S(1)} %copy.51), dimensions={0,2,3} | broadcast | bytes 1572864 | tf_op jit(solution)/shard_map/broadcast_in_dim | solution.py:78
  88.1 7.6 %all-to-all-start.3 = ((bf16[16,256,128]{2,1,0:T(8,128)(2,1)}), bf16[16,256,128]{2,1,0:T(8,128)(2,1)}, u32[]{:S(2)}, u32[]{:S(2)}) async-start(bf16[16,256,128]{2,1,0:T(8,128)(2,1)} %bitcast.97), calls=%async_computation.3 | async-start | bytes 2097152 | tf_op jit(solution)/shard_map/all_to_all | solution.py:79
  95.7 3.3 %copy.54 = bf16[4096,256]{1,0:T(8,128)(2,1)S(1)} copy(bf16[4096,256]{0,1:T(8,128)(2,1)} %bitcast.99) | data formatting | bytes 4194304 | tf_op jit(solution)/shard_map/dot_general | solution.py:108
  99.0 1.5 %reduce_sum.59 = bf16[64,384]{1,0:T(8,128)(2,1)S(1)} reduce(f32[16,64,384]{2,1,0:T(8,128)} %copy-done.1, f32[]{:T(128)} %constant.11.clone.1), dimensions={0}, to_apply=%region_2.0 | reduce | flops 368640 | bytes 1622020 | tf_op jit(solution)/shard_map/reduce_sum | solution.py:68
  100.5 0.4 collective-permute-start
  100.9 0.5 fusion.45
  101.4 6.2 %collective-permute-done = bf16[64,128]{1,0:T(8,128)(2,1)S(1)} collective-permute-done((bf16[64,128]{1,0:T(8,128)(2,1)S(1)}, bf16[64,128]{1,0:T(8,128)(2,1)S(1)}, u32[]{:S(2)}, u32[]{:S(2)}) %collective-permute-start) | collective-permute-done | bytes 16416 | tf_op jit(solution)/shard_map/ppermute | solution.py:72
  107.6 0.2 fusion.46
  107.8 0.5 fusion.2
  108.4 3.0 %all-to-all-done.3 = bf16[16,256,128]{2,1,0:T(8,128)(2,1)} async-done(((bf16[16,256,128]{2,1,0:T(8,128)(2,1)}), bf16[16,256,128]{2,1,0:T(8,128)(2,1)}, u32[]{:S(2)}, u32[]{:S(2)}) %all-to-all-start.3) | async-done | bytes 1048608 | tf_op jit(solution)/shard_map/all_to_all | solution.py:79
  111.4 2.4 %fusion.12 = f32[2,64,128]{2,1,0:T(8,128)S(1)} fusion(bf16[4096,128,1]{1,0,2:T(8,128)(2,1)} %bitcast.17, f32[2,64,4096]{2,1,0:T(8,128)} %copy-done, f32[2,64]{1,0:T(2,128)S(1)} %max.7, pred[4096]{0:T(1024)(128)(4,1)S(1)} %iota_compare_fusion), kind=kOutput, calls=%fused_computation.24 | convolution fusion | flops 135790592 | bytes 3215872 | tf_op jit(solution)/shard_map/htp,pd->htd/dot_general | solution.py:101
  113.8 0.2 fusion.9
  114.1 0.8 fusion.4
  114.8 13.9 %all_to_all.26 = bf16[16,64,256]{2,1,0:T(8,128)(2,1)S(1)} all-to-all(bf16[16,64,256]{2,1,0:T(8,128)(2,1)S(1)} %fusion.4), channel_id=1, replica_groups=mesh['row'=16,'col'=16] {'row'}, dimensions={0} | all-to-all | bytes 1048576 | tf_op jit(solution)/shard_map/all_to_all | solution.py:30
  128.7 0.7 reduce_sum.62
  (39 shorter events, 1.6 us)
Async XLA Ops:
  6.5 46.5 %all-gather.3.cloned.1.call-start = ((), (), s32[]{:S(2)}) async-start(), calls=%async_computation.5 | async-start | bytes 3342336 | tf_op jit(solution)/shard_map/all_gather | solution.py:57
  7.3 88.4 %all-gather.5.cloned.1.call-start = ((), (), s32[]{:S(2)}) async-start(), calls=%async_computation.6 | async-start | bytes 2228224 | tf_op jit(solution)/shard_map/all_gather | solution.py:110
  9.5 13.6 %all-to-all-start = ((f32[16,1,64]{2,1,0:T(1,128)}), f32[16,1,64]{2,1,0:T(1,128)S(1)}, u32[]{:S(2)}, u32[]{:S(2)}) async-start(f32[16,1,64]{2,1,0:T(1,128)} %broadcast_in_dim.61), calls=%async_computation | async-start | bytes 16384 | tf_op jit(solution)/shard_map/all_to_all | solution.py:37
  18.2 11.1 %copy-start.5 = (bf16[256]{0:T(256)(128)(2,1)S(1)}, bf16[256]{0:T(256)(128)(2,1)}, u32[]{:S(2)}) copy-start(bf16[256]{0:T(256)(128)(2,1)} %param.9) | copy-start | bytes 1540
  18.2 34.8 %copy-start.3 = (bf16[64,256]{1,0:T(8,128)(2,1)S(1)}, bf16[64,256]{1,0:T(8,128)(2,1)}, u32[]{:S(2)}) copy-start(bf16[64,256]{1,0:T(8,128)(2,1)} %param.8) | copy-start | bytes 98308
  24.3 33.1 %all-to-all-start.2 = ((bf16[16,256,128]{2,1,0:T(8,128)(2,1)}), bf16[16,256,128]{2,1,0:T(8,128)(2,1)S(1)}, u32[]{:S(2)}, u32[]{:S(2)}) async-start(bf16[16,256,128]{2,1,0:T(8,128)(2,1)} %bitcast.6), calls=%async_computation.2 | async-start | bytes 2097152 | tf_op jit(solution)/shard_map/all_to_all | solution.py:79
  57.4 7.4 %copy-start.4 = (s32[1,64]{1,0:T(1,128)S(1)}, s32[1,64]{1,0:T(1,128)}, u32[]{:S(2)}) copy-start(s32[1,64]{1,0:T(1,128)} %param.15) | copy-start | bytes 772
  57.4 9.2 %copy-start.2 = (bf16[1,256,1024]{2,1,0:T(8,128)(2,1)S(1)}, bf16[1,256,1024]{2,1,0:T(8,128)(2,1)}, u32[]{:S(2)}) copy-start(bf16[1,256,1024]{2,1,0:T(8,128)(2,1)} %param.13) | copy-start | bytes 1572868
  57.4 29.3 %all-to-all-start.1 = ((f32[16,64,384]{2,1,0:T(8,128)}), f32[16,64,384]{2,1,0:T(8,128)S(1)}, u32[]{:S(2)}, u32[]{:S(2)}) async-start(f32[16,64,384]{2,1,0:T(8,128)} %maximum_bitcast_fusion), calls=%async_computation.1 | async-start | bytes 3145728 | tf_op jit(solution)/shard_map/all_to_all | solution.py:68
  86.7 9.0 %copy-start.1 = (f32[16,64,384]{2,1,0:T(8,128)}, f32[16,64,384]{2,1,0:T(8,128)S(1)}, u32[]{:S(2)}) copy-start(f32[16,64,384]{2,1,0:T(8,128)S(1)} %all-to-all-done.1) | copy-start | bytes 4718596
  88.1 23.3 %all-to-all-start.3 = ((bf16[16,256,128]{2,1,0:T(8,128)(2,1)}), bf16[16,256,128]{2,1,0:T(8,128)(2,1)}, u32[]{:S(2)}, u32[]{:S(2)}) async-start(bf16[16,256,128]{2,1,0:T(8,128)(2,1)} %bitcast.97), calls=%async_computation.3 | async-start | bytes 2097152 | tf_op jit(solution)/shard_map/all_to_all | solution.py:79
  100.5 7.1 %collective-permute-start = (bf16[64,128]{1,0:T(8,128)(2,1)S(1)}, bf16[64,128]{1,0:T(8,128)(2,1)S(1)}, u32[]{:S(2)}, u32[]{:S(2)}) collective-permute-start(bf16[64,128]{1,0:T(8,128)(2,1)S(1)} %slice.19), channel_id=1, source_target_pairs={{0,16},{16,0},{32,48},{48,32},{64,80},{80,64},{96,112},{112,96},{1... | collective-permute-start | bytes 49160 | tf_op jit(solution)/shard_map/ppermute | solution.py:72
  101.4 6.4 %copy-start = (f32[2,64,4096]{2,1,0:T(8,128)}, f32[2,64,4096]{2,1,0:T(8,128)S(1)}, u32[]{:S(2)}) copy-start(f32[2,64,4096]{2,1,0:T(8,128)S(1)} %get-tuple-element.6) | copy-start | bytes 6291460
Sparse Core Ops, SparseCore 0:
  9.1 43.8 all-gather.2
  54.7 38.8 all-gather.4

commit v13 on v12

--- a/solution.py
+++ b/solution.py
@@ -56,6 +56,14 @@
     partial_value = jnp.dot(
         normed, lax.all_gather(w_qkv, "col", axis=1, tiled=True), preferred_element_type=jnp.float32
     )
+    local = jnp.stack([cache_k[0], value_cache[0]]).reshape(
+        2, token_positions, KEY_VALUE_HEADS, HEAD_SIZE
+    ).transpose(2, 0, 1, 3)
+    pieces = jnp.repeat(local, row_count // KEY_VALUE_HEADS, axis=0)
+    by_head = lax.all_to_all(pieces, "row", 0, 0)
+    by_head, partial_value = lax.optimization_barrier((by_head, partial_value))
+    keys = by_head[:, 0].reshape(row_count * token_positions, HEAD_SIZE)
+    values = by_head[:, 1].reshape(row_count * token_positions, HEAD_SIZE)
     query_cols = QUERY_HEADS * HEAD_SIZE
     query_part = partial_value[:, :query_cols].reshape(rows_here, row_count, -1)
     pair_part = (
@@ -73,13 +81,6 @@
     is_key = row_index % 2 == 0
     key_mine = jnp.where(is_key, pair_mine, pair_theirs)
     value_mine = jnp.where(is_key, pair_theirs, pair_mine)
-    def by_head(cache):
-        local = cache.reshape(token_positions, KEY_VALUE_HEADS, HEAD_SIZE).transpose(1, 0, 2)
-        pieces = jnp.repeat(local, row_count // KEY_VALUE_HEADS, axis=0)
-        return lax.all_to_all(pieces, "row", 0, 0).reshape(row_count * token_positions, HEAD_SIZE)
-
-    keys = by_head(cache_k[0])
-    values = by_head(value_cache[0])
     window = row_count * token_positions
     query_own = query_mine.reshape(draft_tree, heads_dev, HEAD_SIZE)
     scores = (

time: 137 us -> 132 us (0.964)
  starting transfers between devices: 27.8 us -> 20.6 us
  waiting for transfers between devices: 59.2 us -> 55 us
  local copies, waits for them, and re-layouts: 8.53 us -> 11.9 us
  blocking collectives: 13.9 us -> 16.5 us
    all_gather x1, waiting for transfers between devices: 0.02 us -> 23.7 us  [shards(): lax.all_gather(w_out, 'col', axis=1, tiled=True)]
    all_to_all x1, waiting for transfers between devices: 19.9 us -> 0.01 us  [shards(): lax.all_to_all(owned, 'row', 0, 0)]
    all_to_all x2 -> x1, starting transfers between devices: 12.5 us -> 5.1 us  [shards(): by_head = lax.all_to_all(pieces, 'row', 0, 0)]
    ppermute x1, waiting for transfers between devices: 6.19 us -> 2.72 us  [shards(): pair_theirs = lax.ppermute(pair_mine, 'row', partner)]
    all_to_all x2 -> x1, waiting for transfers between devices: 3.02 us -> 0.01 us  [shards(): by_head = lax.all_to_all(pieces, 'row', 0, 0)]
    all_to_all x1, blocking collectives: 13.9 us -> 16.5 us  [row_reduce(): received = lax.all_to_all(pieces, axis_name, 0, 0)]
    dot_general x1, matrix products: 2.38 us -> 0.54 us  [shards(): jnp.einsum('htp,pd->htd', weights.astype(jnp.bfloat16), values, preferred...]
  transfers between devices with their start and end apart: 7 -> 6, of which waited for: 5 -> 4; matrix products, arithmetic and copies ran while one was open for 12% -> 13% of each run, Pallas kernels for 0% -> 0%
where the time goes in v13:
time: 132 us; the launch traced here: 131 us
  waiting for transfers between devices  55 us (42%)
  starting transfers between devices  20.6 us (16%)
  blocking collectives  16.5 us (12%)
  between operations  14.2 us (11%)
  local copies, waits for them, and re-layouts  11.9 us (9%)
  matrix products  6.86 us (5%)
  other arithmetic  6.37 us (5%)
    all_gather x1, waiting for transfers between devices, shards(): lax.all_gather(w_out, 'col', axis=1, tiled=True)  23.7 us
    all_gather x1, waiting for transfers between devices, shards(): lax.all_gather(w_qkv, 'col', axis=1, tiled=True)  23.6 us
    all_to_all x1, blocking collectives, row_reduce(): received = lax.all_to_all(pieces, axis_name, 0, 0)  16.5 us
    all_to_all x1, starting transfers between devices, row_gather(): return lax.all_to_all(copies, axis_name, 0, 0)  7.48 us
    all_to_all x1, starting transfers between devices, shards(): lax.all_to_all(owned, 'row', 0, 0)  7.4 us
    all_to_all x1, starting transfers between devices, shards(): by_head = lax.all_to_all(pieces, 'row', 0, 0)  5.1 us
    dot_general x1, local copies, waits for them, and re-layouts, shards(): jnp.dot(attended, lax.all_gather(w_out, 'col', axis=1, tiled=True), prefe...  4.09 us
    dot_general x1, matrix products, shards(): jnp.dot(normed, lax.all_gather(w_qkv, 'col', axis=1, tiled=True), preferr...  3.83 us
  transfers between devices with their start and end apart: 6, of which 4 were waited for; matrix products, arithmetic and copies ran while one was open for 13% of the time, Pallas kernels for 0%

profile of v13, /device:TPU:2, one launch (start us, length us, event | category | flops | bytes accessed | tf_op | source)
XLA Modules:
  0.0 131.5 jit_solution(10864486979364258592)
XLA Ops:
  6.5 0.7 all-gather.3.cloned.1.call-update
  7.3 0.9 fusion.17
  8.1 0.6 broadcast_in_dim.59
  8.7 7.5 %all-to-all-start.1 = ((f32[16,1,64]{2,1,0:T(1,128)}), f32[16,1,64]{2,1,0:T(1,128)S(1)}, u32[]{:S(2)}, u32[]{:S(2)}) async-start(f32[16,1,64]{2,1,0:T(1,128)} %broadcast_in_dim.59), calls=%async_computation.1 | async-start | bytes 16384 | tf_op jit(solution)/shard_map/all_to_all | solution.py:37
  16.3 0.7 all-gather.5.cloned.1.call-update
  17.0 1.3 pad_maximum_fusion
  18.3 0.3 copy.53
  18.6 0.2 copy.40
  18.8 3.5 %all-to-all-done.1 = f32[16,1,64]{2,1,0:T(1,128)S(1)} async-done(((f32[16,1,64]{2,1,0:T(1,128)}), f32[16,1,64]{2,1,0:T(1,128)S(1)}, u32[]{:S(2)}, u32[]{:S(2)}) %all-to-all-start.1) | async-done | bytes 4128 | tf_op jit(solution)/shard_map/all_to_all | solution.py:37
  22.4 1.8 %broadcast_in_dim.58 = bf16[8,2,2,256,128]{4,3,2,1,0:T(8,128)(2,1)} broadcast(bf16[8,2,256,128]{3,2,1,0:T(8,128)(2,1)S(1)} %copy.40), dimensions={0,2,3,4} | broadcast | bytes 3145728 | tf_op jit(solution)/shard_map/broadcast_in_dim | solution.py:62
  24.2 5.1 %all-to-all-start = ((bf16[16,2,256,128]{3,2,1,0:T(8,128)(2,1)}), bf16[16,2,256,128]{3,2,1,0:T(8,128)(2,1)S(1)}, u32[]{:S(2)}, u32[]{:S(2)}) async-start(bf16[16,2,256,128]{3,2,1,0:T(8,128)(2,1)} %bitcast.92), calls=%async_computation | async-start | bytes 4194304 | tf_op jit(solution)/shard_map/all_to_all | solution.py:63
  29.4 23.6 %all-gather.3.cloned.1.call-done = bf16[256,6144]{1,0:T(8,128)(2,1)} async-done(((bf16[256,384]{1,0:T(8,128)(2,1)}), bf16[256,6144]{1,0:T(8,128)(2,1)}) %all-gather.3.cloned.1.call-update) | async-done | bytes 3145744 | tf_op jit(solution)/shard_map/all_gather | solution.py:57
  53.0 3.8 %fusion.23 = f32[64,6144]{1,0:T(8,128)} fusion(bf16[256,6144]{1,0:T(8,128)(2,1)} %all-gather.3.cloned.1.call-done, bf16[64,256]{1,0:T(8,128)(2,1)S(1)} %copy-done.3, f32[256]{0:T(256)S(1)} %convert_element_type.87, f32[64]{0:T(128)S(1)} %add_rsqrt_fusion), kind=kOutput, calls=%fused_computation.42 | convolution fusion | flops 201392128 | bytes 4752640 | tf_op jit(solution)/shard_map/dot_general | solution.py:56
  56.8 1.4 %copy-done.1 = f32[64,6144]{1,0:T(8,128)S(1)} copy-done((f32[64,6144]{1,0:T(8,128)S(1)}, f32[64,6144]{1,0:T(8,128)}, u32[]{:S(2)}) %copy-start.1) | copy-done | bytes 1572888
  58.6 0.9 slice-done
  59.6 1.3 maximum_bitcast_fusion
  60.9 7.4 %all-to-all-start.2 = ((f32[16,64,384]{2,1,0:T(8,128)}), f32[16,64,384]{2,1,0:T(8,128)}, u32[]{:S(2)}, u32[]{:S(2)}) async-start(f32[16,64,384]{2,1,0:T(8,128)} %maximum_bitcast_fusion), calls=%async_computation.2 | async-start | bytes 3145728 | tf_op jit(solution)/shard_map/all_to_all | solution.py:76
  70.0 23.7 %all-gather.5.cloned.1.call-done = bf16[256,4096]{1,0:T(8,128)(2,1)} async-done(((bf16[256,256]{1,0:T(8,128)(2,1)}), bf16[256,4096]{1,0:T(8,128)(2,1)}) %all-gather.5.cloned.1.call-update) | async-done | bytes 2097168 | tf_op jit(solution)/shard_map/all_gather | solution.py:111
  93.7 4.1 %copy.49 = bf16[4096,256]{1,0:T(8,128)(2,1)} copy(bf16[4096,256]{0,1:T(8,128)(2,1)} %bitcast.98) | data formatting | bytes 4194304 | tf_op jit(solution)/shard_map/dot_general | solution.py:109
  97.8 1.2 fusion.45
  99.0 1.5 %reduce_sum.59 = bf16[64,384]{1,0:T(8,128)(2,1)S(1)} reduce(f32[16,64,384]{2,1,0:T(8,128)} %all-to-all-done.2, f32[]{:T(128)} %constant.11.clone.1), dimensions={0}, to_apply=%region_2.0 | reduce | flops 368640 | bytes 1622020 | tf_op jit(solution)/shard_map/reduce_sum | solution.py:76
  100.5 0.6 collective-permute-start
  101.1 0.5 fusion.46
  101.6 2.7 %collective-permute-done = bf16[64,128]{1,0:T(8,128)(2,1)S(1)} collective-permute-done((bf16[64,128]{1,0:T(8,128)(2,1)S(1)}, bf16[64,128]{1,0:T(8,128)(2,1)S(1)}, u32[]{:S(2)}, u32[]{:S(2)}) %collective-permute-start) | collective-permute-done | bytes 16416 | tf_op jit(solution)/shard_map/ppermute | solution.py:80
  104.3 0.2 fusion.47
  104.5 0.5 fusion.2
  105.1 0.5 fusion.12
  105.7 0.2 fusion.9
  105.9 0.7 copy-done
  106.7 0.7 fusion.4
  107.4 16.5 %all_to_all.21 = bf16[16,64,256]{2,1,0:T(8,128)(2,1)S(1)} all-to-all(bf16[16,64,256]{2,1,0:T(8,128)(2,1)S(1)} %fusion.4), channel_id=1, replica_groups=mesh['row'=16,'col'=16] {'row'}, dimensions={0} | all-to-all | bytes 1048576 | tf_op jit(solution)/shard_map/all_to_all | solution.py:30
  124.0 0.7 reduce_sum.62
  (38 shorter events, 1.8 us)
Async XLA Ops:
  6.5 46.5 %all-gather.3.cloned.1.call-start = ((), (), s32[]{:S(2)}) async-start(), calls=%async_computation.4 | async-start | bytes 3342336 | tf_op jit(solution)/shard_map/all_gather | solution.py:57
  8.7 13.6 %all-to-all-start.1 = ((f32[16,1,64]{2,1,0:T(1,128)}), f32[16,1,64]{2,1,0:T(1,128)S(1)}, u32[]{:S(2)}, u32[]{:S(2)}) async-start(f32[16,1,64]{2,1,0:T(1,128)} %broadcast_in_dim.59), calls=%async_computation.1 | async-start | bytes 16384 | tf_op jit(solution)/shard_map/all_to_all | solution.py:37
  16.2 77.5 %all-gather.5.cloned.1.call-start = ((), (), s32[]{:S(2)}) async-start(), calls=%async_computation.5 | async-start | bytes 2228224 | tf_op jit(solution)/shard_map/all_gather | solution.py:111
  24.2 5.1 %copy-start.5 = (bf16[256]{0:T(256)(128)(2,1)S(1)}, bf16[256]{0:T(256)(128)(2,1)}, u32[]{:S(2)}) copy-start(bf16[256]{0:T(256)(128)(2,1)} %param.9) | copy-start | bytes 1540
  24.2 28.8 %copy-start.3 = (bf16[64,256]{1,0:T(8,128)(2,1)S(1)}, bf16[64,256]{1,0:T(8,128)(2,1)}, u32[]{:S(2)}) copy-start(bf16[64,256]{1,0:T(8,128)(2,1)} %param.8) | copy-start | bytes 98308
  24.2 32.6 %all-to-all-start = ((bf16[16,2,256,128]{3,2,1,0:T(8,128)(2,1)}), bf16[16,2,256,128]{3,2,1,0:T(8,128)(2,1)S(1)}, u32[]{:S(2)}, u32[]{:S(2)}) async-start(bf16[16,2,256,128]{3,2,1,0:T(8,128)(2,1)} %bitcast.92), calls=%async_computation | async-start | bytes 4194304 | tf_op jit(solution)/shard_map/all_to_all | solution.py:63
  56.8 1.4 %copy-start.1 = (f32[64,6144]{1,0:T(8,128)S(1)}, f32[64,6144]{1,0:T(8,128)}, u32[]{:S(2)}) copy-start(f32[64,6144]{1,0:T(8,128)} %fusion.23) | copy-start | bytes 4718596
  58.2 1.2 slice-start
  60.8 8.1 %copy-start.4 = (s32[1,64]{1,0:T(1,128)S(1)}, s32[1,64]{1,0:T(1,128)}, u32[]{:S(2)}) copy-start(s32[1,64]{1,0:T(1,128)} %param.15) | copy-start | bytes 772
  60.9 38.1 %all-to-all-start.2 = ((f32[16,64,384]{2,1,0:T(8,128)}), f32[16,64,384]{2,1,0:T(8,128)}, u32[]{:S(2)}, u32[]{:S(2)}) async-start(f32[16,64,384]{2,1,0:T(8,128)} %maximum_bitcast_fusion), calls=%async_computation.2 | async-start | bytes 3145728 | tf_op jit(solution)/shard_map/all_to_all | solution.py:76
  100.5 3.8 %collective-permute-start = (bf16[64,128]{1,0:T(8,128)(2,1)S(1)}, bf16[64,128]{1,0:T(8,128)(2,1)S(1)}, u32[]{:S(2)}, u32[]{:S(2)}) collective-permute-start(bf16[64,128]{1,0:T(8,128)(2,1)S(1)} %slice.25), channel_id=1, source_target_pairs={{0,16},{16,0},{32,48},{48,32},{64,80},{80,64},{96,112},{112,96},{1... | collective-permute-start | bytes 49160 | tf_op jit(solution)/shard_map/ppermute | solution.py:80
  101.1 4.0 %copy-start.2 = (bf16[16,1,256,128]{3,2,1,0:T(8,128)(2,1)S(1)}, bf16[16,1,256,128]{3,2,1,0:T(8,128)(2,1)}, u32[]{:S(2)}) copy-start(bf16[16,1,256,128]{3,2,1,0:T(8,128)(2,1)} %get-tuple-element.10) | copy-start | bytes 3145732
  105.1 1.6 %copy-start = (bf16[4096,256]{1,0:T(8,128)(2,1)S(1)}, bf16[4096,256]{1,0:T(8,128)(2,1)}, u32[]{:S(2)}) copy-start(bf16[4096,256]{1,0:T(8,128)(2,1)} %copy.49) | copy-start | bytes 6291460
Sparse Core Ops, SparseCore 0:
  9.1 43.8 all-gather.2
  54.7 38.9 all-gather.4

commit v14 on v13

--- a/solution.py
+++ b/solution.py
@@ -62,6 +62,8 @@
     pieces = jnp.repeat(local, row_count // KEY_VALUE_HEADS, axis=0)
     by_head = lax.all_to_all(pieces, "row", 0, 0)
     by_head, partial_value = lax.optimization_barrier((by_head, partial_value))
+    out_weights = row_gather(w_out, "col").transpose(1, 0, 2).reshape(w_out.shape[0], -1)
+    out_weights, by_head = lax.optimization_barrier((out_weights, by_head))
     keys = by_head[:, 0].reshape(row_count * token_positions, HEAD_SIZE)
     values = by_head[:, 1].reshape(row_count * token_positions, HEAD_SIZE)
     query_cols = QUERY_HEADS * HEAD_SIZE
@@ -108,7 +110,7 @@
     attended = attended.transpose(1, 0, 2).reshape(rows_here, heads_dev * HEAD_SIZE)
     partial_out = jnp.dot(
         attended,
-        lax.all_gather(w_out, "col", axis=1, tiled=True),
+        out_weights,
         preferred_element_type=jnp.float32,
     )
     return row_reduce(partial_out, "row", jnp.bfloat16).astype(jnp.bfloat16)

time: 132 us -> 177 us (1.34)
  waiting for transfers between devices: 55 us -> 94.8 us
  starting transfers between devices: 20.6 us -> 33.2 us
  local copies, waits for them, and re-layouts: 11.9 us -> 8.65 us
  blocking collectives: 16.5 us -> 13.7 us
    all_to_all x1 -> x2, waiting for transfers between devices: 3.54 us -> 49 us  [row_gather(): return lax.all_to_all(copies, axis_name, 0, 0)]
    all_to_all x1, waiting for transfers between devices: 0.01 us -> 26 us  [shards(): by_head = lax.all_to_all(pieces, 'row', 0, 0)]
    all_gather x1 -> x0, waiting for transfers between devices: 23.7 us -> none  [shards(): lax.all_gather(w_out, 'col', axis=1, tiled=True)]
    all_gather x1, waiting for transfers between devices: 23.6 us -> 0.02 us  [shards(): lax.all_gather(w_qkv, 'col', axis=1, tiled=True)]
    all_to_all x1, waiting for transfers between devices: 0.01 us -> 17.8 us  [shards(): lax.all_to_all(owned, 'row', 0, 0)]
    all_to_all x1 -> x2, starting transfers between devices: 7.48 us -> 16 us  [row_gather(): return lax.all_to_all(copies, axis_name, 0, 0)]
    dot_general x1 -> x0, local copies, waits for them, and re-layouts: 4.09 us -> none  [shards(): jnp.dot(attended, lax.all_gather(w_out, 'col', axis=1, tiled=True), prefe...]
    ppermute x1, starting transfers between devices: 0.58 us -> 4.39 us  [shards(): pair_theirs = lax.ppermute(pair_mine, 'row', partner)]
  transfers between devices with their start and end apart: 6 -> 6, of which waited for: 4 -> 5; matrix products, arithmetic and copies ran while one was open for 13% -> 9% of each run, Pallas kernels for 0% -> 0%
where the time goes in v14:
time: 177 us
  waiting for transfers between devices  94.8 us (54%)
  starting transfers between devices  33.2 us (19%)
  between operations  14.3 us (8%)
  blocking collectives  13.7 us (8%)
  local copies, waits for them, and re-layouts  8.65 us (5%)
  other arithmetic  6.38 us (4%)
  matrix products  5.63 us (3%)
    all_to_all x2, waiting for transfers between devices, row_gather(): return lax.all_to_all(copies, axis_name, 0, 0)  49 us
    all_to_all x1, waiting for transfers between devices, shards(): by_head = lax.all_to_all(pieces, 'row', 0, 0)  26 us
    all_to_all x1, waiting for transfers between devices, shards(): lax.all_to_all(owned, 'row', 0, 0)  17.8 us
    all_to_all x2, starting transfers between devices, row_gather(): return lax.all_to_all(copies, axis_name, 0, 0)  16 us
    all_to_all x1, blocking collectives, row_reduce(): received = lax.all_to_all(pieces, axis_name, 0, 0)  13.7 us
    all_to_all x1, starting transfers between devices, shards(): lax.all_to_all(owned, 'row', 0, 0)  7.71 us
    all_to_all x1, starting transfers between devices, shards(): by_head = lax.all_to_all(pieces, 'row', 0, 0)  5.1 us
    ppermute x1, starting transfers between devices, shards(): pair_theirs = lax.ppermute(pair_mine, 'row', partner)  4.39 us
  transfers between devices with their start and end apart: 6, of which 5 were waited for; matrix products, arithmetic and copies ran while one was open for 9% of the time, Pallas kernels for 0%

profile of v14, /device:TPU:2, one launch (start us, length us, event | category | flops | bytes accessed | tf_op | source)
XLA Modules:
  0.0 176.6 jit_solution(17446995758174437676)
XLA Ops:
  6.5 0.7 all-gather.2.cloned.1.call-update
  7.3 0.9 fusion.17
  8.1 0.6 broadcast_in_dim.66
  8.7 7.5 %all-to-all-start.2 = ((f32[16,1,64]{2,1,0:T(1,128)}), f32[16,1,64]{2,1,0:T(1,128)S(1)}, u32[]{:S(2)}, u32[]{:S(2)}) async-start(f32[16,1,64]{2,1,0:T(1,128)} %broadcast_in_dim.66), calls=%async_computation.2 | async-start | bytes 16384 | tf_op jit(solution)/shard_map/all_to_all | solution.py:37
  16.2 1.3 pad_maximum_fusion
  17.5 0.3 copy.53
  17.9 0.2 copy.41
  18.1 4.3 %all-to-all-done.2 = f32[16,1,64]{2,1,0:T(1,128)S(1)} async-done(((f32[16,1,64]{2,1,0:T(1,128)}), f32[16,1,64]{2,1,0:T(1,128)S(1)}, u32[]{:S(2)}, u32[]{:S(2)}) %all-to-all-start.2) | async-done | bytes 4128 | tf_op jit(solution)/shard_map/all_to_all | solution.py:37
  22.4 2.0 %broadcast_in_dim.65 = bf16[8,2,2,256,128]{4,3,2,1,0:T(8,128)(2,1)} broadcast(bf16[8,2,256,128]{3,2,1,0:T(8,128)(2,1)S(1)} %copy.41), dimensions={0,2,3,4} | broadcast | bytes 3145728 | tf_op jit(solution)/shard_map/broadcast_in_dim | solution.py:62
  24.3 5.1 %all-to-all-start.1 = ((bf16[16,2,256,128]{3,2,1,0:T(8,128)(2,1)}), bf16[16,2,256,128]{3,2,1,0:T(8,128)(2,1)S(1)}, u32[]{:S(2)}, u32[]{:S(2)}) async-start(bf16[16,2,256,128]{3,2,1,0:T(8,128)(2,1)} %bitcast.96), calls=%async_computation.1 | async-start | bytes 4194304 | tf_op jit(solution)/shard_map/all_to_all | solution.py:63
  29.6 26.0 %all-to-all-done.1 = bf16[16,2,256,128]{3,2,1,0:T(8,128)(2,1)S(1)} async-done(((bf16[16,2,256,128]{3,2,1,0:T(8,128)(2,1)}), bf16[16,2,256,128]{3,2,1,0:T(8,128)(2,1)S(1)}, u32[]{:S(2)}, u32[]{:S(2)}) %all-to-all-start.1) | async-done | bytes 2097184 | tf_op jit(solution)/shard_map/all_to_all | solution.py:63
  55.5 1.7 broadcast_in_dim.64
  57.2 0.3 copy-done
  57.5 8.6 %all-to-all-start = ((bf16[16,256,256]{1,2,0:T(8,128)(2,1)}), bf16[16,256,256]{1,2,0:T(8,128)(2,1)S(1)}, u32[]{:S(2)}, u32[]{:S(2)}) async-start(bf16[16,256,256]{1,2,0:T(8,128)(2,1)} %broadcast_in_dim.64), calls=%async_computation | async-start | bytes 4194304 | tf_op jit(solution)/shard_map/all_to_all | solution.py:37
  66.2 2.6 %fusion.23 = f32[64,6144]{1,0:T(8,128)S(1)} fusion(bf16[256,6144]{1,0:T(8,128)(2,1)} %all-gather.2.cloned.1.call-done, bf16[64,256]{1,0:T(8,128)(2,1)S(1)} %copy-done.2, f32[256]{0:T(256)S(1)} %convert_element_type.87, f32[64]{0:T(128)S(1)} %add_rsqrt_fusion), kind=kOutput, calls=%fused_computation.42 | convolution fusion | flops 201392128 | bytes 4752640 | tf_op jit(solution)/shard_map/dot_general | solution.py:56
  69.1 0.2 copy.43
  69.3 1.3 maximum_bitcast_fusion
  70.6 44.7 %all-to-all-done = bf16[16,256,256]{1,2,0:T(8,128)(2,1)S(1)} async-done(((bf16[16,256,256]{1,2,0:T(8,128)(2,1)}), bf16[16,256,256]{1,2,0:T(8,128)(2,1)S(1)}, u32[]{:S(2)}, u32[]{:S(2)}) %all-to-all-start) | async-done | bytes 2097184 | tf_op jit(solution)/shard_map/all_to_all | solution.py:37
  115.3 7.7 %all-to-all-start.3 = ((f32[16,64,384]{2,1,0:T(8,128)}), f32[16,64,384]{2,1,0:T(8,128)}, u32[]{:S(2)}, u32[]{:S(2)}) async-start(f32[16,64,384]{2,1,0:T(8,128)} %maximum_bitcast_fusion), calls=%async_computation.3 | async-start | bytes 3145728 | tf_op jit(solution)/shard_map/all_to_all | solution.py:78
  124.8 2.8 %fusion.45 = (bf16[16,1,256,128]{3,2,1,0:T(8,128)(2,1)S(1)}, bf16[16,1,256,128]{3,2,1,0:T(8,128)(2,1)}) fusion(bf16[16,2,256,128]{3,2,1,0:T(8,128)(2,1)} %copy-done), kind=kLoop, calls=%fused_computation.67 | loop fusion | bytes 4194304 | tf_op jit(solution)/shard_map/slice | solution.py:67
  127.6 17.8 %all-to-all-done.3 = f32[16,64,384]{2,1,0:T(8,128)} async-done(((f32[16,64,384]{2,1,0:T(8,128)}), f32[16,64,384]{2,1,0:T(8,128)}, u32[]{:S(2)}, u32[]{:S(2)}) %all-to-all-start.3) | async-done | bytes 1572896 | tf_op jit(solution)/shard_map/all_to_all | solution.py:78
  145.4 1.5 reduce_sum.59
  146.9 4.4 %collective-permute-start = (bf16[64,128]{1,0:T(8,128)(2,1)S(1)}, bf16[64,128]{1,0:T(8,128)(2,1)S(1)}, u32[]{:S(2)}, u32[]{:S(2)}) collective-permute-start(bf16[64,128]{1,0:T(8,128)(2,1)S(1)} %slice.25), channel_id=1, source_target_pairs={{0,16},{16,0},{32,48},{48,32},{64,80},{80,64},{96,112},{112,96},{1... | collective-permute-start | bytes 49160 | tf_op jit(solution)/shard_map/ppermute | solution.py:82
  151.3 0.5 fusion.46
  151.8 1.2 collective-permute-done
  153.0 0.2 fusion.47
  153.2 0.5 fusion.2
  153.8 0.5 fusion.12
  154.4 0.2 fusion.9
  154.6 0.8 fusion.4
  155.4 13.7 %all_to_all.26 = bf16[16,64,256]{2,1,0:T(8,128)(2,1)S(1)} all-to-all(bf16[16,64,256]{2,1,0:T(8,128)(2,1)S(1)} %fusion.4), channel_id=1, replica_groups=mesh['row'=16,'col'=16] {'row'}, dimensions={0} | all-to-all | bytes 1048576 | tf_op jit(solution)/shard_map/all_to_all | solution.py:30
  169.1 0.7 reduce_sum.62
  (37 shorter events, 1.7 us)
Async XLA Ops:
  6.5 59.6 %all-gather.2.cloned.1.call-start = ((), (), s32[]{:S(2)}) async-start(), calls=%async_computation.5 | async-start | bytes 3342336 | tf_op jit(solution)/shard_map/all_gather | solution.py:57
  8.7 13.6 %all-to-all-start.2 = ((f32[16,1,64]{2,1,0:T(1,128)}), f32[16,1,64]{2,1,0:T(1,128)S(1)}, u32[]{:S(2)}, u32[]{:S(2)}) async-start(f32[16,1,64]{2,1,0:T(1,128)} %broadcast_in_dim.66), calls=%async_computation.2 | async-start | bytes 16384 | tf_op jit(solution)/shard_map/all_to_all | solution.py:37
  24.3 5.1 %copy-start.3 = (bf16[256,256]{1,0:T(8,128)(2,1)S(1)}, bf16[256,256]{1,0:T(8,128)(2,1)}, u32[]{:S(2)}) copy-start(bf16[256,256]{1,0:T(8,128)(2,1)} %param.11) | copy-start | bytes 393220
  24.3 31.2 %all-to-all-start.1 = ((bf16[16,2,256,128]{3,2,1,0:T(8,128)(2,1)}), bf16[16,2,256,128]{3,2,1,0:T(8,128)(2,1)S(1)}, u32[]{:S(2)}, u32[]{:S(2)}) async-start(bf16[16,2,256,128]{3,2,1,0:T(8,128)(2,1)} %bitcast.96), calls=%async_computation.1 | async-start | bytes 4194304 | tf_op jit(solution)/shard_map/all_to_all | solution.py:63
  55.5 2.0 %copy-start = (bf16[16,2,256,128]{3,2,1,0:T(8,128)(2,1)}, bf16[16,2,256,128]{3,2,1,0:T(8,128)(2,1)S(1)}, u32[]{:S(2)}) copy-start(bf16[16,2,256,128]{3,2,1,0:T(8,128)(2,1)S(1)} %all-to-all-done.1) | copy-start | bytes 6291460
  57.2 8.9 %copy-start.5 = (bf16[256]{0:T(256)(128)(2,1)S(1)}, bf16[256]{0:T(256)(128)(2,1)}, u32[]{:S(2)}) copy-start(bf16[256]{0:T(256)(128)(2,1)} %param.9) | copy-start | bytes 1540
  57.2 8.9 %copy-start.2 = (bf16[64,256]{1,0:T(8,128)(2,1)S(1)}, bf16[64,256]{1,0:T(8,128)(2,1)}, u32[]{:S(2)}) copy-start(bf16[64,256]{1,0:T(8,128)(2,1)} %param.8) | copy-start | bytes 98308
  57.5 57.8 %all-to-all-start = ((bf16[16,256,256]{1,2,0:T(8,128)(2,1)}), bf16[16,256,256]{1,2,0:T(8,128)(2,1)S(1)}, u32[]{:S(2)}, u32[]{:S(2)}) async-start(bf16[16,256,256]{1,2,0:T(8,128)(2,1)} %broadcast_in_dim.64), calls=%async_computation | async-start | bytes 4194304 | tf_op jit(solution)/shard_map/all_to_all | solution.py:37
  70.6 53.1 %copy-start.4 = (s32[1,64]{1,0:T(1,128)S(1)}, s32[1,64]{1,0:T(1,128)}, u32[]{:S(2)}) copy-start(s32[1,64]{1,0:T(1,128)} %param.15) | copy-start | bytes 772
  115.3 30.1 %all-to-all-start.3 = ((f32[16,64,384]{2,1,0:T(8,128)}), f32[16,64,384]{2,1,0:T(8,128)}, u32[]{:S(2)}, u32[]{:S(2)}) async-start(f32[16,64,384]{2,1,0:T(8,128)} %maximum_bitcast_fusion), calls=%async_computation.3 | async-start | bytes 3145728 | tf_op jit(solution)/shard_map/all_to_all | solution.py:78
  146.9 6.1 %collective-permute-start = (bf16[64,128]{1,0:T(8,128)(2,1)S(1)}, bf16[64,128]{1,0:T(8,128)(2,1)S(1)}, u32[]{:S(2)}, u32[]{:S(2)}) collective-permute-start(bf16[64,128]{1,0:T(8,128)(2,1)S(1)} %slice.25), channel_id=1, source_target_pairs={{0,16},{16,0},{32,48},{48,32},{64,80},{80,64},{96,112},{112,96},{1... | collective-permute-start | bytes 49160 | tf_op jit(solution)/shard_map/ppermute | solution.py:82
  151.3 2.5 %copy-start.1 = (bf16[16,1,256,128]{3,2,1,0:T(8,128)(2,1)S(1)}, bf16[16,1,256,128]{3,2,1,0:T(8,128)(2,1)}, u32[]{:S(2)}) copy-start(bf16[16,1,256,128]{3,2,1,0:T(8,128)(2,1)} %get-tuple-element.14) | copy-start | bytes 3145732
Sparse Core Ops, SparseCore 0:
  9.1 43.8 all-gather.1

commit v15 on v13

--- a/solution.py
+++ b/solution.py
@@ -53,9 +53,12 @@
     normed = (features * row_scale[:, None] * norm_gain.astype(jnp.float32)[None, :]).astype(
         jnp.bfloat16
     )
-    partial_value = jnp.dot(
-        normed, lax.all_gather(w_qkv, "col", axis=1, tiled=True), preferred_element_type=jnp.float32
-    )
+    qkv_width = w_qkv.shape[1]
+    col_count = lax.axis_size("col")
+    weights_all = lax.all_gather(jnp.concatenate([w_qkv, w_out], axis=1), "col", axis=1, tiled=False)
+    qkv_all = weights_all[:, :, :qkv_width].reshape(w_qkv.shape[0], col_count * qkv_width)
+    out_all = weights_all[:, :, qkv_width:].reshape(w_out.shape[0], -1)
+    partial_value = jnp.dot(normed, qkv_all, preferred_element_type=jnp.float32)
     local = jnp.stack([cache_k[0], value_cache[0]]).reshape(
         2, token_positions, KEY_VALUE_HEADS, HEAD_SIZE
     ).transpose(2, 0, 1, 3)
@@ -108,7 +111,7 @@
     attended = attended.transpose(1, 0, 2).reshape(rows_here, heads_dev * HEAD_SIZE)
     partial_out = jnp.dot(
         attended,
-        lax.all_gather(w_out, "col", axis=1, tiled=True),
+        out_all,
         preferred_element_type=jnp.float32,
     )
     return row_reduce(partial_out, "row", jnp.bfloat16).astype(jnp.bfloat16)

time: 132 us -> 129 us (0.977)
  waiting for transfers between devices: 55 us -> 42.1 us
  local copies, waits for them, and re-layouts: 11.9 us -> 21.6 us
  starting transfers between devices: 20.6 us -> 23.6 us
  blocking collectives: 16.5 us -> 14 us
  matrix products: 6.86 us -> 4.97 us
  other arithmetic: 6.37 us -> 8.15 us
    all_gather x2 -> x1, waiting for transfers between devices: 47.3 us -> 25 us  [shards(): lax.all_gather(jnp.concatenate([w_qkv, w_out], axis=1), 'col', axis=1, ti...]
    all_to_all x1, waiting for transfers between devices: 0.01 us -> 11.6 us  [shards(): lax.all_to_all(owned, 'row', 0, 0)]
    slice x0 -> x3, local copies, waits for them, and re-layouts: none -> 7.73 us  [the longest x2 7.42 us: shards(): out_all = weights_all[:, :, qkv_width:].reshape(w_out.shape[0], -1)]
    unnamed x15 -> x19, local copies, waits for them, and re-layouts: 2.54 us -> 9.07 us
    dot_general x1 -> x0, local copies, waits for them, and re-layouts: 4.09 us -> none  [shards(): jnp.dot(attended, lax.all_gather(w_out, 'col', axis=1, tiled=True), prefe...]
    ppermute x1, starting transfers between devices: 0.58 us -> 3.62 us  [shards(): pair_theirs = lax.ppermute(pair_mine, 'row', partner)]
    all_to_all x1, blocking collectives: 16.5 us -> 14 us  [row_reduce(): received = lax.all_to_all(pieces, axis_name, 0, 0)]
    dot_general x2, matrix products: 4.58 us -> 2.7 us  [the longest x1 1.95 us: shards(): partial_value = jnp.dot(normed, qkv_all, preferred_element_type=jnp.float32)]
  transfers between devices with their start and end apart: 6 -> 5, of which waited for: 4 -> 4; matrix products, arithmetic and copies ran while one was open for 13% -> 17% of each run, Pallas kernels for 0% -> 0%
where the time goes in v15:
time: 129 us
  waiting for transfers between devices  42.1 us (33%)
  starting transfers between devices  23.6 us (18%)
  local copies, waits for them, and re-layouts  21.6 us (17%)
  between operations  14.3 us (11%)
  blocking collectives  14 us (11%)
  other arithmetic  8.15 us (6%)
  matrix products  4.97 us (4%)
    all_gather x1, waiting for transfers between devices, shards(): lax.all_gather(jnp.concatenate([w_qkv, w_out], axis=1), 'col', axis=1, ti...  25 us
    all_to_all x1, blocking collectives, row_reduce(): received = lax.all_to_all(pieces, axis_name, 0, 0)  14 us
    all_to_all x1, waiting for transfers between devices, shards(): lax.all_to_all(owned, 'row', 0, 0)  11.6 us
    unnamed x19, local copies, waits for them, and re-layouts  9.07 us
    all_to_all x1, starting transfers between devices, row_gather(): return lax.all_to_all(copies, axis_name, 0, 0)  7.48 us
    slice x2, local copies, waits for them, and re-layouts, shards(): out_all = weights_all[:, :, qkv_width:].reshape(w_out.shape[0], -1)  7.42 us
    all_to_all x1, starting transfers between devices, shards(): lax.all_to_all(owned, 'row', 0, 0)  7.41 us
    all_to_all x1, starting transfers between devices, shards(): by_head = lax.all_to_all(pieces, 'row', 0, 0)  5.1 us
  transfers between devices with their start and end apart: 5, of which 4 were waited for; matrix products, arithmetic and copies ran while one was open for 17% of the time, Pallas kernels for 0%

profile of v15, /device:TPU:2, one launch (start us, length us, event | category | flops | bytes accessed | tf_op | source)
XLA Modules:
  0.0 128.8 jit_solution(8996456725546448085)
XLA Ops:
  6.5 1.7 %pad_maximum_fusion.1 = bf16[256,640]{1,0:T(8,128)(2,1)} fusion(bf16[256,256]{1,0:T(8,128)(2,1)} %param.11, bf16[256,384]{1,0:T(8,128)(2,1)} %param.10), kind=kLoop, calls=%fused_computation.34 | loop fusion | flops 655360 | bytes 655360 | tf_op jit(solution)/shard_map/concatenate | solution.py:58
  8.3 0.9 fusion.24
  9.2 0.6 broadcast_in_dim.59
  9.8 7.5 %all-to-all-start.1 = ((f32[16,1,64]{2,1,0:T(1,128)}), f32[16,1,64]{2,1,0:T(1,128)S(1)}, u32[]{:S(2)}, u32[]{:S(2)}) async-start(f32[16,1,64]{2,1,0:T(1,128)} %broadcast_in_dim.59), calls=%async_computation.1 | async-start | bytes 16384 | tf_op jit(solution)/shard_map/all_to_all | solution.py:37
  17.3 1.3 %pad_maximum_fusion = bf16[2,256,1024]{2,1,0:T(8,128)(2,1)S(1)} fusion(bf16[1,256,1024]{2,1,0:T(8,128)(2,1)} %param.13, bf16[1,256,1024]{2,1,0:T(8,128)(2,1)} %param.12), kind=kLoop, calls=%fused_computation.29 | loop fusion | flops 524288 | bytes 2097152 | tf_op jit(solution)/shard_map/stack | solution.py:62
  19.1 4.3 %all-to-all-done.1 = f32[16,1,64]{2,1,0:T(1,128)S(1)} async-done(((f32[16,1,64]{2,1,0:T(1,128)}), f32[16,1,64]{2,1,0:T(1,128)S(1)}, u32[]{:S(2)}, u32[]{:S(2)}) %all-to-all-start.1) | async-done | bytes 4128 | tf_op jit(solution)/shard_map/all_to_all | solution.py:37
  23.4 2.0 %broadcast_in_dim.58 = bf16[8,2,2,256,128]{4,3,2,1,0:T(8,128)(2,1)} broadcast(bf16[8,2,256,128]{3,2,1,0:T(8,128)(2,1)S(1)} %copy.40), dimensions={0,2,3,4} | broadcast | bytes 3145728 | tf_op jit(solution)/shard_map/broadcast_in_dim | solution.py:65
  25.4 5.1 %all-to-all-start = ((bf16[16,2,256,128]{3,2,1,0:T(8,128)(2,1)}), bf16[16,2,256,128]{3,2,1,0:T(8,128)(2,1)S(1)}, u32[]{:S(2)}, u32[]{:S(2)}) async-start(bf16[16,2,256,128]{3,2,1,0:T(8,128)(2,1)} %bitcast.107), calls=%async_computation | async-start | bytes 4194304 | tf_op jit(solution)/shard_map/all_to_all | solution.py:66
  30.5 25.0 %all-gather.3.cloned.1.call-done = bf16[256,10240]{1,0:T(8,128)(2,1)} async-done(((bf16[256,640]{1,0:T(8,128)(2,1)}), bf16[256,10240]{1,0:T(8,128)(2,1)}) %all-gather.3.cloned.1.call-update) | async-done | bytes 5242896 | tf_op jit(solution)/shard_map/all_gather | solution.py:58
  55.5 3.6 %copy.54 = bf16[32,8,16,640]{3,2,1,0:T(8,128)(2,1)S(1)} copy(bf16[32,8,16,640]{3,1,2,0:T(8,128)(2,1)} %bitcast.109) | data formatting | bytes 10485760
  59.1 0.3 slice.32
  59.4 2.0 %copy-done = bf16[32,8,16,640]{3,2,1,0:T(8,128)(2,1)} copy-done((bf16[32,8,16,640]{3,2,1,0:T(8,128)(2,1)}, bf16[32,8,16,640]{3,2,1,0:T(8,128)(2,1)S(1)}, u32[]{:S(2)}) %copy-start) | copy-done | bytes 5242904
  61.4 0.9 copy.55
  62.4 1.9 %fusion.30 = f32[64,6144]{1,0:T(8,128)} fusion(bf16[256,6144]{1,0:T(8,128)(2,1)S(1)} %bitcast.106, bf16[64,256]{1,0:T(8,128)(2,1)S(1)} %copy-done.4, f32[256]{0:T(256)S(1)} %convert_element_type.87, f32[64]{0:T(128)S(1)} %add_rsqrt_fusion), kind=kOutput, calls=%fused_computation.45 | convolution fusion | flops 201392128 | bytes 4752640 | tf_op jit(solution)/shard_map/dot_general | solution.py:61
  64.3 1.4 %copy-done.2 = f32[64,6144]{1,0:T(8,128)S(1)} copy-done((f32[64,6144]{1,0:T(8,128)S(1)}, f32[64,6144]{1,0:T(8,128)}, u32[]{:S(2)}) %copy-start.2) | copy-done | bytes 1572888
  65.8 0.3 slice-done
  66.5 1.3 %maximum_bitcast_fusion = f32[16,64,384]{2,1,0:T(8,128)} fusion(f32[64,16,128]{2,0,1:T(8,128)S(1)} %bitcast.115, f32[64,16,256]{2,0,1:T(8,128)S(1)} %bitcast.110), kind=kLoop, calls=%fused_computation.8 | loop fusion | flops 393216 | bytes 3145728 | tf_op jit(solution)/shard_map/transpose | solution.py:78
  67.8 7.4 %all-to-all-start.2 = ((f32[16,64,384]{2,1,0:T(8,128)}), f32[16,64,384]{2,1,0:T(8,128)}, u32[]{:S(2)}, u32[]{:S(2)}) async-start(f32[16,64,384]{2,1,0:T(8,128)} %maximum_bitcast_fusion), calls=%async_computation.2 | async-start | bytes 3145728 | tf_op jit(solution)/shard_map/all_to_all | solution.py:79
  77.0 3.1 %slice.35 = bf16[256,16,256]{2,1,0:T(8,128)(2,1)} slice(bf16[256,16,640]{2,1,0:T(8,128)(2,1)} %bitcast.104), slice={[0:256], [0:16], [384:640]} | slice | bytes 4194304 | tf_op jit(solution)/shard_map/slice | solution.py:60
  80.1 4.3 %copy.49 = bf16[256,16,256]{0,2,1:T(8,128)(2,1)} copy(bf16[256,16,256]{2,1,0:T(8,128)(2,1)} %slice.35) | data formatting | bytes 4194304 | tf_op jit(solution)/shard_map/slice | solution.py:60
  84.4 1.2 fusion.52
  85.6 11.6 %all-to-all-done.2 = f32[16,64,384]{2,1,0:T(8,128)} async-done(((f32[16,64,384]{2,1,0:T(8,128)}), f32[16,64,384]{2,1,0:T(8,128)}, u32[]{:S(2)}, u32[]{:S(2)}) %all-to-all-start.2) | async-done | bytes 1572896 | tf_op jit(solution)/shard_map/all_to_all | solution.py:79
  97.2 1.5 %reduce_sum.59 = bf16[64,384]{1,0:T(8,128)(2,1)S(1)} reduce(f32[16,64,384]{2,1,0:T(8,128)} %all-to-all-done.2, f32[]{:T(128)} %constant.11.clone.1), dimensions={0}, to_apply=%region_2.0 | reduce | flops 368640 | bytes 1622020 | tf_op jit(solution)/shard_map/reduce_sum | solution.py:79
  98.7 3.6 %collective-permute-start = (bf16[64,128]{1,0:T(8,128)(2,1)S(1)}, bf16[64,128]{1,0:T(8,128)(2,1)S(1)}, u32[]{:S(2)}, u32[]{:S(2)}) collective-permute-start(bf16[64,128]{1,0:T(8,128)(2,1)S(1)} %slice.34), channel_id=1, source_target_pairs={{0,16},{16,0},{32,48},{48,32},{64,80},{80,64},{96,112},{112,96},{1... | collective-permute-start | bytes 49160 | tf_op jit(solution)/shard_map/ppermute | solution.py:83
  102.4 0.5 fusion.53
  102.9 1.2 collective-permute-done
  104.3 0.5 fusion.4
  104.8 0.5 fusion.19
  105.7 0.8 copy-done.1
  106.4 0.7 fusion.9
  107.2 14.0 %all_to_all.21 = bf16[16,64,256]{2,1,0:T(8,128)(2,1)S(1)} all-to-all(bf16[16,64,256]{2,1,0:T(8,128)(2,1)S(1)} %fusion.9), channel_id=1, replica_groups=mesh['row'=16,'col'=16] {'row'}, dimensions={0} | all-to-all | bytes 1048576 | tf_op jit(solution)/shard_map/all_to_all | solution.py:30
  121.2 0.7 reduce_sum.62
  (42 shorter events, 2.6 us)
Async XLA Ops:
  6.5 49.0 %all-gather.3.cloned.1.call-start = ((), (), s32[]{:S(2)}) async-start(), calls=%async_computation.4 | async-start | bytes 5570560 | tf_op jit(solution)/shard_map/all_gather | solution.py:58
  9.8 13.6 %all-to-all-start.1 = ((f32[16,1,64]{2,1,0:T(1,128)}), f32[16,1,64]{2,1,0:T(1,128)S(1)}, u32[]{:S(2)}, u32[]{:S(2)}) async-start(f32[16,1,64]{2,1,0:T(1,128)} %broadcast_in_dim.59), calls=%async_computation.1 | async-start | bytes 16384 | tf_op jit(solution)/shard_map/all_to_all | solution.py:37
  25.4 5.1 %copy-start.6 = (bf16[256]{0:T(256)(128)(2,1)S(1)}, bf16[256]{0:T(256)(128)(2,1)}, u32[]{:S(2)}) copy-start(bf16[256]{0:T(256)(128)(2,1)} %param.9) | copy-start | bytes 1540
  25.4 38.9 %all-to-all-start = ((bf16[16,2,256,128]{3,2,1,0:T(8,128)(2,1)}), bf16[16,2,256,128]{3,2,1,0:T(8,128)(2,1)S(1)}, u32[]{:S(2)}, u32[]{:S(2)}) async-start(bf16[16,2,256,128]{3,2,1,0:T(8,128)(2,1)} %bitcast.107), calls=%async_computation | async-start | bytes 4194304 | tf_op jit(solution)/shard_map/all_to_all | solution.py:66
  59.1 2.3 %copy-start = (bf16[32,8,16,640]{3,2,1,0:T(8,128)(2,1)}, bf16[32,8,16,640]{3,2,1,0:T(8,128)(2,1)S(1)}, u32[]{:S(2)}) copy-start(bf16[32,8,16,640]{3,2,1,0:T(8,128)(2,1)S(1)} %copy.54) | copy-start | bytes 15728644
  61.4 0.9 copy-start.4
  64.3 1.4 %copy-start.2 = (f32[64,6144]{1,0:T(8,128)S(1)}, f32[64,6144]{1,0:T(8,128)}, u32[]{:S(2)}) copy-start(f32[64,6144]{1,0:T(8,128)} %fusion.30) | copy-start | bytes 4718596
  64.3 1.8 %slice-start = ((f32[64,6144]{1,0:T(8,128)}), f32[64,4096]{1,0:T(8,128)S(1)}, s32[]{:S(2)}) async-start(f32[64,6144]{1,0:T(8,128)} %fusion.30), calls=%async_computation.5 | async-start | bytes 2097152 | tf_op jit(solution)/shard_map/slice | solution.py:71
  67.8 7.4 %copy-start.5 = (s32[1,64]{1,0:T(1,128)S(1)}, s32[1,64]{1,0:T(1,128)}, u32[]{:S(2)}) copy-start(s32[1,64]{1,0:T(1,128)} %param.15) | copy-start | bytes 772
  67.8 29.4 %all-to-all-start.2 = ((f32[16,64,384]{2,1,0:T(8,128)}), f32[16,64,384]{2,1,0:T(8,128)}, u32[]{:S(2)}, u32[]{:S(2)}) async-start(f32[16,64,384]{2,1,0:T(8,128)} %maximum_bitcast_fusion), calls=%async_computation.2 | async-start | bytes 3145728 | tf_op jit(solution)/shard_map/all_to_all | solution.py:79
  98.7 5.3 %collective-permute-start = (bf16[64,128]{1,0:T(8,128)(2,1)S(1)}, bf16[64,128]{1,0:T(8,128)(2,1)S(1)}, u32[]{:S(2)}, u32[]{:S(2)}) collective-permute-start(bf16[64,128]{1,0:T(8,128)(2,1)S(1)} %slice.34), channel_id=1, source_target_pairs={{0,16},{16,0},{32,48},{48,32},{64,80},{80,64},{96,112},{112,96},{1... | collective-permute-start | bytes 49160 | tf_op jit(solution)/shard_map/ppermute | solution.py:83
  102.3 2.5 %copy-start.3 = (bf16[16,1,256,128]{3,2,1,0:T(8,128)(2,1)S(1)}, bf16[16,1,256,128]{3,2,1,0:T(8,128)(2,1)}, u32[]{:S(2)}) copy-start(bf16[16,1,256,128]{3,2,1,0:T(8,128)(2,1)} %get-tuple-element.10) | copy-start | bytes 3145732
  104.8 1.6 %copy-start.1 = (bf16[256,16,256]{0,2,1:T(8,128)(2,1)S(1)}, bf16[256,16,256]{0,2,1:T(8,128)(2,1)}, u32[]{:S(2)}) copy-start(bf16[256,16,256]{0,2,1:T(8,128)(2,1)} %copy.49) | copy-start | bytes 6291460
Sparse Core Ops, SparseCore 0:
  9.1 46.3 all-gather.2

commit v16 on v15

--- a/solution.py
+++ b/solution.py
@@ -55,10 +55,13 @@
     )
     qkv_width = w_qkv.shape[1]
     col_count = lax.axis_size("col")
-    weights_all = lax.all_gather(jnp.concatenate([w_qkv, w_out], axis=1), "col", axis=1, tiled=False)
-    qkv_all = weights_all[:, :, :qkv_width].reshape(w_qkv.shape[0], col_count * qkv_width)
-    out_all = weights_all[:, :, qkv_width:].reshape(w_out.shape[0], -1)
-    partial_value = jnp.dot(normed, qkv_all, preferred_element_type=jnp.float32)
+    weights_all = lax.all_gather(jnp.concatenate([w_qkv, w_out], axis=1), "col", axis=1, tiled=True)
+    weights_all = lax.optimization_barrier(weights_all)
+    partial_all = jnp.dot(
+        normed, weights_all, preferred_element_type=jnp.float32
+    ).reshape(rows_here, col_count, -1)
+    partial_value = partial_all[:, :, :qkv_width].reshape(rows_here, col_count * qkv_width)
+
     local = jnp.stack([cache_k[0], value_cache[0]]).reshape(
         2, token_positions, KEY_VALUE_HEADS, HEAD_SIZE
     ).transpose(2, 0, 1, 3)
@@ -110,10 +113,8 @@
     attended = (blended / totals[..., None]).astype(jnp.bfloat16)
     attended = attended.transpose(1, 0, 2).reshape(rows_here, heads_dev * HEAD_SIZE)
     partial_out = jnp.dot(
-        attended,
-        out_all,
-        preferred_element_type=jnp.float32,
-    )
+        attended, weights_all, preferred_element_type=jnp.float32
+    ).reshape(rows_here, col_count, -1)[:, :, qkv_width:].reshape(rows_here, -1)
     return row_reduce(partial_out, "row", jnp.bfloat16).astype(jnp.bfloat16)
 
 

time: 129 us -> 131 us (1.016)
  matrix products: 4.97 us -> 10 us
  local copies, waits for them, and re-layouts: 21.6 us -> 19.6 us
    dot_general x0 -> x1, local copies, waits for them, and re-layouts: none -> 7.92 us  [shards(): jnp.dot(attended, weights_all, preferred_element_type=jnp.float32)]
    slice x3 -> x1, local copies, waits for them, and re-layouts: 7.73 us -> 0.1 us  [shards(): partial_all[:, :, :qkv_width].reshape(rows_here, col_count * qkv_width)]
    unnamed x19 -> x14, local copies, waits for them, and re-layouts: 9.07 us -> 3.95 us
    dot_general x2, matrix products: 2.7 us -> 7.74 us  [the longest x1 4.18 us: shards(): jnp.dot(attended, weights_all, preferred_element_type=jnp.float32)]
    transpose x0 -> x2, local copies, waits for them, and re-layouts: none -> 1.88 us  [the longest x1 1.71 us: shards(): owned = jnp.concatenate([query_part, pair_part], axis=2).transpose(1, 0, 2)]
where the time goes in v16:
time: 131 us; the launch traced here: 130 us
  waiting for transfers between devices  41.7 us (32%)
  starting transfers between devices  23.6 us (18%)
  local copies, waits for them, and re-layouts  19.6 us (15%)
  between operations  14.3 us (11%)
  blocking collectives  14.1 us (11%)
  matrix products  10 us (8%)
  other arithmetic  6.95 us (5%)
    all_gather x1, waiting for transfers between devices, shards(): lax.all_gather(jnp.concatenate([w_qkv, w_out], axis=1), 'col', axis=1, ti...  25.1 us
    all_to_all x1, blocking collectives, row_reduce(): received = lax.all_to_all(pieces, axis_name, 0, 0)  14.1 us
    all_to_all x1, waiting for transfers between devices, shards(): lax.all_to_all(owned, 'row', 0, 0)  11.1 us
    dot_general x1, local copies, waits for them, and re-layouts, shards(): jnp.dot(attended, weights_all, preferred_element_type=jnp.float32)  7.92 us
    all_to_all x1, starting transfers between devices, row_gather(): return lax.all_to_all(copies, axis_name, 0, 0)  7.48 us
    all_to_all x1, starting transfers between devices, shards(): lax.all_to_all(owned, 'row', 0, 0)  7.41 us
    all_to_all x1, starting transfers between devices, shards(): by_head = lax.all_to_all(pieces, 'row', 0, 0)  5.1 us
    all_to_all x1, waiting for transfers between devices, row_gather(): return lax.all_to_all(copies, axis_name, 0, 0)  4.29 us
  transfers between devices with their start and end apart: 5, of which 4 were waited for; matrix products, arithmetic and copies ran while one was open for 17% of the time, Pallas kernels for 0%

profile of v16, /device:TPU:2, one launch (start us, length us, event | category | flops | bytes accessed | tf_op | source)
XLA Modules:
  0.0 130.2 jit_solution(3898456836432344498)
XLA Ops:
  6.5 1.7 %pad_maximum_fusion.1 = bf16[256,640]{1,0:T(8,128)(2,1)} fusion(bf16[256,256]{1,0:T(8,128)(2,1)} %param.11, bf16[256,384]{1,0:T(8,128)(2,1)} %param.10), kind=kLoop, calls=%fused_computation.31 | loop fusion | flops 655360 | bytes 655360 | tf_op jit(solution)/shard_map/concatenate | solution.py:58
  8.3 0.9 fusion.17
  9.2 0.6 broadcast_in_dim.59
  9.8 7.5 %all-to-all-start.1 = ((f32[16,1,64]{2,1,0:T(1,128)}), f32[16,1,64]{2,1,0:T(1,128)S(1)}, u32[]{:S(2)}, u32[]{:S(2)}) async-start(f32[16,1,64]{2,1,0:T(1,128)} %broadcast_in_dim.59), calls=%async_computation.1 | async-start | bytes 16384 | tf_op jit(solution)/shard_map/all_to_all | solution.py:37
  17.3 1.3 pad_maximum_fusion
  18.6 0.3 copy.72
  18.9 0.2 copy.58
  19.1 4.3 %all-to-all-done.1 = f32[16,1,64]{2,1,0:T(1,128)S(1)} async-done(((f32[16,1,64]{2,1,0:T(1,128)}), f32[16,1,64]{2,1,0:T(1,128)S(1)}, u32[]{:S(2)}, u32[]{:S(2)}) %all-to-all-start.1) | async-done | bytes 4128 | tf_op jit(solution)/shard_map/all_to_all | solution.py:37
  23.4 1.8 %broadcast_in_dim.58 = bf16[8,2,2,256,128]{4,3,2,1,0:T(8,128)(2,1)} broadcast(bf16[8,2,256,128]{3,2,1,0:T(8,128)(2,1)S(1)} %copy.58), dimensions={0,2,3,4} | broadcast | bytes 3145728 | tf_op jit(solution)/shard_map/broadcast_in_dim | solution.py:68
  25.3 5.1 %all-to-all-start = ((bf16[16,2,256,128]{3,2,1,0:T(8,128)(2,1)}), bf16[16,2,256,128]{3,2,1,0:T(8,128)(2,1)S(1)}, u32[]{:S(2)}, u32[]{:S(2)}) async-start(bf16[16,2,256,128]{3,2,1,0:T(8,128)(2,1)} %bitcast.96), calls=%async_computation | async-start | bytes 4194304 | tf_op jit(solution)/shard_map/all_to_all | solution.py:69
  30.4 25.1 %all-gather.2.cloned.1.call-done = bf16[256,10240]{1,0:T(8,128)(2,1)} async-done(((bf16[256,640]{1,0:T(8,128)(2,1)}), bf16[256,10240]{1,0:T(8,128)(2,1)}) %all-gather.2.cloned.1.call-update) | async-done | bytes 5242896 | tf_op jit(solution)/shard_map/all_gather | solution.py:58
  55.5 3.6 %fusion.23 = f32[64,10240]{1,0:T(8,128)S(1)} fusion(bf16[256,10240]{1,0:T(8,128)(2,1)} %all-gather.2.cloned.1.call-done, bf16[64,256]{1,0:T(8,128)(2,1)S(1)} %copy-done.1, f32[256]{0:T(256)S(1)} %convert_element_type.85, f32[64]{0:T(128)S(1)} %add_rsqrt_fusion), kind=kOutput, calls=%fused_computation.42 | convolution fusion | flops 335609856 | bytes 7898368 | tf_op jit(solution)/shard_map/dot_general | solution.py:60
  59.1 0.5 copy.73
  59.7 1.7 %copy.74 = f32[8,8,16,384]{3,1,2,0:T(8,128)} copy(f32[8,8,16,384]{3,2,1,0:T(8,128)S(1)} %bitcast.100) | data formatting | bytes 3145728
  61.4 1.3 slice.27
  62.7 1.1 slice_bitcast_fusion
  63.8 0.3 copy.75
  64.4 0.3 copy.61
  64.8 1.7 %copy.62 = f32[16,64,384]{2,1,0:T(8,128)} copy(f32[16,64,384]{2,0,1:T(8,128)S(1)} %maximum_bitcast_fusion) | data formatting | bytes 3145728 | tf_op jit(solution)/shard_map/transpose | solution.py:81
  66.5 7.4 %all-to-all-start.2 = ((f32[16,64,384]{2,1,0:T(8,128)}), f32[16,64,384]{2,1,0:T(8,128)}, u32[]{:S(2)}, u32[]{:S(2)}) async-start(f32[16,64,384]{2,1,0:T(8,128)} %copy.62), calls=%async_computation.2 | async-start | bytes 3145728 | tf_op jit(solution)/shard_map/all_to_all | solution.py:82
  75.7 7.9 %copy.70 = bf16[10240,256]{1,0:T(8,128)(2,1)} copy(bf16[10240,256]{0,1:T(8,128)(2,1)} %bitcast.93) | data formatting | bytes 10485760 | tf_op jit(solution)/shard_map/dot_general | solution.py:115
  83.6 1.2 fusion.45
  84.8 11.1 %all-to-all-done.2 = f32[16,64,384]{2,1,0:T(8,128)} async-done(((f32[16,64,384]{2,1,0:T(8,128)}), f32[16,64,384]{2,1,0:T(8,128)}, u32[]{:S(2)}, u32[]{:S(2)}) %all-to-all-start.2) | async-done | bytes 1572896 | tf_op jit(solution)/shard_map/all_to_all | solution.py:82
  95.9 1.5 %reduce_sum.59 = bf16[64,384]{1,0:T(8,128)(2,1)S(1)} reduce(f32[16,64,384]{2,1,0:T(8,128)} %all-to-all-done.2, f32[]{:T(128)} %constant.11.clone.1), dimensions={0}, to_apply=%region_2.0 | reduce | flops 368640 | bytes 1622020 | tf_op jit(solution)/shard_map/reduce_sum | solution.py:82
  97.4 3.6 %collective-permute-start = (bf16[64,128]{1,0:T(8,128)(2,1)S(1)}, bf16[64,128]{1,0:T(8,128)(2,1)S(1)}, u32[]{:S(2)}, u32[]{:S(2)}) collective-permute-start(bf16[64,128]{1,0:T(8,128)(2,1)S(1)} %slice.35), channel_id=1, source_target_pairs={{0,16},{16,0},{32,48},{48,32},{64,80},{80,64},{96,112},{112,96},{1... | collective-permute-start | bytes 49160 | tf_op jit(solution)/shard_map/ppermute | solution.py:86
  101.1 0.5 fusion.46
  101.6 1.2 collective-permute-done
  103.0 0.5 fusion.2
  103.6 0.5 fusion.11
  104.4 4.2 %fusion.48 = bf16[64,16,640]{2,0,1:T(8,128)(2,1)S(1)} fusion(bf16[64,256,1]{1,0,2:T(8,128)(2,1)S(1)} %reshape.220, bf16[16,640,256]{2,1,0:T(8,128)(2,1)} %bitcast.94), kind=kOutput, calls=%fused_computation.70 | convolution fusion | flops 335544320 | bytes 6586368 | tf_op jit(solution)/shard_map/dot_general | solution.py:115
  108.6 14.1 %all_to_all.21 = bf16[16,64,256]{2,1,0:T(8,128)(2,1)S(1)} all-to-all(bf16[16,64,256]{2,1,0:T(8,128)(2,1)S(1)} %fusion.16), channel_id=1, replica_groups=mesh['row'=16,'col'=16] {'row'}, dimensions={0} | all-to-all | bytes 1048576 | tf_op jit(solution)/shard_map/all_to_all | solution.py:30
  122.7 0.7 reduce_sum.62
  (37 shorter events, 2.2 us)
Async XLA Ops:
  6.5 49.0 %all-gather.2.cloned.1.call-start = ((), (), s32[]{:S(2)}) async-start(), calls=%async_computation.4 | async-start | bytes 5570560 | tf_op jit(solution)/shard_map/all_gather | solution.py:58
  9.8 13.6 %all-to-all-start.1 = ((f32[16,1,64]{2,1,0:T(1,128)}), f32[16,1,64]{2,1,0:T(1,128)S(1)}, u32[]{:S(2)}, u32[]{:S(2)}) async-start(f32[16,1,64]{2,1,0:T(1,128)} %broadcast_in_dim.59), calls=%async_computation.1 | async-start | bytes 16384 | tf_op jit(solution)/shard_map/all_to_all | solution.py:37
  25.3 5.1 %copy-start.3 = (bf16[256]{0:T(256)(128)(2,1)S(1)}, bf16[256]{0:T(256)(128)(2,1)}, u32[]{:S(2)}) copy-start(bf16[256]{0:T(256)(128)(2,1)} %param.9) | copy-start | bytes 1540
  25.3 30.3 %copy-start.1 = (bf16[64,256]{1,0:T(8,128)(2,1)S(1)}, bf16[64,256]{1,0:T(8,128)(2,1)}, u32[]{:S(2)}) copy-start(bf16[64,256]{1,0:T(8,128)(2,1)} %param.8) | copy-start | bytes 98308
  25.3 36.1 %all-to-all-start = ((bf16[16,2,256,128]{3,2,1,0:T(8,128)(2,1)}), bf16[16,2,256,128]{3,2,1,0:T(8,128)(2,1)S(1)}, u32[]{:S(2)}, u32[]{:S(2)}) async-start(bf16[16,2,256,128]{3,2,1,0:T(8,128)(2,1)} %bitcast.96), calls=%async_computation | async-start | bytes 4194304 | tf_op jit(solution)/shard_map/all_to_all | solution.py:69
  66.5 7.4 %copy-start.2 = (s32[1,64]{1,0:T(1,128)S(1)}, s32[1,64]{1,0:T(1,128)}, u32[]{:S(2)}) copy-start(s32[1,64]{1,0:T(1,128)} %param.15) | copy-start | bytes 772
  66.5 29.4 %all-to-all-start.2 = ((f32[16,64,384]{2,1,0:T(8,128)}), f32[16,64,384]{2,1,0:T(8,128)}, u32[]{:S(2)}, u32[]{:S(2)}) async-start(f32[16,64,384]{2,1,0:T(8,128)} %copy.62), calls=%async_computation.2 | async-start | bytes 3145728 | tf_op jit(solution)/shard_map/all_to_all | solution.py:82
  97.4 5.4 %collective-permute-start = (bf16[64,128]{1,0:T(8,128)(2,1)S(1)}, bf16[64,128]{1,0:T(8,128)(2,1)S(1)}, u32[]{:S(2)}, u32[]{:S(2)}) collective-permute-start(bf16[64,128]{1,0:T(8,128)(2,1)S(1)} %slice.35), channel_id=1, source_target_pairs={{0,16},{16,0},{32,48},{48,32},{64,80},{80,64},{96,112},{112,96},{1... | collective-permute-start | bytes 49160 | tf_op jit(solution)/shard_map/ppermute | solution.py:86
  101.1 2.5 %copy-start = (bf16[16,1,256,128]{3,2,1,0:T(8,128)(2,1)S(1)}, bf16[16,1,256,128]{3,2,1,0:T(8,128)(2,1)}, u32[]{:S(2)}) copy-start(bf16[16,1,256,128]{3,2,1,0:T(8,128)(2,1)} %get-tuple-element.10) | copy-start | bytes 3145732
Sparse Core Ops, SparseCore 0:
  9.1 46.3 all-gather.1

commit v17 on v16

--- a/solution.py
+++ b/solution.py
@@ -112,9 +112,10 @@
     )
     attended = (blended / totals[..., None]).astype(jnp.bfloat16)
     attended = attended.transpose(1, 0, 2).reshape(rows_here, heads_dev * HEAD_SIZE)
+    out_all = weights_all.reshape(w_out.shape[0], col_count, -1)[:, :, qkv_width:]
     partial_out = jnp.dot(
-        attended, weights_all, preferred_element_type=jnp.float32
-    ).reshape(rows_here, col_count, -1)[:, :, qkv_width:].reshape(rows_here, -1)
+        attended, out_all.reshape(w_out.shape[0], -1), preferred_element_type=jnp.float32
+    )
     return row_reduce(partial_out, "row", jnp.bfloat16).astype(jnp.bfloat16)
 
 

time: 131 us -> 128 us (0.977)
  matrix products: 10 us -> 6.59 us
  local copies, waits for them, and re-layouts: 19.6 us -> 21.6 us
  waiting for transfers between devices: 41.7 us -> 40.3 us
    dot_general x1 -> x0, local copies, waits for them, and re-layouts: 7.92 us -> none  [shards(): jnp.dot(attended, weights_all, preferred_element_type=jnp.float32)]
    slice x0 -> x2, local copies, waits for them, and re-layouts: none -> 5.78 us  [shards(): weights_all.reshape(w_out.shape[0], col_count, -1)[:, :, qkv_width:]]
    unnamed x14 -> x17, local copies, waits for them, and re-layouts: 3.95 us -> 8.28 us
    dot_general x1, matrix products: 4.18 us -> 0.75 us  [shards(): jnp.dot(attended, out_all.reshape(w_out.shape[0], -1), preferred_element_...]
    all_to_all x1, waiting for transfers between devices: 11.1 us -> 9.69 us  [shards(): lax.all_to_all(owned, 'row', 0, 0)]
  transfers between devices with their start and end apart: 5 -> 5, of which waited for: 4 -> 4; matrix products, arithmetic and copies ran while one was open for 17% -> 18% of each run, Pallas kernels for 0% -> 0%
where the time goes in v17:
time: 128 us; the launch traced here: 127 us
  waiting for transfers between devices  40.3 us (31%)
  starting transfers between devices  23.6 us (18%)
  local copies, waits for them, and re-layouts  21.6 us (17%)
  between operations  14.3 us (11%)
  blocking collectives  14.1 us (11%)
  other arithmetic  6.95 us (5%)
  matrix products  6.59 us (5%)
    all_gather x1, waiting for transfers between devices, shards(): lax.all_gather(jnp.concatenate([w_qkv, w_out], axis=1), 'col', axis=1, ti...  25.1 us
    all_to_all x1, blocking collectives, row_reduce(): received = lax.all_to_all(pieces, axis_name, 0, 0)  14.1 us
    all_to_all x1, waiting for transfers between devices, shards(): lax.all_to_all(owned, 'row', 0, 0)  9.69 us
    unnamed x17, local copies, waits for them, and re-layouts  8.28 us
    all_to_all x1, starting transfers between devices, row_gather(): return lax.all_to_all(copies, axis_name, 0, 0)  7.48 us
    all_to_all x1, starting transfers between devices, shards(): lax.all_to_all(owned, 'row', 0, 0)  7.41 us
    slice x2, local copies, waits for them, and re-layouts, shards(): weights_all.reshape(w_out.shape[0], col_count, -1)[:, :, qkv_width:]  5.78 us
    all_to_all x1, starting transfers between devices, shards(): by_head = lax.all_to_all(pieces, 'row', 0, 0)  5.1 us
  transfers between devices with their start and end apart: 5, of which 4 were waited for; matrix products, arithmetic and copies ran while one was open for 18% of the time, Pallas kernels for 0%

profile of v17, /device:TPU:2, one launch (start us, length us, event | category | flops | bytes accessed | tf_op | source)
XLA Modules:
  0.0 127.4 jit_solution(11809727180555643218)
XLA Ops:
  6.5 1.7 %pad_maximum_fusion.1 = bf16[256,640]{1,0:T(8,128)(2,1)} fusion(bf16[256,256]{1,0:T(8,128)(2,1)} %param.11, bf16[256,384]{1,0:T(8,128)(2,1)} %param.10), kind=kLoop, calls=%fused_computation.33 | loop fusion | flops 655360 | bytes 655360 | tf_op jit(solution)/shard_map/concatenate | solution.py:58
  8.3 0.9 fusion.24
  9.2 0.6 broadcast_in_dim.59
  9.8 7.5 %all-to-all-start.1 = ((f32[16,1,64]{2,1,0:T(1,128)}), f32[16,1,64]{2,1,0:T(1,128)S(1)}, u32[]{:S(2)}, u32[]{:S(2)}) async-start(f32[16,1,64]{2,1,0:T(1,128)} %broadcast_in_dim.59), calls=%async_computation.1 | async-start | bytes 16384 | tf_op jit(solution)/shard_map/all_to_all | solution.py:37
  17.3 1.3 %pad_maximum_fusion = bf16[2,256,1024]{2,1,0:T(8,128)(2,1)S(1)} fusion(bf16[1,256,1024]{2,1,0:T(8,128)(2,1)} %param.13, bf16[1,256,1024]{2,1,0:T(8,128)(2,1)} %param.12), kind=kLoop, calls=%fused_computation.28 | loop fusion | flops 524288 | bytes 2097152 | tf_op jit(solution)/shard_map/stack | solution.py:65
  19.1 4.3 %all-to-all-done.1 = f32[16,1,64]{2,1,0:T(1,128)S(1)} async-done(((f32[16,1,64]{2,1,0:T(1,128)}), f32[16,1,64]{2,1,0:T(1,128)S(1)}, u32[]{:S(2)}, u32[]{:S(2)}) %all-to-all-start.1) | async-done | bytes 4128 | tf_op jit(solution)/shard_map/all_to_all | solution.py:37
  23.4 1.8 %broadcast_in_dim.58 = bf16[8,2,2,256,128]{4,3,2,1,0:T(8,128)(2,1)} broadcast(bf16[8,2,256,128]{3,2,1,0:T(8,128)(2,1)S(1)} %copy.58), dimensions={0,2,3,4} | broadcast | bytes 3145728 | tf_op jit(solution)/shard_map/broadcast_in_dim | solution.py:68
  25.3 5.1 %all-to-all-start = ((bf16[16,2,256,128]{3,2,1,0:T(8,128)(2,1)}), bf16[16,2,256,128]{3,2,1,0:T(8,128)(2,1)S(1)}, u32[]{:S(2)}, u32[]{:S(2)}) async-start(bf16[16,2,256,128]{3,2,1,0:T(8,128)(2,1)} %bitcast.106), calls=%async_computation | async-start | bytes 4194304 | tf_op jit(solution)/shard_map/all_to_all | solution.py:69
  30.4 25.1 %all-gather.2.cloned.1.call-done = bf16[256,10240]{1,0:T(8,128)(2,1)} async-done(((bf16[256,640]{1,0:T(8,128)(2,1)}), bf16[256,10240]{1,0:T(8,128)(2,1)}) %all-gather.2.cloned.1.call-update) | async-done | bytes 5242896 | tf_op jit(solution)/shard_map/all_gather | solution.py:58
  55.5 3.6 %fusion.30 = f32[64,10240]{1,0:T(8,128)S(1)} fusion(bf16[256,10240]{1,0:T(8,128)(2,1)} %all-gather.2.cloned.1.call-done, bf16[64,256]{1,0:T(8,128)(2,1)S(1)} %copy-done.2, f32[256]{0:T(256)S(1)} %convert_element_type.87, f32[64]{0:T(128)S(1)} %add_rsqrt_fusion), kind=kOutput, calls=%fused_computation.44 | convolution fusion | flops 335609856 | bytes 7898368 | tf_op jit(solution)/shard_map/dot_general | solution.py:60
  59.1 0.5 copy.72
  59.7 1.7 %copy.73 = f32[8,8,16,384]{3,1,2,0:T(8,128)} copy(f32[8,8,16,384]{3,2,1,0:T(8,128)S(1)} %bitcast.110) | data formatting | bytes 3145728
  61.4 1.3 %slice.26 = f32[64,4096]{1,0:T(8,128)S(1)} slice(f32[64,6144]{1,0:T(8,128)} %bitcast.108), slice={[0:64], [0:4096]} | slice | bytes 2097152 | tf_op jit(solution)/shard_map/slice | solution.py:74
  62.7 1.1 slice_bitcast_fusion
  63.8 0.3 copy.74
  64.8 1.6 %copy.62 = f32[16,64,384]{2,1,0:T(8,128)} copy(f32[16,64,384]{2,0,1:T(8,128)S(1)} %maximum_bitcast_fusion) | data formatting | bytes 3145728 | tf_op jit(solution)/shard_map/transpose | solution.py:81
  66.4 7.4 %all-to-all-start.2 = ((f32[16,64,384]{2,1,0:T(8,128)}), f32[16,64,384]{2,1,0:T(8,128)}, u32[]{:S(2)}, u32[]{:S(2)}) async-start(f32[16,64,384]{2,1,0:T(8,128)} %copy.62), calls=%async_computation.2 | async-start | bytes 3145728 | tf_op jit(solution)/shard_map/all_to_all | solution.py:82
  75.6 3.6 %copy.76 = bf16[32,8,16,640]{3,2,1,0:T(8,128)(2,1)S(1)} copy(bf16[32,8,16,640]{3,1,2,0:T(8,128)(2,1)} %bitcast.103) | data formatting | bytes 10485760
  79.2 1.5 %slice.35 = bf16[256,16,256]{2,1,0:T(8,128)(2,1)} slice(bf16[256,16,640]{2,1,0:T(8,128)(2,1)S(1)} %bitcast.105), slice={[0:256], [0:16], [384:640]} | slice | bytes 4194304 | tf_op jit(solution)/shard_map/slice | solution.py:115
  80.7 4.3 %copy.68 = bf16[256,16,256]{0,2,1:T(8,128)(2,1)} copy(bf16[256,16,256]{2,1,0:T(8,128)(2,1)} %slice.35) | data formatting | bytes 4194304 | tf_op jit(solution)/shard_map/slice | solution.py:115
  85.0 1.2 fusion.52
  86.2 9.7 %all-to-all-done.2 = f32[16,64,384]{2,1,0:T(8,128)} async-done(((f32[16,64,384]{2,1,0:T(8,128)}), f32[16,64,384]{2,1,0:T(8,128)}, u32[]{:S(2)}, u32[]{:S(2)}) %all-to-all-start.2) | async-done | bytes 1572896 | tf_op jit(solution)/shard_map/all_to_all | solution.py:82
  95.8 1.5 %reduce_sum.59 = bf16[64,384]{1,0:T(8,128)(2,1)S(1)} reduce(f32[16,64,384]{2,1,0:T(8,128)} %all-to-all-done.2, f32[]{:T(128)} %constant.11.clone.1), dimensions={0}, to_apply=%region_2.0 | reduce | flops 368640 | bytes 1622020 | tf_op jit(solution)/shard_map/reduce_sum | solution.py:82
  97.3 3.6 %collective-permute-start = (bf16[64,128]{1,0:T(8,128)(2,1)S(1)}, bf16[64,128]{1,0:T(8,128)(2,1)S(1)}, u32[]{:S(2)}, u32[]{:S(2)}) collective-permute-start(bf16[64,128]{1,0:T(8,128)(2,1)S(1)} %slice.34), channel_id=1, source_target_pairs={{0,16},{16,0},{32,48},{48,32},{64,80},{80,64},{96,112},{112,96},{1... | collective-permute-start | bytes 49160 | tf_op jit(solution)/shard_map/ppermute | solution.py:86
  101.0 0.5 fusion.53
  101.5 1.2 collective-permute-done
  102.9 0.5 fusion.4
  103.5 0.5 fusion.19
  104.3 0.8 copy-done
  105.1 0.7 fusion.9
  105.8 14.1 %all_to_all.21 = bf16[16,64,256]{2,1,0:T(8,128)(2,1)S(1)} all-to-all(bf16[16,64,256]{2,1,0:T(8,128)(2,1)S(1)} %fusion.9), channel_id=1, replica_groups=mesh['row'=16,'col'=16] {'row'}, dimensions={0} | all-to-all | bytes 1048576 | tf_op jit(solution)/shard_map/all_to_all | solution.py:30
  119.9 0.7 reduce_sum.62
  (40 shorter events, 3.0 us)
Async XLA Ops:
  6.5 49.0 %all-gather.2.cloned.1.call-start = ((), (), s32[]{:S(2)}) async-start(), calls=%async_computation.4 | async-start | bytes 5570560 | tf_op jit(solution)/shard_map/all_gather | solution.py:58
  9.8 13.6 %all-to-all-start.1 = ((f32[16,1,64]{2,1,0:T(1,128)}), f32[16,1,64]{2,1,0:T(1,128)S(1)}, u32[]{:S(2)}, u32[]{:S(2)}) async-start(f32[16,1,64]{2,1,0:T(1,128)} %broadcast_in_dim.59), calls=%async_computation.1 | async-start | bytes 16384 | tf_op jit(solution)/shard_map/all_to_all | solution.py:37
  25.3 5.1 %copy-start.4 = (bf16[256]{0:T(256)(128)(2,1)S(1)}, bf16[256]{0:T(256)(128)(2,1)}, u32[]{:S(2)}) copy-start(bf16[256]{0:T(256)(128)(2,1)} %param.9) | copy-start | bytes 1540
  25.3 30.3 %copy-start.2 = (bf16[64,256]{1,0:T(8,128)(2,1)S(1)}, bf16[64,256]{1,0:T(8,128)(2,1)}, u32[]{:S(2)}) copy-start(bf16[64,256]{1,0:T(8,128)(2,1)} %param.8) | copy-start | bytes 98308
  25.3 36.1 %all-to-all-start = ((bf16[16,2,256,128]{3,2,1,0:T(8,128)(2,1)}), bf16[16,2,256,128]{3,2,1,0:T(8,128)(2,1)S(1)}, u32[]{:S(2)}, u32[]{:S(2)}) async-start(bf16[16,2,256,128]{3,2,1,0:T(8,128)(2,1)} %bitcast.106), calls=%async_computation | async-start | bytes 4194304 | tf_op jit(solution)/shard_map/all_to_all | solution.py:69
  66.4 7.4 %copy-start.3 = (s32[1,64]{1,0:T(1,128)S(1)}, s32[1,64]{1,0:T(1,128)}, u32[]{:S(2)}) copy-start(s32[1,64]{1,0:T(1,128)} %param.15) | copy-start | bytes 772
  66.4 29.4 %all-to-all-start.2 = ((f32[16,64,384]{2,1,0:T(8,128)}), f32[16,64,384]{2,1,0:T(8,128)}, u32[]{:S(2)}, u32[]{:S(2)}) async-start(f32[16,64,384]{2,1,0:T(8,128)} %copy.62), calls=%async_computation.2 | async-start | bytes 3145728 | tf_op jit(solution)/shard_map/all_to_all | solution.py:82
  97.3 5.4 %collective-permute-start = (bf16[64,128]{1,0:T(8,128)(2,1)S(1)}, bf16[64,128]{1,0:T(8,128)(2,1)S(1)}, u32[]{:S(2)}, u32[]{:S(2)}) collective-permute-start(bf16[64,128]{1,0:T(8,128)(2,1)S(1)} %slice.34), channel_id=1, source_target_pairs={{0,16},{16,0},{32,48},{48,32},{64,80},{80,64},{96,112},{112,96},{1... | collective-permute-start | bytes 49160 | tf_op jit(solution)/shard_map/ppermute | solution.py:86
  101.0 2.5 %copy-start.1 = (bf16[16,1,256,128]{3,2,1,0:T(8,128)(2,1)S(1)}, bf16[16,1,256,128]{3,2,1,0:T(8,128)(2,1)}, u32[]{:S(2)}) copy-start(bf16[16,1,256,128]{3,2,1,0:T(8,128)(2,1)} %get-tuple-element.10) | copy-start | bytes 3145732
  103.5 1.6 %copy-start = (bf16[256,16,256]{0,2,1:T(8,128)(2,1)S(1)}, bf16[256,16,256]{0,2,1:T(8,128)(2,1)}, u32[]{:S(2)}) copy-start(bf16[256,16,256]{0,2,1:T(8,128)(2,1)} %copy.68) | copy-start | bytes 6291460
Sparse Core Ops, SparseCore 0:
  9.1 46.3 all-gather.1

commit v18 on v17

--- a/solution.py
+++ b/solution.py
@@ -79,7 +79,14 @@
         .reshape(rows_here, row_count, -1)
     )
     owned = jnp.concatenate([query_part, pair_part], axis=2).transpose(1, 0, 2)
-    summed = jnp.sum(lax.all_to_all(owned, "row", 0, 0), axis=0).astype(jnp.bfloat16)
+    side = 4
+    along_x = [[y * side + x for x in range(side)] for y in range(side)]
+    along_y = [[y * side + x for y in range(side)] for x in range(side)]
+    owned = owned.reshape(side, side, rows_here, -1)
+    first = lax.all_to_all(owned, "row", 1, 1, axis_index_groups=along_x)
+    first = jnp.sum(first, axis=1)
+    second = lax.all_to_all(first, "row", 0, 0, axis_index_groups=along_y)
+    summed = jnp.sum(second, axis=0).astype(jnp.bfloat16)
     query_mine = summed[:, : heads_dev * HEAD_SIZE]
     pair_mine = summed[:, heads_dev * HEAD_SIZE :]
     partner = [(i, i ^ 1) for i in range(row_count)]

time: 128 us -> 135 us (1.055)
  waiting for transfers between devices: 40.3 us -> 46.4 us
    all_to_all x1 -> x2, waiting for transfers between devices: 9.69 us -> 15.3 us  [the longest x1 8.9 us: shards(): first = lax.all_to_all(owned, 'row', 1, 1, axis_index_groups=along_x)]
    reshape x0 -> x1, local copies, waits for them, and re-layouts: none -> 2.16 us  [shards(): owned = owned.reshape(side, side, rows_here, -1)]
    ppermute x1, starting transfers between devices: 3.63 us -> 1.55 us  [shards(): pair_theirs = lax.ppermute(pair_mine, 'row', partner)]
    all_to_all x1 -> x2, starting transfers between devices: 7.41 us -> 9.27 us  [the longest x1 4.99 us: shards(): first = lax.all_to_all(owned, 'row', 1, 1, axis_index_groups=along_x)]
    unnamed x17 -> x19, local copies, waits for them, and re-layouts: 8.28 us -> 7.53 us
  transfers between devices with their start and end apart: 5 -> 6, of which waited for: 4 -> 5; matrix products, arithmetic and copies ran while one was open for 18% -> 17% of each run, Pallas kernels for 0% -> 0%
where the time goes in v18:
time: 135 us
  waiting for transfers between devices  46.4 us (34%)
  starting transfers between devices  23.4 us (17%)
  local copies, waits for them, and re-layouts  22.8 us (17%)
  between operations  14.3 us (11%)
  blocking collectives  13.1 us (10%)
  matrix products  7.37 us (5%)
  other arithmetic  7.26 us (5%)
    all_gather x1, waiting for transfers between devices, shards(): lax.all_gather(jnp.concatenate([w_qkv, w_out], axis=1), 'col', axis=1, ti...  25 us
    all_to_all x1, blocking collectives, row_reduce(): received = lax.all_to_all(pieces, axis_name, 0, 0)  13.1 us
    all_to_all x1, waiting for transfers between devices, shards(): first = lax.all_to_all(owned, 'row', 1, 1, axis_index_groups=along_x)  8.9 us
    unnamed x19, local copies, waits for them, and re-layouts  7.53 us
    all_to_all x1, starting transfers between devices, row_gather(): return lax.all_to_all(copies, axis_name, 0, 0)  7.48 us
    all_to_all x1, waiting for transfers between devices, shards(): second = lax.all_to_all(first, 'row', 0, 0, axis_index_groups=along_y)  6.44 us
    slice x2, local copies, waits for them, and re-layouts, shards(): weights_all.reshape(w_out.shape[0], col_count, -1)[:, :, qkv_width:]  5.78 us
    all_to_all x1, starting transfers between devices, shards(): by_head = lax.all_to_all(pieces, 'row', 0, 0)  5.1 us
  transfers between devices with their start and end apart: 6, of which 5 were waited for; matrix products, arithmetic and copies ran while one was open for 17% of the time, Pallas kernels for 0%

profile of v18, /device:TPU:2, one launch (start us, length us, event | category | flops | bytes accessed | tf_op | source)
XLA Modules:
  0.0 134.6 jit_solution(7198953140066685788)
XLA Ops:
  6.5 1.7 %pad_maximum_fusion.1 = bf16[256,640]{1,0:T(8,128)(2,1)} fusion(bf16[256,256]{1,0:T(8,128)(2,1)} %param.11, bf16[256,384]{1,0:T(8,128)(2,1)} %param.10), kind=kLoop, calls=%fused_computation.33 | loop fusion | flops 655360 | bytes 655360 | tf_op jit(solution)/shard_map/concatenate | solution.py:58
  8.3 0.9 fusion.24
  9.2 0.6 broadcast_in_dim.59
  9.8 7.5 %all-to-all-start.1 = ((f32[16,1,64]{2,1,0:T(1,128)}), f32[16,1,64]{2,1,0:T(1,128)S(1)}, u32[]{:S(2)}, u32[]{:S(2)}) async-start(f32[16,1,64]{2,1,0:T(1,128)} %broadcast_in_dim.59), calls=%async_computation.1 | async-start | bytes 16384 | tf_op jit(solution)/shard_map/all_to_all | solution.py:37
  17.3 1.3 pad_maximum_fusion
  19.1 4.3 %all-to-all-done.1 = f32[16,1,64]{2,1,0:T(1,128)S(1)} async-done(((f32[16,1,64]{2,1,0:T(1,128)}), f32[16,1,64]{2,1,0:T(1,128)S(1)}, u32[]{:S(2)}, u32[]{:S(2)}) %all-to-all-start.1) | async-done | bytes 4128 | tf_op jit(solution)/shard_map/all_to_all | solution.py:37
  23.4 2.0 %broadcast_in_dim.58 = bf16[8,2,2,256,128]{4,3,2,1,0:T(8,128)(2,1)} broadcast(bf16[8,2,256,128]{3,2,1,0:T(8,128)(2,1)S(1)} %copy.88), dimensions={0,2,3,4} | broadcast | bytes 3145728 | tf_op jit(solution)/shard_map/broadcast_in_dim | solution.py:68
  25.4 5.1 %all-to-all-start = ((bf16[16,2,256,128]{3,2,1,0:T(8,128)(2,1)}), bf16[16,2,256,128]{3,2,1,0:T(8,128)(2,1)S(1)}, u32[]{:S(2)}, u32[]{:S(2)}) async-start(bf16[16,2,256,128]{3,2,1,0:T(8,128)(2,1)} %bitcast.107), calls=%async_computation | async-start | bytes 4194304 | tf_op jit(solution)/shard_map/all_to_all | solution.py:69
  30.5 25.0 %all-gather.2.cloned.1.call-done = bf16[256,10240]{1,0:T(8,128)(2,1)} async-done(((bf16[256,640]{1,0:T(8,128)(2,1)}), bf16[256,10240]{1,0:T(8,128)(2,1)}) %all-gather.2.cloned.1.call-update) | async-done | bytes 5242896 | tf_op jit(solution)/shard_map/all_gather | solution.py:58
  55.5 3.6 %fusion.30 = f32[64,10240]{1,0:T(8,128)S(1)} fusion(bf16[256,10240]{1,0:T(8,128)(2,1)} %all-gather.2.cloned.1.call-done, bf16[64,256]{1,0:T(8,128)(2,1)S(1)} %copy-done.3, f32[256]{0:T(256)S(1)} %convert_element_type.87, f32[64]{0:T(128)S(1)} %add_rsqrt_fusion), kind=kOutput, calls=%fused_computation.44 | convolution fusion | flops 335609856 | bytes 7898368 | tf_op jit(solution)/shard_map/dot_general | solution.py:60
  59.7 1.7 %copy.107 = f32[8,8,16,384]{3,1,2,0:T(8,128)} copy(f32[8,8,16,384]{3,2,1,0:T(8,128)S(1)} %bitcast.111) | data formatting | bytes 3145728
  61.4 1.3 slice.26
  62.7 1.1 slice_bitcast_fusion
  65.3 2.2 %copy.93 = f32[4,4,64,384]{3,0,2,1:T(4,128)} copy(f32[4,4,64,384]{3,2,1,0:T(8,128)S(1)} %bitcast.112) | data formatting | bytes 3145728 | tf_op jit(solution)/shard_map/reshape | solution.py:85
  67.5 5.0 %all-to-all-start.2 = ((f32[4,4,64,384]{3,0,2,1:T(4,128)}), f32[4,4,64,384]{3,0,2,1:T(4,128)}, u32[]{:S(2)}, u32[]{:S(2)}) async-start(f32[4,4,64,384]{3,0,2,1:T(4,128)} %copy.93), calls=%async_computation.2 | async-start | bytes 3145728 | tf_op jit(solution)/shard_map/all_to_all | solution.py:86
  74.2 3.6 %copy.110 = bf16[32,8,16,640]{3,2,1,0:T(8,128)(2,1)S(1)} copy(bf16[32,8,16,640]{3,1,2,0:T(8,128)(2,1)} %bitcast.104) | data formatting | bytes 10485760
  77.8 1.5 %slice.35 = bf16[256,16,256]{2,1,0:T(8,128)(2,1)} slice(bf16[256,16,640]{2,1,0:T(8,128)(2,1)S(1)} %bitcast.106), slice={[0:256], [0:16], [384:640]} | slice | bytes 4194304 | tf_op jit(solution)/shard_map/slice | solution.py:122
  79.3 4.3 %copy.101 = bf16[256,16,256]{0,2,1:T(8,128)(2,1)} copy(bf16[256,16,256]{2,1,0:T(8,128)(2,1)} %slice.35) | data formatting | bytes 4194304 | tf_op jit(solution)/shard_map/slice | solution.py:122
  83.6 8.9 %all-to-all-done.2 = f32[4,4,64,384]{3,0,2,1:T(4,128)} async-done(((f32[4,4,64,384]{3,0,2,1:T(4,128)}), f32[4,4,64,384]{3,0,2,1:T(4,128)}, u32[]{:S(2)}, u32[]{:S(2)}) %all-to-all-start.2) | async-done | bytes 1572896 | tf_op jit(solution)/shard_map/all_to_all | solution.py:86
  92.5 1.8 %reduce_sum.68 = f32[4,64,384]{2,0,1:T(4,128)S(1)} reduce(f32[4,4,64,384]{3,0,2,1:T(4,128)} %all-to-all-done.2, f32[]{:T(128)} %constant.11.clone.1), dimensions={1}, to_apply=%region_2.0 | reduce | flops 294912 | bytes 1966084 | tf_op jit(solution)/shard_map/reduce_sum | solution.py:87
  94.3 0.8 copy.95
  95.1 4.3 %all-to-all-start.3 = ((f32[4,64,384]{2,1,0:T(8,128)}), f32[4,64,384]{2,1,0:T(8,128)S(1)}, u32[]{:S(2)}, u32[]{:S(2)}) async-start(f32[4,64,384]{2,1,0:T(8,128)} %copy.95), calls=%async_computation.3 | async-start | bytes 786432 | tf_op jit(solution)/shard_map/all_to_all | solution.py:88
  99.3 1.2 fusion.52
  100.5 6.4 %all-to-all-done.3 = f32[4,64,384]{2,1,0:T(8,128)S(1)} async-done(((f32[4,64,384]{2,1,0:T(8,128)}), f32[4,64,384]{2,1,0:T(8,128)S(1)}, u32[]{:S(2)}, u32[]{:S(2)}) %all-to-all-start.3) | async-done | bytes 393248 | tf_op jit(solution)/shard_map/all_to_all | solution.py:88
  107.0 1.5 %collective-permute-start = (bf16[64,128]{1,0:T(8,128)(2,1)S(1)}, bf16[64,128]{1,0:T(8,128)(2,1)S(1)}, u32[]{:S(2)}, u32[]{:S(2)}) collective-permute-start(bf16[64,128]{1,0:T(8,128)(2,1)S(1)} %slice.34), channel_id=1, source_target_pairs={{0,16},{16,0},{32,48},{48,32},{64,80},{80,64},{96,112},{112,96},{1... | collective-permute-start | bytes 49160 | tf_op jit(solution)/shard_map/ppermute | solution.py:93
  109.1 1.8 %collective-permute-done = bf16[64,128]{1,0:T(8,128)(2,1)S(1)} collective-permute-done((bf16[64,128]{1,0:T(8,128)(2,1)S(1)}, bf16[64,128]{1,0:T(8,128)(2,1)S(1)}, u32[]{:S(2)}, u32[]{:S(2)}) %collective-permute-start) | collective-permute-done | bytes 16416 | tf_op jit(solution)/shard_map/ppermute | solution.py:93
  111.1 0.5 fusion.4
  111.6 0.5 fusion.19
  112.2 1.0 fusion.16
  113.2 0.7 fusion.9
  114.0 13.1 %all_to_all.26 = bf16[16,64,256]{2,1,0:T(8,128)(2,1)S(1)} all-to-all(bf16[16,64,256]{2,1,0:T(8,128)(2,1)S(1)} %fusion.9), channel_id=1, replica_groups=mesh['row'=16,'col'=16] {'row'}, dimensions={0} | all-to-all | bytes 1048576 | tf_op jit(solution)/shard_map/all_to_all | solution.py:30
  127.1 0.7 reduce_sum.72
  (47 shorter events, 4.6 us)
Async XLA Ops:
  6.5 49.0 %all-gather.2.cloned.1.call-start = ((), (), s32[]{:S(2)}) async-start(), calls=%async_computation.5 | async-start | bytes 5570560 | tf_op jit(solution)/shard_map/all_gather | solution.py:58
  9.8 13.6 %all-to-all-start.1 = ((f32[16,1,64]{2,1,0:T(1,128)}), f32[16,1,64]{2,1,0:T(1,128)S(1)}, u32[]{:S(2)}, u32[]{:S(2)}) async-start(f32[16,1,64]{2,1,0:T(1,128)} %broadcast_in_dim.59), calls=%async_computation.1 | async-start | bytes 16384 | tf_op jit(solution)/shard_map/all_to_all | solution.py:37
  25.4 5.1 %copy-start.5 = (bf16[256]{0:T(256)(128)(2,1)S(1)}, bf16[256]{0:T(256)(128)(2,1)}, u32[]{:S(2)}) copy-start(bf16[256]{0:T(256)(128)(2,1)} %param.9) | copy-start | bytes 1540
  25.4 30.1 %copy-start.3 = (bf16[64,256]{1,0:T(8,128)(2,1)S(1)}, bf16[64,256]{1,0:T(8,128)(2,1)}, u32[]{:S(2)}) copy-start(bf16[64,256]{1,0:T(8,128)(2,1)} %param.8) | copy-start | bytes 98308
  25.4 36.0 %all-to-all-start = ((bf16[16,2,256,128]{3,2,1,0:T(8,128)(2,1)}), bf16[16,2,256,128]{3,2,1,0:T(8,128)(2,1)S(1)}, u32[]{:S(2)}, u32[]{:S(2)}) async-start(bf16[16,2,256,128]{3,2,1,0:T(8,128)(2,1)} %bitcast.107), calls=%async_computation | async-start | bytes 4194304 | tf_op jit(solution)/shard_map/all_to_all | solution.py:69
  67.5 5.0 %copy-start.4 = (s32[1,64]{1,0:T(1,128)S(1)}, s32[1,64]{1,0:T(1,128)}, u32[]{:S(2)}) copy-start(s32[1,64]{1,0:T(1,128)} %param.15) | copy-start | bytes 772
  67.5 25.0 %all-to-all-start.2 = ((f32[4,4,64,384]{3,0,2,1:T(4,128)}), f32[4,4,64,384]{3,0,2,1:T(4,128)}, u32[]{:S(2)}, u32[]{:S(2)}) async-start(f32[4,4,64,384]{3,0,2,1:T(4,128)} %copy.93), calls=%async_computation.2 | async-start | bytes 3145728 | tf_op jit(solution)/shard_map/all_to_all | solution.py:86
  95.1 11.9 %all-to-all-start.3 = ((f32[4,64,384]{2,1,0:T(8,128)}), f32[4,64,384]{2,1,0:T(8,128)S(1)}, u32[]{:S(2)}, u32[]{:S(2)}) async-start(f32[4,64,384]{2,1,0:T(8,128)} %copy.95), calls=%async_computation.3 | async-start | bytes 786432 | tf_op jit(solution)/shard_map/all_to_all | solution.py:88
  107.0 4.1 %copy-start.2 = (bf16[64,384]{1,0:T(8,128)(2,1)}, bf16[64,384]{1,0:T(8,128)(2,1)S(1)}, u32[]{:S(2)}) copy-start(bf16[64,384]{1,0:T(8,128)(2,1)S(1)} %reduce_sum.69) | copy-start | bytes 147460
  107.0 3.8 %collective-permute-start = (bf16[64,128]{1,0:T(8,128)(2,1)S(1)}, bf16[64,128]{1,0:T(8,128)(2,1)S(1)}, u32[]{:S(2)}, u32[]{:S(2)}) collective-permute-start(bf16[64,128]{1,0:T(8,128)(2,1)S(1)} %slice.34), channel_id=1, source_target_pairs={{0,16},{16,0},{32,48},{48,32},{64,80},{80,64},{96,112},{112,96},{1... | collective-permute-start | bytes 49160 | tf_op jit(solution)/shard_map/ppermute | solution.py:93
  108.5 3.1 %copy-start.1 = (bf16[16,1,256,128]{3,2,1,0:T(8,128)(2,1)S(1)}, bf16[16,1,256,128]{3,2,1,0:T(8,128)(2,1)}, u32[]{:S(2)}) copy-start(bf16[16,1,256,128]{3,2,1,0:T(8,128)(2,1)} %get-tuple-element.10) | copy-start | bytes 3145732
  111.6 1.6 %copy-start = (bf16[256,16,256]{0,2,1:T(8,128)(2,1)S(1)}, bf16[256,16,256]{0,2,1:T(8,128)(2,1)}, u32[]{:S(2)}) copy-start(bf16[256,16,256]{0,2,1:T(8,128)(2,1)} %copy.101) | copy-start | bytes 6291460
Sparse Core Ops, SparseCore 0:
  9.1 46.3 all-gather.1

commit v19 on v17

--- a/solution.py
+++ b/solution.py
@@ -101,15 +101,26 @@
         * score_scale
     )
     tree_scores = jnp.where(allowed, tree_scores, masked_score)
-    highest = jnp.maximum(jnp.max(scores, axis=-1), jnp.max(tree_scores, axis=-1))
-    weights = jnp.where(visible, jnp.exp(scores - highest[..., None]), 0.0)
-    tree_weights = jnp.where(allowed, jnp.exp(tree_scores - highest[..., None]), 0.0)
-    totals = jnp.sum(weights, axis=-1) + jnp.sum(tree_weights, axis=-1)
-    blended = jnp.einsum(
+    cache_max = jnp.max(scores, axis=-1)
+    weights = jnp.where(visible, jnp.exp(scores - cache_max[..., None]), 0.0)
+    cache_total = jnp.sum(weights, axis=-1)
+    cache_blend = jnp.einsum(
         "htp,pd->htd", weights.astype(jnp.bfloat16), values, preferred_element_type=jnp.float32
-    ) + jnp.einsum(
+    )
+    cache_max, cache_total, cache_blend, tree_scores, value_mine = lax.optimization_barrier(
+        (cache_max, cache_total, cache_blend, tree_scores, value_mine)
+    )
+    tree_max = jnp.max(tree_scores, axis=-1)
+    tree_weights = jnp.where(allowed, jnp.exp(tree_scores - tree_max[..., None]), 0.0)
+    tree_total = jnp.sum(tree_weights, axis=-1)
+    tree_blend = jnp.einsum(
         "hts,sd->htd", tree_weights.astype(jnp.bfloat16), value_mine, preferred_element_type=jnp.float32
     )
+    joint_max = jnp.maximum(cache_max, tree_max)
+    cache_scale = jnp.exp(cache_max - joint_max)
+    tree_scale = jnp.exp(tree_max - joint_max)
+    totals = cache_total * cache_scale + tree_total * tree_scale
+    blended = cache_blend * cache_scale[..., None] + tree_blend * tree_scale[..., None]
     attended = (blended / totals[..., None]).astype(jnp.bfloat16)
     attended = attended.transpose(1, 0, 2).reshape(rows_here, heads_dev * HEAD_SIZE)
     out_all = weights_all.reshape(w_out.shape[0], col_count, -1)[:, :, qkv_width:]

time: 128 us -> 126 us (0.984)
  transfers between devices with their start and end apart: 5 -> 5, of which waited for: 4 -> 4; matrix products, arithmetic and copies ran while one was open for 18% -> 19% of each run, Pallas kernels for 0% -> 0%
where the time goes in v19:
time: 126 us
  waiting for transfers between devices  39.2 us (31%)
  starting transfers between devices  23.6 us (19%)
  local copies, waits for them, and re-layouts  21.3 us (17%)
  between operations  14.3 us (11%)
  blocking collectives  13.7 us (11%)
  other arithmetic  6.99 us (6%)
  matrix products  6.58 us (5%)
    all_gather x1, waiting for transfers between devices, shards(): lax.all_gather(jnp.concatenate([w_qkv, w_out], axis=1), 'col', axis=1, ti...  25.1 us
    all_to_all x1, blocking collectives, row_reduce(): received = lax.all_to_all(pieces, axis_name, 0, 0)  13.7 us
    all_to_all x1, waiting for transfers between devices, shards(): lax.all_to_all(owned, 'row', 0, 0)  9.69 us
    unnamed x17, local copies, waits for them, and re-layouts  7.94 us
    all_to_all x1, starting transfers between devices, row_gather(): return lax.all_to_all(copies, axis_name, 0, 0)  7.48 us
    all_to_all x1, starting transfers between devices, shards(): lax.all_to_all(owned, 'row', 0, 0)  7.41 us
    slice x2, local copies, waits for them, and re-layouts, shards(): weights_all.reshape(w_out.shape[0], col_count, -1)[:, :, qkv_width:]  5.78 us
    all_to_all x1, starting transfers between devices, shards(): by_head = lax.all_to_all(pieces, 'row', 0, 0)  5.1 us
  transfers between devices with their start and end apart: 5, of which 4 were waited for; matrix products, arithmetic and copies ran while one was open for 19% of the time, Pallas kernels for 0%

profile of v19, /device:TPU:2, one launch (start us, length us, event | category | flops | bytes accessed | tf_op | source)
XLA Modules:
  0.0 125.6 jit_solution(13140964346871023235)
XLA Ops:
  6.5 1.7 %pad_maximum_fusion.1 = bf16[256,640]{1,0:T(8,128)(2,1)} fusion(bf16[256,256]{1,0:T(8,128)(2,1)} %param.11, bf16[256,384]{1,0:T(8,128)(2,1)} %param.10), kind=kLoop, calls=%fused_computation.30 | loop fusion | flops 655360 | bytes 655360 | tf_op jit(solution)/shard_map/concatenate | solution.py:58
  8.3 0.9 fusion.21
  9.2 0.6 broadcast_in_dim.60
  9.8 7.5 %all-to-all-start.1 = ((f32[16,1,64]{2,1,0:T(1,128)}), f32[16,1,64]{2,1,0:T(1,128)S(1)}, u32[]{:S(2)}, u32[]{:S(2)}) async-start(f32[16,1,64]{2,1,0:T(1,128)} %broadcast_in_dim.60), calls=%async_computation.1 | async-start | bytes 16384 | tf_op jit(solution)/shard_map/all_to_all | solution.py:37
  17.3 1.3 %pad_maximum_fusion = bf16[2,256,1024]{2,1,0:T(8,128)(2,1)S(1)} fusion(bf16[1,256,1024]{2,1,0:T(8,128)(2,1)} %param.13, bf16[1,256,1024]{2,1,0:T(8,128)(2,1)} %param.12), kind=kLoop, calls=%fused_computation.25 | loop fusion | flops 524288 | bytes 2097152 | tf_op jit(solution)/shard_map/stack | solution.py:65
  19.1 4.3 %all-to-all-done.1 = f32[16,1,64]{2,1,0:T(1,128)S(1)} async-done(((f32[16,1,64]{2,1,0:T(1,128)}), f32[16,1,64]{2,1,0:T(1,128)S(1)}, u32[]{:S(2)}, u32[]{:S(2)}) %all-to-all-start.1) | async-done | bytes 4128 | tf_op jit(solution)/shard_map/all_to_all | solution.py:37
  23.4 1.8 %broadcast_in_dim.59 = bf16[8,2,2,256,128]{4,3,2,1,0:T(8,128)(2,1)} broadcast(bf16[8,2,256,128]{3,2,1,0:T(8,128)(2,1)S(1)} %copy.58), dimensions={0,2,3,4} | broadcast | bytes 3145728 | tf_op jit(solution)/shard_map/broadcast_in_dim | solution.py:68
  25.3 5.1 %all-to-all-start = ((bf16[16,2,256,128]{3,2,1,0:T(8,128)(2,1)}), bf16[16,2,256,128]{3,2,1,0:T(8,128)(2,1)S(1)}, u32[]{:S(2)}, u32[]{:S(2)}) async-start(bf16[16,2,256,128]{3,2,1,0:T(8,128)(2,1)} %bitcast.96), calls=%async_computation | async-start | bytes 4194304 | tf_op jit(solution)/shard_map/all_to_all | solution.py:69
  30.4 25.1 %all-gather.2.cloned.1.call-done = bf16[256,10240]{1,0:T(8,128)(2,1)} async-done(((bf16[256,640]{1,0:T(8,128)(2,1)}), bf16[256,10240]{1,0:T(8,128)(2,1)}) %all-gather.2.cloned.1.call-update) | async-done | bytes 5242896 | tf_op jit(solution)/shard_map/all_gather | solution.py:58
  55.5 3.6 %fusion.32 = f32[64,10240]{1,0:T(8,128)S(1)} fusion(bf16[256,10240]{1,0:T(8,128)(2,1)} %all-gather.2.cloned.1.call-done, bf16[64,256]{1,0:T(8,128)(2,1)S(1)} %copy-done.2, f32[256]{0:T(256)S(1)} %convert_element_type.86, f32[64]{0:T(128)S(1)} %add_rsqrt_fusion), kind=kOutput, calls=%fused_computation.43 | convolution fusion | flops 335609856 | bytes 7898368 | tf_op jit(solution)/shard_map/dot_general | solution.py:60
  59.1 0.5 copy.72
  59.7 1.7 %copy.73 = f32[8,8,16,384]{3,1,2,0:T(8,128)} copy(f32[8,8,16,384]{3,2,1,0:T(8,128)S(1)} %bitcast.100) | data formatting | bytes 3145728
  61.4 1.3 %slice.26 = f32[64,4096]{1,0:T(8,128)S(1)} slice(f32[64,6144]{1,0:T(8,128)} %bitcast.98), slice={[0:64], [0:4096]} | slice | bytes 2097152 | tf_op jit(solution)/shard_map/slice | solution.py:74
  62.7 1.1 slice_bitcast_fusion
  63.8 0.3 copy.74
  64.4 0.3 copy.61
  64.8 1.6 %copy.62 = f32[16,64,384]{2,1,0:T(8,128)} copy(f32[16,64,384]{2,0,1:T(8,128)S(1)} %maximum_bitcast_fusion) | data formatting | bytes 3145728 | tf_op jit(solution)/shard_map/transpose | solution.py:81
  66.4 7.4 %all-to-all-start.2 = ((f32[16,64,384]{2,1,0:T(8,128)}), f32[16,64,384]{2,1,0:T(8,128)}, u32[]{:S(2)}, u32[]{:S(2)}) async-start(f32[16,64,384]{2,1,0:T(8,128)} %copy.62), calls=%async_computation.2 | async-start | bytes 3145728 | tf_op jit(solution)/shard_map/all_to_all | solution.py:82
  75.6 3.6 %copy.76 = bf16[32,8,16,640]{3,2,1,0:T(8,128)(2,1)S(1)} copy(bf16[32,8,16,640]{3,1,2,0:T(8,128)(2,1)} %bitcast.93) | data formatting | bytes 10485760
  79.2 1.5 %slice.35 = bf16[256,16,256]{2,1,0:T(8,128)(2,1)} slice(bf16[256,16,640]{2,1,0:T(8,128)(2,1)S(1)} %bitcast.95), slice={[0:256], [0:16], [384:640]} | slice | bytes 4194304 | tf_op jit(solution)/shard_map/slice | solution.py:126
  80.7 4.3 %copy.68 = bf16[256,16,256]{0,2,1:T(8,128)(2,1)} copy(bf16[256,16,256]{2,1,0:T(8,128)(2,1)} %slice.35) | data formatting | bytes 4194304 | tf_op jit(solution)/shard_map/slice | solution.py:126
  85.0 1.2 fusion.55
  86.2 9.7 %all-to-all-done.2 = f32[16,64,384]{2,1,0:T(8,128)} async-done(((f32[16,64,384]{2,1,0:T(8,128)}), f32[16,64,384]{2,1,0:T(8,128)}, u32[]{:S(2)}, u32[]{:S(2)}) %all-to-all-start.2) | async-done | bytes 1572896 | tf_op jit(solution)/shard_map/all_to_all | solution.py:82
  95.8 1.5 %reduce_sum.59 = bf16[64,384]{1,0:T(8,128)(2,1)S(1)} reduce(f32[16,64,384]{2,1,0:T(8,128)} %all-to-all-done.2, f32[]{:T(128)} %constant.11.clone.1), dimensions={0}, to_apply=%region_2.0 | reduce | flops 368640 | bytes 1622020 | tf_op jit(solution)/shard_map/reduce_sum | solution.py:82
  97.3 3.6 %collective-permute-start = (bf16[64,128]{1,0:T(8,128)(2,1)S(1)}, bf16[64,128]{1,0:T(8,128)(2,1)S(1)}, u32[]{:S(2)}, u32[]{:S(2)}) collective-permute-start(bf16[64,128]{1,0:T(8,128)(2,1)S(1)} %slice.34), channel_id=1, source_target_pairs={{0,16},{16,0},{32,48},{48,32},{64,80},{80,64},{96,112},{112,96},{1... | collective-permute-start | bytes 49160 | tf_op jit(solution)/shard_map/ppermute | solution.py:86
  101.0 0.5 fusion.56
  101.5 0.5 fusion.16
  102.1 0.5 fusion.5
  103.2 0.4 copy-done
  103.7 0.8 fusion.9
  104.4 13.7 %all_to_all.21 = bf16[16,64,256]{2,1,0:T(8,128)(2,1)S(1)} all-to-all(bf16[16,64,256]{2,1,0:T(8,128)(2,1)S(1)} %fusion.9), channel_id=1, replica_groups=mesh['row'=16,'col'=16] {'row'}, dimensions={0} | all-to-all | bytes 1048576 | tf_op jit(solution)/shard_map/all_to_all | solution.py:30
  118.1 0.7 reduce_sum.62
  (41 shorter events, 2.8 us)
Async XLA Ops:
  6.5 49.0 %all-gather.2.cloned.1.call-start = ((), (), s32[]{:S(2)}) async-start(), calls=%async_computation.4 | async-start | bytes 5570560 | tf_op jit(solution)/shard_map/all_gather | solution.py:58
  9.8 13.6 %all-to-all-start.1 = ((f32[16,1,64]{2,1,0:T(1,128)}), f32[16,1,64]{2,1,0:T(1,128)S(1)}, u32[]{:S(2)}, u32[]{:S(2)}) async-start(f32[16,1,64]{2,1,0:T(1,128)} %broadcast_in_dim.60), calls=%async_computation.1 | async-start | bytes 16384 | tf_op jit(solution)/shard_map/all_to_all | solution.py:37
  25.3 5.1 %copy-start.4 = (bf16[256]{0:T(256)(128)(2,1)S(1)}, bf16[256]{0:T(256)(128)(2,1)}, u32[]{:S(2)}) copy-start(bf16[256]{0:T(256)(128)(2,1)} %param.9) | copy-start | bytes 1540
  25.3 30.3 %copy-start.2 = (bf16[64,256]{1,0:T(8,128)(2,1)S(1)}, bf16[64,256]{1,0:T(8,128)(2,1)}, u32[]{:S(2)}) copy-start(bf16[64,256]{1,0:T(8,128)(2,1)} %param.8) | copy-start | bytes 98308
  25.3 36.1 %all-to-all-start = ((bf16[16,2,256,128]{3,2,1,0:T(8,128)(2,1)}), bf16[16,2,256,128]{3,2,1,0:T(8,128)(2,1)S(1)}, u32[]{:S(2)}, u32[]{:S(2)}) async-start(bf16[16,2,256,128]{3,2,1,0:T(8,128)(2,1)} %bitcast.96), calls=%async_computation | async-start | bytes 4194304 | tf_op jit(solution)/shard_map/all_to_all | solution.py:69
  66.4 7.4 %copy-start.3 = (s32[1,64]{1,0:T(1,128)S(1)}, s32[1,64]{1,0:T(1,128)}, u32[]{:S(2)}) copy-start(s32[1,64]{1,0:T(1,128)} %param.15) | copy-start | bytes 772
  66.4 29.4 %all-to-all-start.2 = ((f32[16,64,384]{2,1,0:T(8,128)}), f32[16,64,384]{2,1,0:T(8,128)}, u32[]{:S(2)}, u32[]{:S(2)}) async-start(f32[16,64,384]{2,1,0:T(8,128)} %copy.62), calls=%async_computation.2 | async-start | bytes 3145728 | tf_op jit(solution)/shard_map/all_to_all | solution.py:82
  86.2 15.4 %copy-start.1 = (bf16[16,1,256,128]{3,2,1,0:T(8,128)(2,1)S(1)}, bf16[16,1,256,128]{3,2,1,0:T(8,128)(2,1)}, u32[]{:S(2)}) copy-start(bf16[16,1,256,128]{3,2,1,0:T(8,128)(2,1)} %get-tuple-element.22) | copy-start | bytes 3145732
  97.3 5.4 %collective-permute-start = (bf16[64,128]{1,0:T(8,128)(2,1)S(1)}, bf16[64,128]{1,0:T(8,128)(2,1)S(1)}, u32[]{:S(2)}, u32[]{:S(2)}) collective-permute-start(bf16[64,128]{1,0:T(8,128)(2,1)S(1)} %slice.34), channel_id=1, source_target_pairs={{0,16},{16,0},{32,48},{48,32},{64,80},{80,64},{96,112},{112,96},{1... | collective-permute-start | bytes 49160 | tf_op jit(solution)/shard_map/ppermute | solution.py:86
  102.1 1.6 %copy-start = (bf16[256,16,256]{0,2,1:T(8,128)(2,1)S(1)}, bf16[256,16,256]{0,2,1:T(8,128)(2,1)}, u32[]{:S(2)}) copy-start(bf16[256,16,256]{0,2,1:T(8,128)(2,1)} %copy.68) | copy-start | bytes 6291460
Sparse Core Ops, SparseCore 0:
  9.1 46.3 all-gather.1

commit v20 on v19

--- a/solution.py
+++ b/solution.py
@@ -55,12 +55,10 @@
     )
     qkv_width = w_qkv.shape[1]
     col_count = lax.axis_size("col")
-    weights_all = lax.all_gather(jnp.concatenate([w_qkv, w_out], axis=1), "col", axis=1, tiled=True)
+    out_padded = jnp.pad(w_out, ((0, 0), (0, qkv_width - w_out.shape[1])))
+    weights_all = lax.all_gather(jnp.stack([w_qkv, out_padded]), "col", axis=2, tiled=True)
     weights_all = lax.optimization_barrier(weights_all)
-    partial_all = jnp.dot(
-        normed, weights_all, preferred_element_type=jnp.float32
-    ).reshape(rows_here, col_count, -1)
-    partial_value = partial_all[:, :, :qkv_width].reshape(rows_here, col_count * qkv_width)
+    partial_value = jnp.dot(normed, weights_all[0], preferred_element_type=jnp.float32)
 
     local = jnp.stack([cache_k[0], value_cache[0]]).reshape(
         2, token_positions, KEY_VALUE_HEADS, HEAD_SIZE
@@ -123,7 +121,7 @@
     blended = cache_blend * cache_scale[..., None] + tree_blend * tree_scale[..., None]
     attended = (blended / totals[..., None]).astype(jnp.bfloat16)
     attended = attended.transpose(1, 0, 2).reshape(rows_here, heads_dev * HEAD_SIZE)
-    out_all = weights_all.reshape(w_out.shape[0], col_count, -1)[:, :, qkv_width:]
+    out_all = weights_all[1].reshape(w_out.shape[0], col_count, -1)[:, :, : w_out.shape[1]]
     partial_out = jnp.dot(
         attended, out_all.reshape(w_out.shape[0], -1), preferred_element_type=jnp.float32
     )

time: 126 us -> 127 us (level)
  local copies, waits for them, and re-layouts: 21.3 us -> 16.4 us
  waiting for transfers between devices: 39.2 us -> 42.9 us
    unnamed x17 -> x14, local copies, waits for them, and re-layouts: 7.94 us -> 2.53 us
    all_gather x1, waiting for transfers between devices: 25.1 us -> 27.8 us  [shards(): lax.all_gather(jnp.stack([w_qkv, out_padded]), 'col', axis=2, tiled=True)]
    transpose x2 -> x0, local copies, waits for them, and re-layouts: 1.8 us -> none  [the longest x1 1.63 us: shards(): owned = jnp.concatenate([query_part, pair_part], axis=2).transpose(1, 0, 2)]
    slice x3 -> x4, local copies, waits for them, and re-layouts: 5.89 us -> 7.67 us  [shards(): weights_all[1].reshape(w_out.shape[0], col_count, -1)[:, :, :w_out.shape[1]]]
    another operation x0 -> x1, other arithmetic: none -> 1.77 us  [shards(): jnp.stack([w_qkv, out_padded])]
    concatenate x1 -> x0, other arithmetic: 1.74 us -> none  [shards(): jnp.concatenate([w_qkv, w_out], axis=1)]
  transfers between devices with their start and end apart: 5 -> 5, of which waited for: 4 -> 4; matrix products, arithmetic and copies ran while one was open for 19% -> 15% of each run, Pallas kernels for 0% -> 0%
where the time goes in v20:
time: 127 us; the launch traced here: 126 us
  waiting for transfers between devices  42.9 us (34%)
  starting transfers between devices  23.6 us (19%)
  local copies, waits for them, and re-layouts  16.4 us (13%)
  between operations  14.3 us (11%)
  blocking collectives  13.7 us (11%)
  other arithmetic  8.26 us (7%)
  matrix products  6.85 us (5%)
    all_gather x1, waiting for transfers between devices, shards(): lax.all_gather(jnp.stack([w_qkv, out_padded]), 'col', axis=2, tiled=True)  27.8 us
    all_to_all x1, blocking collectives, row_reduce(): received = lax.all_to_all(pieces, axis_name, 0, 0)  13.7 us
    all_to_all x1, waiting for transfers between devices, shards(): lax.all_to_all(owned, 'row', 0, 0)  10.7 us
    slice x4, local copies, waits for them, and re-layouts, shards(): weights_all[1].reshape(w_out.shape[0], col_count, -1)[:, :, :w_out.shape[1]]  7.67 us
    all_to_all x1, starting transfers between devices, row_gather(): return lax.all_to_all(copies, axis_name, 0, 0)  7.48 us
    all_to_all x1, starting transfers between devices, shards(): lax.all_to_all(owned, 'row', 0, 0)  7.42 us
    all_to_all x1, starting transfers between devices, shards(): by_head = lax.all_to_all(pieces, 'row', 0, 0)  5.1 us
    all_to_all x1, waiting for transfers between devices, row_gather(): return lax.all_to_all(copies, axis_name, 0, 0)  4.29 us
  transfers between devices with their start and end apart: 5, of which 4 were waited for; matrix products, arithmetic and copies ran while one was open for 15% of the time, Pallas kernels for 0%

profile of v20, /device:TPU:2, one launch (start us, length us, event | category | flops | bytes accessed | tf_op | source)
XLA Modules:
  0.0 125.9 jit_solution(176477066593047376)
XLA Ops:
  6.5 0.9 pad_bitcast_fusion
  7.5 1.8 %pad_maximum_fusion.1 = bf16[2,256,384]{2,1,0:T(8,128)(2,1)} fusion(bf16[1,256,384]{2,1,0:T(8,128)(2,1)S(1)} %pad_bitcast_fusion, bf16[1,256,384]{2,1,0:T(8,128)(2,1)} %bitcast.109), kind=kLoop, calls=%fused_computation.33 | loop fusion | flops 196608 | bytes 786432 | tf_op jit(solution)/shard_map/stack | solution.py:59
  9.3 0.9 fusion.22
  10.1 0.6 broadcast_in_dim.60
  10.7 7.5 %all-to-all-start.1 = ((f32[16,1,64]{2,1,0:T(1,128)}), f32[16,1,64]{2,1,0:T(1,128)S(1)}, u32[]{:S(2)}, u32[]{:S(2)}) async-start(f32[16,1,64]{2,1,0:T(1,128)} %broadcast_in_dim.60), calls=%async_computation.1 | async-start | bytes 16384 | tf_op jit(solution)/shard_map/all_to_all | solution.py:37
  18.2 1.3 %pad_maximum_fusion = bf16[2,256,1024]{2,1,0:T(8,128)(2,1)S(1)} fusion(bf16[1,256,1024]{2,1,0:T(8,128)(2,1)} %param.13, bf16[1,256,1024]{2,1,0:T(8,128)(2,1)} %param.12), kind=kLoop, calls=%fused_computation.28 | loop fusion | flops 524288 | bytes 2097152 | tf_op jit(solution)/shard_map/stack | solution.py:63
  19.5 0.3 copy.53
  19.9 0.2 copy.40
  20.1 4.3 %all-to-all-done.1 = f32[16,1,64]{2,1,0:T(1,128)S(1)} async-done(((f32[16,1,64]{2,1,0:T(1,128)}), f32[16,1,64]{2,1,0:T(1,128)S(1)}, u32[]{:S(2)}, u32[]{:S(2)}) %all-to-all-start.1) | async-done | bytes 4128 | tf_op jit(solution)/shard_map/all_to_all | solution.py:37
  24.4 1.8 %broadcast_in_dim.59 = bf16[8,2,2,256,128]{4,3,2,1,0:T(8,128)(2,1)} broadcast(bf16[8,2,256,128]{3,2,1,0:T(8,128)(2,1)S(1)} %copy.40), dimensions={0,2,3,4} | broadcast | bytes 3145728 | tf_op jit(solution)/shard_map/broadcast_in_dim | solution.py:66
  26.2 5.1 %all-to-all-start = ((bf16[16,2,256,128]{3,2,1,0:T(8,128)(2,1)}), bf16[16,2,256,128]{3,2,1,0:T(8,128)(2,1)S(1)}, u32[]{:S(2)}, u32[]{:S(2)}) async-start(bf16[16,2,256,128]{3,2,1,0:T(8,128)(2,1)} %bitcast.99), calls=%async_computation | async-start | bytes 4194304 | tf_op jit(solution)/shard_map/all_to_all | solution.py:67
  31.3 27.8 %all-gather.2.cloned.1.call-done = bf16[2,256,6144]{2,1,0:T(8,128)(2,1)} async-done(((bf16[2,256,384]{2,1,0:T(8,128)(2,1)}), bf16[2,256,6144]{2,1,0:T(8,128)(2,1)}) %all-gather.2.cloned.1.call-update) | async-done | bytes 6291472 | tf_op jit(solution)/shard_map/all_gather | solution.py:59
  59.2 3.8 %fusion.2 = f32[64,6144]{1,0:T(8,128)} fusion(bf16[2,256,6144]{2,1,0:T(8,128)(2,1)} %all-gather.2.cloned.1.call-done, bf16[64,256]{1,0:T(8,128)(2,1)S(1)} %copy-done.2, f32[256]{0:T(256)S(1)} %convert_element_type.88, f32[64]{0:T(128)S(1)} %add_rsqrt_fusion), kind=kOutput, calls=%fused_computation.4 | convolution fusion | flops 201392128 | bytes 4752640 | tf_op jit(solution)/shard_map/dot_general | solution.py:61
  63.0 1.1 slice_bitcast_fusion.2
  64.4 0.9 slice-done.1
  65.4 1.4 %maximum_bitcast_fusion = f32[16,64,384]{2,1,0:T(8,128)} fusion(f32[64,16,128]{2,0,1:T(8,128)S(1)} %bitcast.106, f32[64,16,256]{2,0,1:T(8,128)S(1)} %bitcast.101), kind=kLoop, calls=%fused_computation.10 | loop fusion | flops 393216 | bytes 3145728 | tf_op jit(solution)/shard_map/transpose | solution.py:79
  66.8 7.4 %all-to-all-start.2 = ((f32[16,64,384]{2,1,0:T(8,128)}), f32[16,64,384]{2,1,0:T(8,128)}, u32[]{:S(2)}, u32[]{:S(2)}) async-start(f32[16,64,384]{2,1,0:T(8,128)} %maximum_bitcast_fusion), calls=%async_computation.2 | async-start | bytes 3145728 | tf_op jit(solution)/shard_map/all_to_all | solution.py:80
  76.0 1.9 %slice-done = bf16[1,256,6144]{2,1,0:T(8,128)(2,1)S(1)} async-done(((bf16[2,256,6144]{2,1,0:T(8,128)(2,1)}), bf16[1,256,6144]{2,1,0:T(8,128)(2,1)S(1)}, s32[]{:S(2)}) %slice-start) | async-done | bytes 3145752 | tf_op jit(solution)/shard_map/slice | solution.py:124
  77.9 0.7 copy.55
  78.6 1.5 %slice.40 = bf16[256,16,256]{2,1,0:T(8,128)(2,1)} slice(bf16[256,16,384]{2,1,0:T(8,128)(2,1)S(1)} %bitcast.98), slice={[0:256], [0:16], [0:256]} | slice | bytes 4194304 | tf_op jit(solution)/shard_map/slice | solution.py:124
  80.0 4.3 %copy.49 = bf16[256,16,256]{0,2,1:T(8,128)(2,1)} copy(bf16[256,16,256]{2,1,0:T(8,128)(2,1)} %slice.40) | data formatting | bytes 4194304 | tf_op jit(solution)/shard_map/slice | solution.py:124
  84.4 1.2 fusion.55
  85.5 10.7 %all-to-all-done.2 = f32[16,64,384]{2,1,0:T(8,128)} async-done(((f32[16,64,384]{2,1,0:T(8,128)}), f32[16,64,384]{2,1,0:T(8,128)}, u32[]{:S(2)}, u32[]{:S(2)}) %all-to-all-start.2) | async-done | bytes 1572896 | tf_op jit(solution)/shard_map/all_to_all | solution.py:80
  96.2 1.5 %reduce_sum.59 = bf16[64,384]{1,0:T(8,128)(2,1)S(1)} reduce(f32[16,64,384]{2,1,0:T(8,128)} %all-to-all-done.2, f32[]{:T(128)} %constant.12.clone.1), dimensions={0}, to_apply=%region_2.3 | reduce | flops 368640 | bytes 1622020 | tf_op jit(solution)/shard_map/reduce_sum | solution.py:80
  97.7 3.6 %collective-permute-start = (bf16[64,128]{1,0:T(8,128)(2,1)S(1)}, bf16[64,128]{1,0:T(8,128)(2,1)S(1)}, u32[]{:S(2)}, u32[]{:S(2)}) collective-permute-start(bf16[64,128]{1,0:T(8,128)(2,1)S(1)} %slice.38), channel_id=1, source_target_pairs={{0,16},{16,0},{32,48},{48,32},{64,80},{80,64},{96,112},{112,96},{1... | collective-permute-start | bytes 49160 | tf_op jit(solution)/shard_map/ppermute | solution.py:84
  101.3 0.5 fusion.56
  101.9 0.5 fusion.17
  102.4 0.5 fusion.6
  103.6 0.4 copy-done
  104.0 0.7 fusion.10
  104.8 13.7 %all_to_all.21 = bf16[16,64,256]{2,1,0:T(8,128)(2,1)S(1)} all-to-all(bf16[16,64,256]{2,1,0:T(8,128)(2,1)S(1)} %fusion.10), channel_id=1, replica_groups=mesh['row'=16,'col'=16] {'row'}, dimensions={0} | all-to-all | bytes 1048576 | tf_op jit(solution)/shard_map/all_to_all | solution.py:30
  118.4 0.7 reduce_sum.62
  (40 shorter events, 2.2 us)
Async XLA Ops:
  6.5 52.6 %all-gather.2.cloned.1.call-start = ((), (), s32[]{:S(2)}) async-start(), calls=%async_computation.4 | async-start | bytes 6684672 | tf_op jit(solution)/shard_map/all_gather | solution.py:59
  10.7 13.6 %all-to-all-start.1 = ((f32[16,1,64]{2,1,0:T(1,128)}), f32[16,1,64]{2,1,0:T(1,128)S(1)}, u32[]{:S(2)}, u32[]{:S(2)}) async-start(f32[16,1,64]{2,1,0:T(1,128)} %broadcast_in_dim.60), calls=%async_computation.1 | async-start | bytes 16384 | tf_op jit(solution)/shard_map/all_to_all | solution.py:37
  26.2 5.1 %copy-start.4 = (bf16[256]{0:T(256)(128)(2,1)S(1)}, bf16[256]{0:T(256)(128)(2,1)}, u32[]{:S(2)}) copy-start(bf16[256]{0:T(256)(128)(2,1)} %param.9) | copy-start | bytes 1540
  26.2 33.0 %copy-start.2 = (bf16[64,256]{1,0:T(8,128)(2,1)S(1)}, bf16[64,256]{1,0:T(8,128)(2,1)}, u32[]{:S(2)}) copy-start(bf16[64,256]{1,0:T(8,128)(2,1)} %param.8) | copy-start | bytes 98308
  26.2 36.8 %all-to-all-start = ((bf16[16,2,256,128]{3,2,1,0:T(8,128)(2,1)}), bf16[16,2,256,128]{3,2,1,0:T(8,128)(2,1)S(1)}, u32[]{:S(2)}, u32[]{:S(2)}) async-start(bf16[16,2,256,128]{3,2,1,0:T(8,128)(2,1)} %bitcast.99), calls=%async_computation | async-start | bytes 4194304 | tf_op jit(solution)/shard_map/all_to_all | solution.py:67
  64.1 1.2 slice-start.1
  66.8 8.1 %copy-start.3 = (s32[1,64]{1,0:T(1,128)S(1)}, s32[1,64]{1,0:T(1,128)}, u32[]{:S(2)}) copy-start(s32[1,64]{1,0:T(1,128)} %param.15) | copy-start | bytes 772
  66.8 29.4 %all-to-all-start.2 = ((f32[16,64,384]{2,1,0:T(8,128)}), f32[16,64,384]{2,1,0:T(8,128)}, u32[]{:S(2)}, u32[]{:S(2)}) async-start(f32[16,64,384]{2,1,0:T(8,128)} %maximum_bitcast_fusion), calls=%async_computation.2 | async-start | bytes 3145728 | tf_op jit(solution)/shard_map/all_to_all | solution.py:80
  76.0 1.9 %slice-start = ((bf16[2,256,6144]{2,1,0:T(8,128)(2,1)}), bf16[1,256,6144]{2,1,0:T(8,128)(2,1)S(1)}, s32[]{:S(2)}) async-start(bf16[2,256,6144]{2,1,0:T(8,128)(2,1)} %all-gather.2.cloned.1.call-done), calls=%async_computation.5 | async-start | bytes 6291456 | tf_op jit(solution)/shard_map/slice | solution.py:124
  85.5 16.3 %copy-start.1 = (bf16[16,1,256,128]{3,2,1,0:T(8,128)(2,1)S(1)}, bf16[16,1,256,128]{3,2,1,0:T(8,128)(2,1)}, u32[]{:S(2)}) copy-start(bf16[16,1,256,128]{3,2,1,0:T(8,128)(2,1)} %get-tuple-element.22) | copy-start | bytes 3145732
  97.7 5.3 %collective-permute-start = (bf16[64,128]{1,0:T(8,128)(2,1)S(1)}, bf16[64,128]{1,0:T(8,128)(2,1)S(1)}, u32[]{:S(2)}, u32[]{:S(2)}) collective-permute-start(bf16[64,128]{1,0:T(8,128)(2,1)S(1)} %slice.38), channel_id=1, source_target_pairs={{0,16},{16,0},{32,48},{48,32},{64,80},{80,64},{96,112},{112,96},{1... | collective-permute-start | bytes 49160 | tf_op jit(solution)/shard_map/ppermute | solution.py:84
  102.4 1.6 %copy-start = (bf16[256,16,256]{0,2,1:T(8,128)(2,1)S(1)}, bf16[256,16,256]{0,2,1:T(8,128)(2,1)}, u32[]{:S(2)}) copy-start(bf16[256,16,256]{0,2,1:T(8,128)(2,1)} %copy.49) | copy-start | bytes 6291460
Sparse Core Ops, SparseCore 0:
  9.4 49.7 all-gather.1

commit v21 on v20

--- a/solution.py
+++ b/solution.py
@@ -55,10 +55,15 @@
     )
     qkv_width = w_qkv.shape[1]
     col_count = lax.axis_size("col")
-    out_padded = jnp.pad(w_out, ((0, 0), (0, qkv_width - w_out.shape[1])))
-    weights_all = lax.all_gather(jnp.stack([w_qkv, out_padded]), "col", axis=2, tiled=True)
+    feature_rows = w_qkv.shape[0]
+    out_rows = -(-w_out.size // qkv_width)
+    out_rows = -(-out_rows // 8) * 8
+    out_flat = jnp.pad(w_out.reshape(-1), (0, out_rows * qkv_width - w_out.size))
+    weights_all = lax.all_gather(
+        jnp.concatenate([w_qkv, out_flat.reshape(out_rows, qkv_width)]), "col", axis=1, tiled=True
+    )
     weights_all = lax.optimization_barrier(weights_all)
-    partial_value = jnp.dot(normed, weights_all[0], preferred_element_type=jnp.float32)
+    partial_value = jnp.dot(normed, weights_all[:feature_rows], preferred_element_type=jnp.float32)
 
     local = jnp.stack([cache_k[0], value_cache[0]]).reshape(
         2, token_positions, KEY_VALUE_HEADS, HEAD_SIZE
@@ -121,7 +126,14 @@
     blended = cache_blend * cache_scale[..., None] + tree_blend * tree_scale[..., None]
     attended = (blended / totals[..., None]).astype(jnp.bfloat16)
     attended = attended.transpose(1, 0, 2).reshape(rows_here, heads_dev * HEAD_SIZE)
-    out_all = weights_all[1].reshape(w_out.shape[0], col_count, -1)[:, :, : w_out.shape[1]]
+    out_all = (
+        weights_all[feature_rows:]
+        .reshape(out_rows, col_count, qkv_width)
+        .transpose(1, 0, 2)
+        .reshape(col_count, -1)[:, : w_out.size]
+        .reshape(col_count, w_out.shape[0], w_out.shape[1])
+        .transpose(1, 0, 2)
+    )
     partial_out = jnp.dot(
         attended, out_all.reshape(w_out.shape[0], -1), preferred_element_type=jnp.float32
     )

time: 127 us -> 125 us (0.984)
  other arithmetic: 8.26 us -> 6.9 us
    slice x4 -> x3, local copies, waits for them, and re-layouts: 7.67 us -> 1.74 us  [shards(): weights_all[feature_rows:].reshape(out_rows, col_count, qkv_width)]
    transpose x0 -> x1, local copies, waits for them, and re-layouts: none -> 3.92 us  [shards(): out_all = weights_all[feature_rows:].reshape(out_rows, col_count, qkv_wid...]
    unnamed x14 -> x20, local copies, waits for them, and re-layouts: 2.53 us -> 5.21 us
    all_gather x1, waiting for transfers between devices: 27.8 us -> 25.6 us  [shards(): lax.all_gather(jnp.concatenate([w_qkv, out_flat.reshape(out_rows, qkv_wid...]
    another operation x1 -> x0, other arithmetic: 1.77 us -> none  [shards(): jnp.stack([w_qkv, out_padded])]
    concatenate x0 -> x1, other arithmetic: none -> 1.68 us  [shards(): jnp.concatenate([w_qkv, out_flat.reshape(out_rows, qkv_width)])]
where the time goes in v21:
time: 125 us; the launch traced here: 124 us
  waiting for transfers between devices  42.1 us (34%)
  starting transfers between devices  23.6 us (19%)
  local copies, waits for them, and re-layouts  16.5 us (13%)
  between operations  14.3 us (11%)
  blocking collectives  13.7 us (11%)
  other arithmetic  6.9 us (6%)
  matrix products  6.86 us (5%)
    all_gather x1, waiting for transfers between devices, shards(): lax.all_gather(jnp.concatenate([w_qkv, out_flat.reshape(out_rows, qkv_wid...  25.6 us
    all_to_all x1, blocking collectives, row_reduce(): received = lax.all_to_all(pieces, axis_name, 0, 0)  13.7 us
    all_to_all x1, waiting for transfers between devices, shards(): lax.all_to_all(owned, 'row', 0, 0)  10.9 us
    all_to_all x1, starting transfers between devices, row_gather(): return lax.all_to_all(copies, axis_name, 0, 0)  7.48 us
    all_to_all x1, starting transfers between devices, shards(): lax.all_to_all(owned, 'row', 0, 0)  7.4 us
    all_to_all x1, waiting for transfers between devices, row_gather(): return lax.all_to_all(copies, axis_name, 0, 0)  5.47 us
    unnamed x20, local copies, waits for them, and re-layouts  5.21 us
    all_to_all x1, starting transfers between devices, shards(): by_head = lax.all_to_all(pieces, 'row', 0, 0)  5.13 us
  transfers between devices with their start and end apart: 5, of which 4 were waited for; matrix products, arithmetic and copies ran while one was open for 15% of the time, Pallas kernels for 0%

profile of v21, /device:TPU:2, one launch (start us, length us, event | category | flops | bytes accessed | tf_op | source)
XLA Modules:
  0.0 123.9 jit_solution(737645219438558461)
XLA Ops:
  6.5 1.1 copy.67
  7.7 1.7 %pad_maximum_fusion.1 = bf16[432,384]{1,0:T(8,128)(2,1)} fusion(bf16[176,384]{1,0:T(8,128)(2,1)S(1)} %reshape.217, bf16[256,384]{1,0:T(8,128)(2,1)} %param.10), kind=kLoop, calls=%fused_computation.34 | loop fusion | flops 663552 | bytes 663552 | tf_op jit(solution)/shard_map/concatenate | solution.py:63
  9.4 0.9 fusion.23
  10.3 0.6 broadcast_in_dim.60
  10.9 7.5 %all-to-all-start.1 = ((f32[16,1,64]{2,1,0:T(1,128)}), f32[16,1,64]{2,1,0:T(1,128)S(1)}, u32[]{:S(2)}, u32[]{:S(2)}) async-start(f32[16,1,64]{2,1,0:T(1,128)} %broadcast_in_dim.60), calls=%async_computation.1 | async-start | bytes 16384 | tf_op jit(solution)/shard_map/all_to_all | solution.py:37
  18.5 0.3 copy.66
  18.9 0.2 copy.51
  19.1 5.5 %all-to-all-done.1 = f32[16,1,64]{2,1,0:T(1,128)S(1)} async-done(((f32[16,1,64]{2,1,0:T(1,128)}), f32[16,1,64]{2,1,0:T(1,128)S(1)}, u32[]{:S(2)}, u32[]{:S(2)}) %all-to-all-start.1) | async-done | bytes 4128 | tf_op jit(solution)/shard_map/all_to_all | solution.py:37
  24.6 1.8 %broadcast_in_dim.59 = bf16[8,2,2,256,128]{4,3,2,1,0:T(8,128)(2,1)} broadcast(bf16[8,2,256,128]{3,2,1,0:T(8,128)(2,1)S(1)} %copy.51), dimensions={0,2,3,4} | broadcast | bytes 3145728 | tf_op jit(solution)/shard_map/broadcast_in_dim | solution.py:71
  26.4 5.1 %all-to-all-start = ((bf16[16,2,256,128]{3,2,1,0:T(8,128)(2,1)}), bf16[16,2,256,128]{3,2,1,0:T(8,128)(2,1)S(1)}, u32[]{:S(2)}, u32[]{:S(2)}) async-start(bf16[16,2,256,128]{3,2,1,0:T(8,128)(2,1)} %bitcast.104), calls=%async_computation | async-start | bytes 4194304 | tf_op jit(solution)/shard_map/all_to_all | solution.py:72
  31.6 25.6 %all-gather.2.cloned.1.call-done = bf16[432,6144]{1,0:T(8,128)(2,1)} async-done(((bf16[432,384]{1,0:T(8,128)(2,1)}), bf16[432,6144]{1,0:T(8,128)(2,1)}) %all-gather.2.cloned.1.call-update) | async-done | bytes 5308432 | tf_op jit(solution)/shard_map/all_gather | solution.py:62
  57.2 3.8 %fusion.2 = f32[64,6144]{1,0:T(8,128)} fusion(bf16[432,6144]{1,0:T(8,128)(2,1)} %all-gather.2.cloned.1.call-done, bf16[64,256]{1,0:T(8,128)(2,1)S(1)} %copy-done.4, f32[256]{0:T(256)S(1)} %convert_element_type.88, f32[64]{0:T(128)S(1)} %add_rsqrt_fusion), kind=kOutput, calls=%fused_computation.3 | convolution fusion | flops 201392128 | bytes 4752640 | tf_op jit(solution)/shard_map/dot_general | solution.py:66
  61.0 1.1 slice_bitcast_fusion
  62.4 0.9 slice-done.1
  63.5 1.3 %maximum_bitcast_fusion = f32[16,64,384]{2,1,0:T(8,128)} fusion(f32[64,16,128]{2,0,1:T(8,128)S(1)} %bitcast.113, f32[64,16,256]{2,0,1:T(8,128)S(1)} %bitcast.108), kind=kLoop, calls=%fused_computation.11 | loop fusion | flops 393216 | bytes 3145728 | tf_op jit(solution)/shard_map/transpose | solution.py:84
  64.7 7.4 %all-to-all-start.2 = ((f32[16,64,384]{2,1,0:T(8,128)}), f32[16,64,384]{2,1,0:T(8,128)}, u32[]{:S(2)}, u32[]{:S(2)}) async-start(f32[16,64,384]{2,1,0:T(8,128)} %maximum_bitcast_fusion), calls=%async_computation.2 | async-start | bytes 3145728 | tf_op jit(solution)/shard_map/all_to_all | solution.py:85
  73.9 1.6 %slice-done = bf16[176,6144]{1,0:T(8,128)(2,1)S(1)} async-done(((bf16[432,6144]{1,0:T(8,128)(2,1)}), bf16[176,6144]{1,0:T(8,128)(2,1)S(1)}, s32[]{:S(2)}) %slice-start) | async-done | bytes 2162712 | tf_op jit(solution)/shard_map/slice | solution.py:130
  75.5 0.2 copy.83
  75.8 0.5 copy.69
  76.4 1.8 %copy.70 = bf16[2,8,256,256]{3,2,1,0:T(8,128)(2,1)} copy(bf16[2,8,256,256]{3,1,2,0:T(8,128)(2,1)S(1)} %bitcast.105) | data formatting | bytes 4194304
  78.2 3.9 %copy.61 = bf16[256,16,256]{0,2,1:T(8,128)(2,1)} copy(bf16[256,16,256]{2,0,1:T(8,128)(2,1)} %bitcast.106) | data formatting | bytes 4194304 | tf_op jit(solution)/shard_map/transpose | solution.py:135
  82.1 1.2 fusion.56
  83.3 10.9 %all-to-all-done.2 = f32[16,64,384]{2,1,0:T(8,128)} async-done(((f32[16,64,384]{2,1,0:T(8,128)}), f32[16,64,384]{2,1,0:T(8,128)}, u32[]{:S(2)}, u32[]{:S(2)}) %all-to-all-start.2) | async-done | bytes 1572896 | tf_op jit(solution)/shard_map/all_to_all | solution.py:85
  94.1 1.5 %reduce_sum.59 = bf16[64,384]{1,0:T(8,128)(2,1)S(1)} reduce(f32[16,64,384]{2,1,0:T(8,128)} %all-to-all-done.2, f32[]{:T(128)} %constant.12.clone.1), dimensions={0}, to_apply=%region_2.3 | reduce | flops 368640 | bytes 1622020 | tf_op jit(solution)/shard_map/reduce_sum | solution.py:85
  95.6 3.6 %collective-permute-start = (bf16[64,128]{1,0:T(8,128)(2,1)S(1)}, bf16[64,128]{1,0:T(8,128)(2,1)S(1)}, u32[]{:S(2)}, u32[]{:S(2)}) collective-permute-start(bf16[64,128]{1,0:T(8,128)(2,1)S(1)} %slice.38), channel_id=1, source_target_pairs={{0,16},{16,0},{32,48},{48,32},{64,80},{80,64},{96,112},{112,96},{1... | collective-permute-start | bytes 49160 | tf_op jit(solution)/shard_map/ppermute | solution.py:89
  99.3 0.5 fusion.57
  99.8 0.5 fusion.18
  100.4 0.5 fusion.7
  101.5 0.4 copy-done
  101.9 0.8 fusion.11
  102.7 13.7 %all_to_all.21 = bf16[16,64,256]{2,1,0:T(8,128)(2,1)S(1)} all-to-all(bf16[16,64,256]{2,1,0:T(8,128)(2,1)S(1)} %fusion.11), channel_id=1, replica_groups=mesh['row'=16,'col'=16] {'row'}, dimensions={0} | all-to-all | bytes 1048576 | tf_op jit(solution)/shard_map/all_to_all | solution.py:30
  116.3 0.7 reduce_sum.62
  (48 shorter events, 2.5 us)
Async XLA Ops:
  6.5 11.9 %copy-start.2 = (bf16[1,256,1024]{2,1,0:T(8,128)(2,1)S(1)}, bf16[1,256,1024]{2,1,0:T(8,128)(2,1)}, u32[]{:S(2)}) copy-start(bf16[1,256,1024]{2,1,0:T(8,128)(2,1)} %param.13) | copy-start | bytes 1572868
  6.5 11.9 %copy-start.3 = (bf16[1,256,1024]{2,1,0:T(8,128)(2,1)S(1)}, bf16[1,256,1024]{2,1,0:T(8,128)(2,1)}, u32[]{:S(2)}) copy-start(bf16[1,256,1024]{2,1,0:T(8,128)(2,1)} %param.12) | copy-start | bytes 1572868
  6.5 50.6 %all-gather.2.cloned.1.call-start = ((), (), s32[]{:S(2)}) async-start(), calls=%async_computation.4 | async-start | bytes 5640192 | tf_op jit(solution)/shard_map/all_gather | solution.py:62
  10.9 13.6 %all-to-all-start.1 = ((f32[16,1,64]{2,1,0:T(1,128)}), f32[16,1,64]{2,1,0:T(1,128)S(1)}, u32[]{:S(2)}, u32[]{:S(2)}) async-start(f32[16,1,64]{2,1,0:T(1,128)} %broadcast_in_dim.60), calls=%async_computation.1 | async-start | bytes 16384 | tf_op jit(solution)/shard_map/all_to_all | solution.py:37
  26.4 5.1 %copy-start.6 = (bf16[256]{0:T(256)(128)(2,1)S(1)}, bf16[256]{0:T(256)(128)(2,1)}, u32[]{:S(2)}) copy-start(bf16[256]{0:T(256)(128)(2,1)} %param.9) | copy-start | bytes 1540
  26.4 30.8 %copy-start.4 = (bf16[64,256]{1,0:T(8,128)(2,1)S(1)}, bf16[64,256]{1,0:T(8,128)(2,1)}, u32[]{:S(2)}) copy-start(bf16[64,256]{1,0:T(8,128)(2,1)} %param.8) | copy-start | bytes 98308
  26.4 34.6 %all-to-all-start = ((bf16[16,2,256,128]{3,2,1,0:T(8,128)(2,1)}), bf16[16,2,256,128]{3,2,1,0:T(8,128)(2,1)S(1)}, u32[]{:S(2)}, u32[]{:S(2)}) async-start(bf16[16,2,256,128]{3,2,1,0:T(8,128)(2,1)} %bitcast.104), calls=%async_computation | async-start | bytes 4194304 | tf_op jit(solution)/shard_map/all_to_all | solution.py:72
  62.1 1.2 slice-start.1
  64.7 8.1 %copy-start.5 = (s32[1,64]{1,0:T(1,128)S(1)}, s32[1,64]{1,0:T(1,128)}, u32[]{:S(2)}) copy-start(s32[1,64]{1,0:T(1,128)} %param.15) | copy-start | bytes 772
  64.7 29.4 %all-to-all-start.2 = ((f32[16,64,384]{2,1,0:T(8,128)}), f32[16,64,384]{2,1,0:T(8,128)}, u32[]{:S(2)}, u32[]{:S(2)}) async-start(f32[16,64,384]{2,1,0:T(8,128)} %maximum_bitcast_fusion), calls=%async_computation.2 | async-start | bytes 3145728 | tf_op jit(solution)/shard_map/all_to_all | solution.py:85
  73.9 1.6 %slice-start = ((bf16[432,6144]{1,0:T(8,128)(2,1)}), bf16[176,6144]{1,0:T(8,128)(2,1)S(1)}, s32[]{:S(2)}) async-start(bf16[432,6144]{1,0:T(8,128)(2,1)} %all-gather.2.cloned.1.call-done), calls=%async_computation.5 | async-start | bytes 4325376 | tf_op jit(solution)/shard_map/slice | solution.py:130
  83.3 16.5 %copy-start.1 = (bf16[16,1,256,128]{3,2,1,0:T(8,128)(2,1)S(1)}, bf16[16,1,256,128]{3,2,1,0:T(8,128)(2,1)}, u32[]{:S(2)}) copy-start(bf16[16,1,256,128]{3,2,1,0:T(8,128)(2,1)} %get-tuple-element.22) | copy-start | bytes 3145732
  95.6 5.3 %collective-permute-start = (bf16[64,128]{1,0:T(8,128)(2,1)S(1)}, bf16[64,128]{1,0:T(8,128)(2,1)S(1)}, u32[]{:S(2)}, u32[]{:S(2)}) collective-permute-start(bf16[64,128]{1,0:T(8,128)(2,1)S(1)} %slice.38), channel_id=1, source_target_pairs={{0,16},{16,0},{32,48},{48,32},{64,80},{80,64},{96,112},{112,96},{1... | collective-permute-start | bytes 49160 | tf_op jit(solution)/shard_map/ppermute | solution.py:89
  100.3 1.6 %copy-start = (bf16[256,16,256]{0,2,1:T(8,128)(2,1)S(1)}, bf16[256,16,256]{0,2,1:T(8,128)(2,1)}, u32[]{:S(2)}) copy-start(bf16[256,16,256]{0,2,1:T(8,128)(2,1)} %copy.61) | copy-start | bytes 6291460
Sparse Core Ops, SparseCore 0:
  9.6 47.5 all-gather.1
